TPU v7x, 1024 devices: a whole 4x4x32 slice. The times are simulated.
1024 devices in a mesh: elem: 128 (over z, x), grp: 8 (over y, core).
Axes of the slice: x: 4, y: 4, z: 32, core: 2. Of those that a mesh axis runs over, the one named last changes fastest.
Arguments:
- state: float32 [8192, 6, 512], P(('elem', 'grp')), may hold values from -6 to 20, as said below
- material: int32 [8192], P(('elem', 'grp')), may hold values from 0 to 1
- metric: float32 [8192], P(('elem', 'grp')), may hold values from 1 to 4
- mortar_proj: float32 [4, 64, 64], replicated, may hold values from 0 to 1, as said below
- mortar_map: int32 [1024, 4, 128], P(('elem', 'grp')), may hold values from 0 to 7, as said below
- mortar_count: int32 [1024, 10], P(('elem', 'grp')), may hold values from 0 to 32, as said below
- neighbours: int32 [8192, 6], P(('elem', 'grp')), may hold values from -1 to 7, as said below
Outputs:
- new_state: float32 [8192, 6, 512], P(('elem', 'grp'))
Inputs may be any that keep to these rules, and one draw needn't show every extreme that they name: `state`: density and pressure, with either heat ratio, are positive at every node. `mortar_proj`: entries are nonnegative and every row sums to one. `mortar_map`: Rows: local element, face (0 to 5), subface (0 conforming, 1 to 4 a quadrant of a coarse face), orientation (0 to 7). Slot s below 64 pairs with slot (own grp index) * 8 + s % 8 of the device with the same elem index and grp index s // 8; the next 32 slots pair, position by position, with the last 32 slots of the device one elem index higher, the last 32 with the middle 32 of the device one elem index lower, same grp index. Paired faces lie along one dimension with opposite normals; at most one side of a pair has a nonzero subface. `mortar_count`: entry g below 8 counts the live slots toward grp peer g, 0 for the device itself, equal to the peer's entry for this device, at most 8 and reaching it on some devices; entry 8 toward the next elem index equals that device's entry 9; the top elem index has 0 in entry 8, the bottom one 0 in entry 9. Slots at positions below the count are live. `neighbours`: local element across the face, meeting its opposite face, or -1.
All inputs are finite; a program needn't handle non-finite values.
Results may differ from a plain program's by a relative error of at most 0.0003.
Values sent between devices are 32-bit elements; how exact they have to be, the bound alone decides.
No kernel may reach another device: no remote copies, remote signals or barrier semaphores. Data moves between devices by JAX's collectives and lax.ppermute only.
A program may use at most 64 MiB of HBM per device.

v0:
```python
import math

import jax
import jax.numpy as jnp
import numpy as np
from jax import lax
from jax.sharding import PartitionSpec as P

NV = 6
NP = 8
FN = 64
VN = 512
SUBS = 4
CAPG = 8
CAPS = 32


highest = lax.Precision.HIGHEST
step_size = 0.002
lift_weight = 49.0


def in_one_piece(arrays, axis, split_dim, concat_dim, along):
    widths = [math.prod(a.shape[along:]) for a in arrays]
    both = jnp.concatenate(
        [a.reshape(*a.shape[:along], w) for a, w in zip(arrays, widths)], axis=along
    )
    out = lax.all_to_all(both, axis, split_axis=split_dim, concat_axis=concat_dim, tiled=True)
    parts = jnp.split(out, [sum(widths[:k]) for k in range(1, len(widths))], axis=along)
    return tuple((b.reshape(*out.shape[:along], *a.shape[along:]) for a, b in zip(arrays, parts)))


def from_behind(block, axis, distance):
    devices = range(lax.axis_size(axis))
    route = [(i - distance, i) for i in devices if i - distance in devices]
    return lax.ppermute(block, axis, route)


def cheb_matrix():
    points = -np.cos(np.pi * np.arange(8) / 7.0)
    factor = np.array([2.0, 1.0, 1.0, 1.0, 1.0, 1.0, 1.0, 2.0])
    alternating = np.where(np.arange(8) % 2 == 0, 1.0, -1.0)
    scaled = factor * alternating
    differ = points[:, None] - points[None, :] + np.eye(8)
    matrix = scaled[:, None] / scaled[None, :] / differ
    matrix = matrix * (1.0 - np.eye(8))
    return matrix - np.eye(8) * matrix.sum(axis=1)[:, None]


def face_plane(node_grid, face):
    index = 0 if face % 2 == 0 else 7
    if face // 2 == 0:
        return node_grid[index]
    if face // 2 == 1:
        return node_grid[:, index]
    return node_grid[:, :, index]


def face_select():
    node_grid = np.arange(512).reshape(8, 8, 8)
    layers = []
    for face in range(6):
        layers.append(face_plane(node_grid, face).reshape(64))
    nodes = np.concatenate(layers)
    return (nodes[:, None] == np.arange(512)[None, :]).astype(np.float32)


def orient_matrices():
    first, second = np.meshgrid(np.arange(8), np.arange(8), indexing="ij")
    result = []
    for orient in range(8):
        row_p, row_r = (second, first) if orient & 4 else (first, second)
        if orient & 1:
            row_p = 7 - row_p
        if orient & 2:
            row_r = 7 - row_r
        source = (8 * row_p + row_r).reshape(64)
        result.append((source[:, None] == np.arange(64)[None, :]).astype(np.float32))
    return np.stack(result)


def state_parts(cons, heat_ratio, normal):
    density = cons[:, 0]
    momentum = cons[:, 1:4]
    energy = cons[:, 4]
    scalar = cons[:, 5]
    velocity = momentum / density[:, None]
    pressure = (heat_ratio[:, None] - 1.0) * (energy - 0.5 * jnp.sum(momentum * velocity, axis=1))
    direction = normal[:, :, None]
    speed_n = jnp.sum(direction * velocity, axis=1)
    sound_speed = jnp.sqrt(heat_ratio[:, None] * pressure / density)
    phys_flux = jnp.concatenate(
        [
            (density * speed_n)[:, None],
            momentum * speed_n[:, None] + pressure[:, None] * direction,
            ((energy + pressure) * speed_n)[:, None],
            (scalar * speed_n)[:, None],
        ],
        axis=1,
    )
    return (density, velocity, pressure, speed_n, sound_speed, energy, scalar, phys_flux)


def star_state(parts, wave_speed, middle, normal):
    density, velocity, pressure, speed_n, sound_speed, energy, scalar, phys_flux = parts
    relative = wave_speed - speed_n
    factor = density * relative / (wave_speed - middle)
    shifted = middle - speed_n
    momentum = factor[:, None] * (velocity + shifted[:, None] * normal[:, :, None])
    energy_star = factor * (energy / density + shifted * (middle + pressure / (density * relative)))
    return jnp.concatenate(
        [factor[:, None], momentum, energy_star[:, None], (factor * scalar / density)[:, None]],
        axis=1,
    )


def hllc_flux(left, right, heat_left, heat_right, normal):
    left_parts = state_parts(left, heat_left, normal)
    right_parts = state_parts(right, heat_right, normal)
    left_wave = jnp.minimum(left_parts[3] - left_parts[4], right_parts[3] - right_parts[4])
    right_wave = jnp.maximum(left_parts[3] + left_parts[4], right_parts[3] + right_parts[4])
    left_mass = left_parts[0] * (left_wave - left_parts[3])
    right_mass = right_parts[0] * (right_wave - right_parts[3])
    middle = (
        right_parts[2] - left_parts[2] + left_mass * left_parts[3] - right_mass * right_parts[3]
    ) / (left_mass - right_mass)
    left_star = left_parts[7] + left_wave[:, None] * (
        star_state(left_parts, left_wave, middle, normal) - left
    )
    right_star = right_parts[7] + right_wave[:, None] * (
        star_state(right_parts, right_wave, middle, normal) - right
    )
    return jnp.where(
        (left_wave >= 0.0)[:, None],
        left_parts[7],
        jnp.where(
            (middle >= 0.0)[:, None],
            left_star,
            jnp.where((right_wave > 0.0)[:, None], right_star, right_parts[7]),
        ),
    )


def normals_of(face):
    axis_id = face // 2
    orient_sign = jnp.where(face % 2 == 1, 1.0, -1.0).astype(jnp.float32)
    return orient_sign[:, None] * (
        axis_id[:, None] == jnp.arange(3, dtype=jnp.int32)[None, :]
    ).astype(jnp.float32)


def face_traces(elements, select):
    count_el = elements.shape[0]
    flat_state = elements.reshape(count_el * NV, VN)
    traces = jnp.dot(flat_state, select.T, precision=highest, preferred_element_type=jnp.float32)
    return traces.reshape(count_el, NV, 6, FN).transpose(0, 2, 1, 3).reshape(count_el * 6, NV, FN)


def slot_operators(mortar_proj, mortar_info):
    identity = jnp.eye(FN, dtype=jnp.float32)
    proj_table = jnp.concatenate([identity[None], mortar_proj], axis=0)
    orients = jnp.asarray(orient_matrices(), jnp.float32)
    combos = jnp.einsum("spq,oqr->sopr", proj_table, orients, precision=highest).reshape(
        (SUBS + 1) * 8, FN, FN
    )
    return combos[mortar_info[2] * 8 + mortar_info[3]]


def mortar_traces(face_rows, operators, heat_ratio, mortar_info):
    picked = face_rows[mortar_info[0] * 6 + mortar_info[1]]
    native = jnp.einsum("spq,svq->svp", operators, picked, precision=highest)
    return (native, heat_ratio[mortar_info[0]])


def slot_layout(groups, grp_index, counts):
    grp_slots = groups * CAPG
    slot_index = jnp.arange(grp_slots + 2 * CAPS, dtype=jnp.int32)
    peer_index = slot_index // CAPG
    in_grp = slot_index < grp_slots
    in_up = (slot_index >= grp_slots) & (slot_index < grp_slots + CAPS)
    group_id = jnp.where(in_grp, peer_index, jnp.where(in_up, groups, groups + 1))
    position = jnp.where(in_grp, slot_index % CAPG, (slot_index - grp_slots) % CAPS)
    slot_limit = jnp.sum(
        jnp.where(
            group_id[:, None] == jnp.arange(groups + 2, dtype=jnp.int32)[None, :],
            counts[None, :],
            0,
        ),
        axis=1,
    )
    is_live = position < slot_limit
    is_lower = jnp.where(in_grp, grp_index < peer_index, in_up)
    return (is_lower, is_live)


def mortar_flux(native, partner, native_heat, partner_heat, normal, is_lower, is_live):
    live_mask = is_live[:, None, None]
    partner = jnp.where(live_mask, partner, native)
    partner_heat = jnp.where(is_live, partner_heat, native_heat)
    lower_mask = is_lower[:, None, None]
    low_side = jnp.where(lower_mask, native, partner)
    high_side = jnp.where(lower_mask, partner, native)
    low_heat = jnp.where(is_lower, native_heat, partner_heat)
    high_heat = jnp.where(is_lower, partner_heat, native_heat)
    low_normal = jnp.where(is_lower[:, None], normal, -normal)
    return hllc_flux(low_side, high_side, low_heat, high_heat, low_normal)


def volume_term(elements, heat_ratio):
    count_el = elements.shape[0]
    deriv = jnp.asarray(cheb_matrix(), jnp.float32)
    fluxes = []
    for axis_id in range(3):
        direction = jnp.eye(3, dtype=jnp.float32)[axis_id][None, :]
        fluxes.append(
            state_parts(elements, heat_ratio, direction)[7].reshape(count_el, NV, NP, NP, NP)
        )
    total = jnp.einsum("ia,evabc->evibc", deriv, fluxes[0], precision=highest)
    total = total + jnp.einsum("jb,evabc->evajc", deriv, fluxes[1], precision=highest)
    total = total + jnp.einsum("kc,evabc->evabk", deriv, fluxes[2], precision=highest)
    return -total.reshape(count_el, NV, VN)


def section_update(
    elements,
    heat_ratio,
    metric,
    mortar_info,
    neighbours,
    face_rows,
    operators,
    native,
    native_heat,
    flux_own,
    is_live,
    select,
    volume,
):
    count_el = elements.shape[0]
    normal = normals_of(mortar_info[1])
    correction = state_parts(native, native_heat, normal)[7] - flux_own
    correction = jnp.where(is_live[:, None, None], correction, 0.0)
    back_weight = jnp.where(mortar_info[2] == 0, 1.0, 0.25).astype(jnp.float32)
    projected = back_weight[:, None, None] * jnp.einsum(
        "spq,svp->svq", operators, correction, precision=highest
    )
    face_id = jnp.tile(jnp.arange(6, dtype=jnp.int32), count_el)
    face_owner = jnp.repeat(jnp.arange(count_el, dtype=jnp.int32), 6)
    face_normal = normals_of(face_id)
    across = neighbours.reshape(count_el * 6)
    has_across = across >= 0
    safe_across = jnp.where(has_across, across, face_owner)
    source = jnp.where(
        has_across,
        across * 6 + jnp.bitwise_xor(face_id, 1),
        jnp.arange(count_el * 6, dtype=jnp.int32),
    )
    partner = face_rows[source]
    row_heat = heat_ratio[face_owner]
    local_term = state_parts(face_rows, row_heat, face_normal)[7] - hllc_flux(
        face_rows, partner, row_heat, heat_ratio[safe_across], face_normal
    )
    local_term = jnp.where(has_across[:, None, None], local_term, 0.0)
    face_sum = local_term + jax.ops.segment_sum(
        projected, mortar_info[0] * 6 + mortar_info[1], num_segments=count_el * 6
    )
    placed = (
        face_sum.reshape(count_el, 6, NV, FN).transpose(0, 2, 1, 3).reshape(count_el * NV, 6 * FN)
    )
    surface = jnp.dot(
        placed, select, precision=highest, preferred_element_type=jnp.float32
    ).reshape(count_el, NV, VN)
    return elements + step_size * metric[:, None, None] * (volume + lift_weight * surface)


def shards(state, material, metric, mortar_proj, mortar_map, mortar_count, neighbours):
    select = jnp.asarray(face_select(), jnp.float32)
    mortar_info = mortar_map[0]
    counts = mortar_count[0]
    groups = lax.axis_size("grp")
    grp_index = lax.axis_index("grp")
    heat_ratio = 1.4 + 0.27 * material.astype(jnp.float32)
    face_rows = face_traces(state, select)
    operators = slot_operators(mortar_proj, mortar_info)
    native, native_heat = mortar_traces(face_rows, operators, heat_ratio, mortar_info)
    is_lower, is_live = slot_layout(groups, grp_index, counts)
    normal = normals_of(mortar_info[1])
    grp_slots = groups * CAPG
    upper_end = grp_slots + CAPS
    row_width = NV * FN
    arrived, arrived_heat = in_one_piece(
        (
            native[:grp_slots].reshape(groups, CAPG, row_width),
            native_heat[:grp_slots].reshape(groups, CAPG),
        ),
        "grp",
        0,
        0,
        2,
    )
    arrived = arrived.reshape(grp_slots, NV, FN)
    arrived_heat = arrived_heat.reshape(grp_slots)
    from_below, below_heat = from_behind(
        (native[grp_slots:upper_end].reshape(CAPS, row_width), native_heat[grp_slots:upper_end]),
        "elem",
        1,
    )
    from_below = from_below.reshape(CAPS, NV, FN)

    def skip_up(values):
        return jnp.concatenate([values[:grp_slots], values[upper_end:]], axis=0)

    partner = jnp.concatenate([arrived, from_below], axis=0)
    partner_heat = jnp.concatenate([arrived_heat, below_heat], axis=0)
    kept_lower = skip_up(is_lower)
    star_flux = mortar_flux(
        skip_up(native),
        partner,
        skip_up(native_heat),
        partner_heat,
        skip_up(normal),
        kept_lower,
        skip_up(is_live),
    )
    returned = from_behind(star_flux[grp_slots:].reshape(CAPS, row_width), "elem", -1)
    kept = jnp.where(kept_lower[:, None, None], star_flux, -star_flux)
    flux_own = jnp.concatenate(
        [kept[:grp_slots], returned.reshape(CAPS, NV, FN), kept[grp_slots:]], axis=0
    )
    volume = volume_term(state, heat_ratio)
    return section_update(
        state,
        heat_ratio,
        metric,
        mortar_info,
        neighbours,
        face_rows,
        operators,
        native,
        native_heat,
        flux_own,
        is_live,
        select,
        volume,
    )


def solution(mesh):
    return jax.shard_map(
        shards,
        mesh=mesh,
        in_specs=(
            P(("elem", "grp"), None, None),
            P(("elem", "grp")),
            P(("elem", "grp")),
            P(),
            P(("elem", "grp"), None, None),
            P(("elem", "grp"), None),
            P(("elem", "grp"), None),
        ),
        out_specs=P(("elem", "grp"), None, None),
        check_vma=False,
    )
```

profile of v0, /device:TPU:1, one launch (start us, length us, event | category | flops | bytes accessed | tf_op | source)
XLA Modules:
  0.0 134.3 jit_solution(4474177264113753372)
XLA Ops:
  0.0 0.7 fusion.78
  0.7 0.7 fusion.102
  1.3 6.3 %broadcast_add_fusion.2 = (f32[128]{0:T(128)}, f32[128]{0:T(128)S(1)}) fusion(f32[]{:T(128)} %bitcast.29, f32[]{:T(128)} %bitcast.28, f32[]{:T(128)} %bitcast.27, f32[]{:T(128)} %bitcast.26, f32[]{:T(128)} %bitcast.25, f32[]{:T(128)} %bitcast.24, f32[]{:T(128)} %bitcast.23, f32[]{:T(128)} %bitcast.22, s32[1,4,128]{2,1,0:T(4,128)} %param.14), kind=kLoop, calls=%fused_computation.294 | loop fusion | flops 2304 | bytes 1568 | tf_op jit(solution)/shard_map/sub | solution.py:88
  8.3 4.5 %collective-permute-start.1 = (f32[32]{0:T(128)}, f32[32]{0:T(128)}, u32[]{:S(2)}, u32[]{:S(2)}) collective-permute-start(f32[32]{0:T(128)} %get-tuple-element.141), channel_id=1, source_target_pairs={{0,8},{8,16},{16,24},{24,32},{32,40},{40,48},{48,56},{56,64},{64,7... | collective-permute-start | bytes 392 | tf_op jit(solution)/shard_map/ppermute | solution.py:36
  12.8 1.4 %fusion.75 = (s32[128]{0:T(128)S(1)}, s32[128,1]{0,1:T(1,128)}, s32[128]{0:T(128)S(1)}) fusion(s32[1,4,128]{2,1,0:T(4,128)} %param.14), kind=kLoop, calls=%fused_computation.278 | loop fusion | flops 1280 | bytes 3584 | tf_op jit(solution)/shard_map/select_n | solution.py:170
  14.2 2.4 %convolution_bitcast_fusion = f32[8,6,6,64]{3,0,2,1:T(8,128)S(1)} fusion(f32[6,64,512,1]{2,1,3,0:T(8,128)} %constant.195, f32[8,6,512]{2,0,1:T(8,128)} %param.10), kind=kOutput, calls=%fused_computation.27 | convolution fusion | flops 113246208 | bytes 958464 | tf_op jit(solution)/shard_map/dot_general | solution.py:155
  16.9 0.8 gather_fusion.1
  17.7 1.2 fusion.36
  18.8 2.8 %gather_fusion.2 = f32[128,64,64]{2,1,0:T(8,128)} fusion(f32[40,64,64]{2,1,0:T(8,128)S(1)} %bitcast.392, s32[1024]{0:T(1024)S(1)} %get-tuple-element.155), kind=kCustom, calls=%fused_computation.2 | custom fusion | bytes 4194816 | tf_op jit(solution)/shard_map/gather | solution.py:166
  21.6 8.3 %fusion.103 = f32[128,6,64]{2,1,0:T(8,128)S(1)} fusion(f32[128,6,64]{2,1,0:T(8,128)S(1)} %gather_fusion.1, f32[128,64,64]{2,1,0:T(8,128)} %gather_fusion.2), kind=kOutput, calls=%fused_computation.309 | convolution fusion | flops 37748736 | bytes 2490368 | tf_op jit(solution)/shard_map/spq,svq->svp/dot_general | solution.py:171
  30.1 0.7 pad_maximum_fusion.5
  30.8 15.3 %all-to-all-start = ((f32[8,8,385]{2,1,0:T(8,128)}), f32[8,8,385]{2,1,0:T(8,128)}, u32[]{:S(2)}, u32[]{:S(2)}) async-start(f32[8,8,385]{2,1,0:T(8,128)} %pad_maximum_fusion.5), calls=%async_computation | async-start | bytes 262144 | tf_op jit(solution)/shard_map/all_to_all | solution.py:28
  46.8 0.7 reshape.1664
  47.5 1.9 %collective-permute-start = (f32[32,384]{1,0:T(8,128)}, f32[32,384]{1,0:T(8,128)}, u32[]{:S(2)}, u32[]{:S(2)}) collective-permute-start(f32[32,384]{1,0:T(8,128)} %reshape.1664), channel_id=1, source_target_pairs={{0,8},{8,16},{16,24},{24,32},{32,40},{40,48},{48,56},{56,64},{64,7... | collective-permute-start | bytes 147464 | tf_op jit(solution)/shard_map/ppermute | solution.py:36
  55.9 0.7 multiply_add_fusion.5
  57.1 1.2 copy.179
  58.6 2.5 %fusion.8 = f32[8,6,8,8,8]{4,3,2,1,0:T(8,128)S(1)} fusion(f32[8,8,1,1,1]{1,0,4,3,2:T(8,128)S(1)} %copy-done.27, f32[8,1,8,8,8]{3,4,2,1,0:T(8,128)S(1)} %copy.181, f32[8,1,8,8,8]{3,4,2,1,0:T(8,128)S(1)} %copy.180, f32[8,3,8,8,8]{3,4,2,1,0:T(8,128)} %copy.179, f32[8,1,8,8,8]{3,4,2,1,0:T(8,128)S(1)} %copy.178), kind=kOutput, calls=%fused_computation.12 | convolution fusion | flops 2433024 | bytes 196864 | tf_op jit(solution)/shard_map/jb,evabc->evajc/dot_general | solution.py:219
  61.1 1.7 %copy.182 = f32[8,6,8,8,8]{2,3,4,1,0:T(8,128)} copy(f32[8,6,8,8,8]{4,3,2,1,0:T(8,128)S(1)} %fusion.8) | data formatting | bytes 196608 | tf_op jit(solution)/shard_map/jb,evabc->evajc/dot_general | solution.py:219
  63.3 0.9 copy.176
  65.1 0.9 copy.174
  66.0 0.9 concatenate.179
  66.9 0.8 concatenate.178
  67.7 0.9 concatenate.176
  69.8 0.7 fusion.100
  70.5 5.2 %broadcast_add_fusion.4 = (f32[48]{0:T(128)S(1)}, f32[48]{0:T(128)S(1)}, f32[48]{0:T(128)S(1)}, f32[48]{0:T(128)S(1)}) fusion(f32[]{:T(128)} %bitcast.29, f32[]{:T(128)} %bitcast.28, f32[]{:T(128)} %bitcast.27, f32[]{:T(128)} %bitcast.26, f32[]{:T(128)} %bitcast.25, f32[]{:T(128)} %bitcast.24, f32[]{:T(128)} %bitcast.23, f32[]{:T(128)} %bitcast.22, ...), kind=kLoop, calls=%fused_computation.296 | loop fusion | flops 1824 | bytes 1184 | tf_op jit(solution)/shard_map/sub | solution.py:88
  76.7 0.7 compare_bitcast_fusion.5
  77.5 0.7 compare_bitcast_fusion.4
  79.4 0.9 slice_multiply_fusion.1
  80.3 0.9 multiply_add_fusion
  81.2 0.7 select_reduce_fusion
  82.0 0.8 add_multiply_fusion.7
  82.8 0.8 multiply_divide_fusion.2
  83.6 2.5 %fusion = f32[8,6,8,8,8]{4,3,2,1,0:T(8,128)S(1)} fusion(f32[8,8,1,1,1]{1,0,4,3,2:T(8,128)S(1)} %copy-done.27, f32[8,1,8,8,8]{2,4,3,1,0:T(8,128)S(1)} %copy.177, f32[8,1,8,8,8]{2,4,3,1,0:T(8,128)} %copy.176, f32[8,3,8,8,8]{2,4,3,1,0:T(8,128)S(1)} %copy.175, f32[8,1,8,8,8]{2,4,3,1,0:T(8,128)} %copy.174), kind=kOutput, calls=%fused_computation.4 | convolution fusion | flops 2433024 | bytes 196864 | tf_op jit(solution)/shard_map/ia,evabc->evibc/dot_general | solution.py:218
  86.3 1.2 copy-done.2
  87.6 21.0 %fusion.17 = f32[8,6,8,8,8]{2,4,3,1,0:T(8,128)S(1)} fusion(f32[8,6,8,8,8]{2,3,4,1,0:T(8,128)S(1)} %copy-done.2, f32[8,6,8,8,8]{4,3,2,1,0:T(8,128)S(1)} %fusion, f32[8,8,1,1,1]{1,0,4,3,2:T(8,128)S(1)} %copy-done.27, f32[8,6,8,8,8]{4,3,2,1,0:T(8,128)S(1)} %pad_maximum_fusion), kind=kOutput, calls=%fused_computation.23 | convolution fusion | flops 2433024 | bytes 393472 | tf_op jit(solution)/shard_map/kc,evabc->evabk/dot_general | solution.py:220
  110.0 0.9 copy.226
  110.9 0.8 slice_reduce_fusion
  111.8 0.9 split.8
  113.0 0.7 broadcast_add_fusion
  114.0 0.7 broadcast_add_fusion.1
  115.3 0.7 copy.227
  116.0 1.5 %collective-permute-start.2 = (f32[32,384]{1,0:T(8,128)}, f32[32,384]{1,0:T(8,128)}, u32[]{:S(2)}, u32[]{:S(2)}) collective-permute-start(f32[32,384]{1,0:T(8,128)} %copy.227), channel_id=1, source_target_pairs={{8,0},{16,8},{24,16},{32,24},{40,32},{48,40},{56,48},{64,56},{72,6... | collective-permute-start | bytes 147464 | tf_op jit(solution)/shard_map/ppermute | solution.py:36
  118.2 0.8 neg.17
  119.6 1.6 %collective-permute-done.2 = f32[32,384]{1,0:T(8,128)} collective-permute-done((f32[32,384]{1,0:T(8,128)}, f32[32,384]{1,0:T(8,128)}, u32[]{:S(2)}, u32[]{:S(2)}) %collective-permute-start.2) | collective-permute-done | bytes 49184 | tf_op jit(solution)/shard_map/ppermute | solution.py:36
  121.2 0.9 copy.228
  122.6 5.3 %convolution_multiply_fusion = f32[128,6,64]{2,1,0:T(8,128)S(1)} fusion(f32[128,6,64]{2,1,0:T(8,128)S(1)} %copy.219, f32[128,64,64]{2,1,0:T(8,128)} %gather_fusion.2, f32[128]{0:T(128)S(1)} %copy-done.46), kind=kOutput, calls=%fused_computation.26 | convolution fusion | flops 37797888 | bytes 2490880 | tf_op jit(solution)/shard_map/spq,svp->svq/dot_general | solution.py:244
  127.9 5.0 %scatter_fusion = f32[48,6,64]{2,1,0:T(8,128)S(1)} fusion(f32[48,6,64]{2,1,0:T(8,128)S(1)} %fusion.26, s32[128]{0:T(128)S(1)} %bitcast.442, f32[128,6,64]{2,1,0:T(8,128)S(1)} %convolution_multiply_fusion), kind=kCustom, calls=%fused_computation.3 | custom fusion | flops 49152 | bytes 590336 | tf_op jit(solution)/shard_map/scatter-add | solution.py:264
  133.0 1.2 fusion.24
  (196 shorter events, 18.0 us)
Async XLA Ops:
  8.3 104.7 %collective-permute-start.1 = (f32[32]{0:T(128)}, f32[32]{0:T(128)}, u32[]{:S(2)}, u32[]{:S(2)}) collective-permute-start(f32[32]{0:T(128)} %get-tuple-element.141), channel_id=1, source_target_pairs={{0,8},{8,16},{16,24},{24,32},{32,40},{40,48},{48,56},{56,64},{64,7... | collective-permute-start | bytes 392 | tf_op jit(solution)/shard_map/ppermute | solution.py:36
  14.2 3.5 %copy-start.11 = (f32[8,64,64,1]{2,1,0,3:T(8,128)S(1)}, f32[8,64,64,1]{2,1,0,3:T(8,128)}, u32[]{:S(2)}) copy-start(f32[8,64,64,1]{2,1,0,3:T(8,128)} %constant.196) | copy-start | bytes 393220
  14.2 3.5 %copy-start.22 = (f32[4,64,64]{2,1,0:T(8,128)S(1)}, f32[4,64,64]{2,1,0:T(8,128)}, u32[]{:S(2)}) copy-start(f32[4,64,64]{2,1,0:T(8,128)} %param.13) | copy-start | bytes 196612
  29.9 25.1 %copy-start = (f32[128,6,64]{2,1,0:T(8,128)}, f32[128,6,64]{2,1,0:T(8,128)S(1)}, u32[]{:S(2)}) copy-start(f32[128,6,64]{2,1,0:T(8,128)S(1)} %fusion.103) | copy-start | bytes 589828
  29.9 19.4 %copy-start.3 = (f32[8,6,512]{2,0,1:T(8,128)S(1)}, f32[8,6,512]{2,0,1:T(8,128)}, u32[]{:S(2)}) copy-start(f32[8,6,512]{2,0,1:T(8,128)} %param.10) | copy-start | bytes 294916
  30.0 21.3 %copy-start.31 = (s32[8,6]{1,0:T(8,128)S(1)}, s32[8,6]{1,0:T(8,128)}, u32[]{:S(2)}) copy-start(s32[8,6]{1,0:T(8,128)} %param.16) | copy-start | bytes 580
  30.0 22.4 %copy-start.34 = (s32[1,4,128]{2,1,0:T(4,128)S(1)}, s32[1,4,128]{2,1,0:T(4,128)}, u32[]{:S(2)}) copy-start(s32[1,4,128]{2,1,0:T(4,128)} %param.14) | copy-start | bytes 6148
  30.8 80.1 %all-to-all-start = ((f32[8,8,385]{2,1,0:T(8,128)}), f32[8,8,385]{2,1,0:T(8,128)}, u32[]{:S(2)}, u32[]{:S(2)}) async-start(f32[8,8,385]{2,1,0:T(8,128)} %pad_maximum_fusion.5), calls=%async_computation | async-start | bytes 262144 | tf_op jit(solution)/shard_map/all_to_all | solution.py:28
  47.5 62.5 %collective-permute-start = (f32[32,384]{1,0:T(8,128)}, f32[32,384]{1,0:T(8,128)}, u32[]{:S(2)}, u32[]{:S(2)}) collective-permute-start(f32[32,384]{1,0:T(8,128)} %reshape.1664), channel_id=1, source_target_pairs={{0,8},{8,16},{16,24},{24,32},{32,40},{40,48},{48,56},{56,64},{64,7... | collective-permute-start | bytes 147464 | tf_op jit(solution)/shard_map/ppermute | solution.py:36
  51.2 25.2 %copy-start.16 = (f32[48,64]{1,0:T(8,128)}, f32[48,64]{1,0:T(8,128)S(1)}, u32[]{:S(2)}) copy-start(f32[48,64]{1,0:T(8,128)S(1)} %slice_bitcast_fusion.2) | copy-start | bytes 36868
  56.6 1.9 %copy-start.27 = (f32[8,8,1,1,1]{1,0,4,3,2:T(8,128)S(1)}, f32[8,8,1,1,1]{1,0,4,3,2:T(8,128)}, u32[]{:S(2)}) copy-start(f32[8,8,1,1,1]{1,0,4,3,2:T(8,128)} %constant.194) | copy-start | bytes 772
  61.1 1.8 %copy-start.25 = (f32[8,1,512]{2,0,1:T(8,128)S(1)}, f32[8,1,512]{2,0,1:T(8,128)}, u32[]{:S(2)}) copy-start(f32[8,1,512]{2,0,1:T(8,128)} %get-tuple-element.106) | copy-start | bytes 49156
  61.1 2.1 %copy-start.26 = (f32[8,1,512]{2,0,1:T(8,128)S(1)}, f32[8,1,512]{2,0,1:T(8,128)}, u32[]{:S(2)}) copy-start(f32[8,1,512]{2,0,1:T(8,128)} %get-tuple-element.131) | copy-start | bytes 49156
  63.1 1.8 %copy-start.24 = (f32[8,1,512]{2,0,1:T(8,128)S(1)}, f32[8,1,512]{2,0,1:T(8,128)}, u32[]{:S(2)}) copy-start(f32[8,1,512]{2,0,1:T(8,128)} %get-tuple-element.107) | copy-start | bytes 49156
  64.2 1.8 %copy-start.23 = (f32[8,1,512]{2,0,1:T(8,128)S(1)}, f32[8,1,512]{2,0,1:T(8,128)}, u32[]{:S(2)}) copy-start(f32[8,1,512]{2,0,1:T(8,128)} %get-tuple-element.96) | copy-start | bytes 49156
  64.6 4.0 %copy-start.20 = (f32[8,3,512]{2,0,1:T(8,128)S(1)}, f32[8,3,512]{2,0,1:T(8,128)}, u32[]{:S(2)}) copy-start(f32[8,3,512]{2,0,1:T(8,128)} %get-tuple-element.97) | copy-start | bytes 147460
  64.9 4.1 %copy-start.32 = (s32[8,6]{1,0:T(8,128)S(1)}, s32[8,6]{1,0:T(8,128)}, u32[]{:S(2)}) copy-start(s32[8,6]{1,0:T(8,128)} %iota_xor_fusion) | copy-start | bytes 580
  64.9 4.2 %copy-start.39 = (s32[48,1]{0,1:T(1,128)S(1)}, s32[48,1]{0,1:T(1,128)}, u32[]{:S(2)}) copy-start(s32[48,1]{0,1:T(1,128)} %reshape.1660) | copy-start | bytes 580
  64.9 10.7 %copy-start.41 = (pred[8,6]{1,0:T(8,128)(4,1)S(1)}, pred[8,6]{1,0:T(8,128)(4,1)}, u32[]{:S(2)}) copy-start(pred[8,6]{1,0:T(8,128)(4,1)} %broadcast_compare_fusion) | copy-start | bytes 148
  64.9 11.4 %copy-start.43 = (f32[48]{0:T(128)S(1)}, f32[48]{0:T(128)}, u32[]{:S(2)}) copy-start(f32[48]{0:T(128)} %compare_select_fusion.31) | copy-start | bytes 580
  65.0 11.4 %copy-start.44 = (s32[48]{0:T(128)S(1)}, s32[48]{0:T(128)}, u32[]{:S(2)}) copy-start(s32[48]{0:T(128)} %and_select_fusion.6) | copy-start | bytes 580
  66.0 12.8 %copy-start.48 = (s32[128]{0:T(128)S(1)}, s32[128]{0:T(128)}, u32[]{:S(2)}) copy-start(s32[128]{0:T(128)} %get-tuple-element.43) | copy-start | bytes 1540
  66.0 12.8 %copy-start.45 = (s32[128]{0:T(128)S(1)}, s32[128]{0:T(128)}, u32[]{:S(2)}) copy-start(s32[128]{0:T(128)} %get-tuple-element.42) | copy-start | bytes 1540
  66.9 12.1 %copy-start.1 = (f32[128,6,64]{2,1,0:T(8,128)S(1)}, f32[128,6,64]{2,1,0:T(8,128)}, u32[]{:S(2)}) copy-start(f32[128,6,64]{2,1,0:T(8,128)} %copy-done) | copy-start | bytes 589828
  66.9 12.1 %slice-start = ((f32[128,6,64]{2,1,0:T(8,128)}), f32[128,1,64]{2,1,0:T(1,128)S(1)}, s32[]{:S(2)}) async-start(f32[128,6,64]{2,1,0:T(8,128)} %copy-done), calls=%async_computation.1 | async-start | bytes 131072 | tf_op jit(solution)/shard_map/slice | solution.py:83
  68.6 10.8 %copy-start.40 = (f32[128]{0:T(128)S(1)}, f32[128]{0:T(128)}, u32[]{:S(2)}) copy-start(f32[128]{0:T(128)} %get-tuple-element.40) | copy-start | bytes 1540
  70.4 8.4 %copy-start.15 = (f32[48,1,64]{2,1,0:T(1,128)}, f32[48,1,64]{2,1,0:T(1,128)S(1)}, u32[]{:S(2)}) copy-start(f32[48,1,64]{2,1,0:T(1,128)S(1)} %get-tuple-element.89) | copy-start | bytes 36868
  76.4 2.4 %copy-start.18 = (f32[48,3]{1,0:T(8,128)}, f32[48,3]{1,0:T(8,128)S(1)}, u32[]{:S(2)}) copy-start(f32[48,3]{1,0:T(8,128)S(1)} %fusion.59) | copy-start | bytes 1732
  82.0 27.8 %copy-start.35 = (pred[128]{0:T(512)(128)(4,1)}, pred[128]{0:T(512)(128)(4,1)S(1)}, u32[]{:S(2)}) copy-start(pred[128]{0:T(512)(128)(4,1)S(1)} %fusion.69) | copy-start | bytes 388
  83.6 2.5 %copy-start.5 = (f32[8,1,8,8,8]{4,3,2,1,0:T(8,128)S(1)}, f32[8,1,8,8,8]{4,3,2,1,0:T(8,128)}, u32[]{:S(2)}) copy-start(f32[8,1,8,8,8]{4,3,2,1,0:T(8,128)} %concatenate.179) | copy-start | bytes 49156
  83.6 2.5 %copy-start.6 = (f32[8,1,8,8,8]{4,3,2,1,0:T(8,128)S(1)}, f32[8,1,8,8,8]{4,3,2,1,0:T(8,128)}, u32[]{:S(2)}) copy-start(f32[8,1,8,8,8]{4,3,2,1,0:T(8,128)} %concatenate.178) | copy-start | bytes 49156
  83.6 2.5 %copy-start.7 = (f32[8,1,8,8,8]{4,3,2,1,0:T(8,128)S(1)}, f32[8,1,8,8,8]{4,3,2,1,0:T(8,128)}, u32[]{:S(2)}) copy-start(f32[8,1,8,8,8]{4,3,2,1,0:T(8,128)} %concatenate.176) | copy-start | bytes 49156
  86.1 1.4 %copy-start.2 = (f32[8,6,8,8,8]{2,3,4,1,0:T(8,128)S(1)}, f32[8,6,8,8,8]{2,3,4,1,0:T(8,128)}, u32[]{:S(2)}) copy-start(f32[8,6,8,8,8]{2,3,4,1,0:T(8,128)} %copy.182) | copy-start | bytes 294916
  87.5 21.0 %copy-start.17 = (f32[48,64]{1,0:T(8,128)S(1)}, f32[48,64]{1,0:T(8,128)}, u32[]{:S(2)}) copy-start(f32[48,64]{1,0:T(8,128)} %copy-done.16) | copy-start | bytes 36868
  87.5 21.0 %copy-start.19 = (f32[48,3]{1,0:T(8,128)S(1)}, f32[48,3]{1,0:T(8,128)}, u32[]{:S(2)}) copy-start(f32[48,3]{1,0:T(8,128)} %copy-done.18) | copy-start | bytes 1732
  87.5 21.3 %copy-start.28 = (pred[48,64]{1,0:T(8,128)(4,1)S(1)}, pred[48,64]{1,0:T(8,128)(4,1)}, u32[]{:S(2)}) copy-start(pred[48,64]{1,0:T(8,128)(4,1)} %compare_bitcast_fusion.3) | copy-start | bytes 9220
  87.5 21.3 %copy-start.29 = (pred[48,64]{1,0:T(8,128)(4,1)S(1)}, pred[48,64]{1,0:T(8,128)(4,1)}, u32[]{:S(2)}) copy-start(pred[48,64]{1,0:T(8,128)(4,1)} %get-tuple-element.46) | copy-start | bytes 9220
  87.5 21.3 %copy-start.30 = (pred[48,64]{1,0:T(8,128)(4,1)S(1)}, pred[48,64]{1,0:T(8,128)(4,1)}, u32[]{:S(2)}) copy-start(pred[48,64]{1,0:T(8,128)(4,1)} %get-tuple-element.50) | copy-start | bytes 9220
  87.6 21.3 %copy-start.42 = (pred[48]{0:T(512)(128)(4,1)S(1)}, pred[48]{0:T(512)(128)(4,1)}, u32[]{:S(2)}) copy-start(pred[48]{0:T(512)(128)(4,1)} %ge.49) | copy-start | bytes 148
  108.8 4.1 %copy-start.33 = (f32[32]{0:T(128)S(1)}, f32[32]{0:T(128)}, u32[]{:S(2)}) copy-start(f32[32]{0:T(128)} %get-tuple-element.142) | copy-start | bytes 388
  109.8 3.2 %copy-start.36 = (pred[128]{0:T(512)(128)(4,1)S(1)}, pred[128]{0:T(512)(128)(4,1)}, u32[]{:S(2)}) copy-start(pred[128]{0:T(512)(128)(4,1)} %copy-done.35) | copy-start | bytes 388
  115.0 2.6 %copy-start.47 = (f32[8]{0:T(128)S(1)}, f32[8]{0:T(128)}, u32[]{:S(2)}) copy-start(f32[8]{0:T(128)} %param.12) | copy-start | bytes 100
  116.0 5.1 %collective-permute-start.2 = (f32[32,384]{1,0:T(8,128)}, f32[32,384]{1,0:T(8,128)}, u32[]{:S(2)}, u32[]{:S(2)}) collective-permute-start(f32[32,384]{1,0:T(8,128)} %copy.227), channel_id=1, source_target_pairs={{8,0},{16,8},{24,16},{32,24},{40,32},{48,40},{56,48},{64,56},{72,6... | collective-permute-start | bytes 147464 | tf_op jit(solution)/shard_map/ppermute | solution.py:36
  118.2 3.9 %copy-start.37 = (pred[128]{0:T(512)(128)(4,1)S(1)}, pred[128]{0:T(512)(128)(4,1)}, u32[]{:S(2)}) copy-start(pred[128]{0:T(512)(128)(4,1)} %copy-done.35) | copy-start | bytes 388
  119.0 3.5 %copy-start.46 = (f32[128]{0:T(128)S(1)}, f32[128]{0:T(128)}, u32[]{:S(2)}) copy-start(f32[128]{0:T(128)} %fusion.71) | copy-start | bytes 1540
  122.6 5.3 %copy-start.38 = (s32[128,1]{0,1:T(1,128)S(1)}, s32[128,1]{0,1:T(1,128)}, u32[]{:S(2)}) copy-start(s32[128,1]{0,1:T(1,128)} %get-tuple-element.45) | copy-start | bytes 1540
  127.9 5.2 %copy-start.4 = (f32[8,6,512]{2,0,1:T(8,128)S(1)}, f32[8,6,512]{2,0,1:T(8,128)}, u32[]{:S(2)}) copy-start(f32[8,6,512]{2,0,1:T(8,128)} %param.10) | copy-start | bytes 294916
  127.9 5.1 %copy-start.9 = (f32[384,512,1]{1,0,2:T(8,128)S(1)}, f32[384,512,1]{1,0,2:T(8,128)}, u32[]{:S(2)}) copy-start(f32[384,512,1]{1,0,2:T(8,128)} %constant.197) | copy-start | bytes 2359300
  (6 other events, 6.6 us)
where the time goes:
time: 135 us; the launch traced here: 134 us
  matrix products  44.4 us (33%)
  other arithmetic  35.5 us (26%)
  local copies, waits for them, and re-layouts  28.5 us (21%)
  starting transfers between devices  23.2 us (17%)
  waiting for transfers between devices  1.62 us (1%)
    dot_general x1, matrix products, volume_term(): jnp.einsum('kc,evabc->evabk', deriv, fluxes[2], precision=highest)  21 us
    all_to_all x1, starting transfers between devices, in_one_piece(): lax.all_to_all(both, axis, split_axis=split_dim, concat_axis=concat_dim,...  15.3 us
    sub x4, other arithmetic, state_parts(): heat_ratio[:, None] - 1.0  12.9 us
    concatenate x20, local copies, waits for them, and re-layouts, state_parts(): jnp.concatenate([(density * speed_n)[:, None], momentum * speed_n[:, None...  8.49 us
    dot_general x1, matrix products, mortar_traces(): native = jnp.einsum('spq,svq->svp', operators, picked, precision=highest)  8.31 us
    ppermute x3, starting transfers between devices, from_behind(): return lax.ppermute(block, axis, route)  7.89 us
    dot_general x1, matrix products, section_update(): jnp.einsum('spq,svp->svq', operators, correction, precision=highest)  5.3 us
    scatter-add x1, other arithmetic, section_update(): jax.ops.segment_sum(projected, mortar_info[0] * 6 + mortar_info[1], num_s...  4.97 us
  transfers between devices with their start and end apart: 4, of which 1 were waited for; matrix products, arithmetic and copies ran while one was open for 62% of the time, Pallas kernels for 0%

commit v1 on v0

v1 whole, which is shorter than its diff:
```python
import functools

import jax
import jax.numpy as jnp
import numpy as np
from jax import lax
from jax.experimental import pallas as pl
from jax.experimental.pallas import tpu as pltpu
from jax.sharding import PartitionSpec as P

CAPG = 8
CAPS = 32
SLOTS = 128
STEP = 0.002
LIFT = 49.0

f32 = jnp.float32
bf16 = jnp.bfloat16


def cheb_matrix():
    points = -np.cos(np.pi * np.arange(8) / 7.0)
    factor = np.array([2.0, 1.0, 1.0, 1.0, 1.0, 1.0, 1.0, 2.0])
    alternating = np.where(np.arange(8) % 2 == 0, 1.0, -1.0)
    scaled = factor * alternating
    differ = points[:, None] - points[None, :] + np.eye(8)
    matrix = scaled[:, None] / scaled[None, :] / differ
    matrix = matrix * (1.0 - np.eye(8))
    return (matrix - np.eye(8) * matrix.sum(axis=1)[:, None]).astype(np.float32)


def face_select():
    grid = np.arange(512).reshape(8, 8, 8)
    planes = [grid[:, 0], grid[:, 7], grid[:, :, 0], grid[:, :, 7]]
    nodes = np.concatenate([p.reshape(64) for p in planes])
    return (np.arange(512)[:, None] == nodes[None, :]).astype(np.float32)


def orient_table():
    first, second = np.meshgrid(np.arange(8), np.arange(8), indexing="ij")
    out = np.zeros((128, 1024), np.float32)
    for orient in range(8):
        p, r = (second, first) if orient & 4 else (first, second)
        p = 7 - p if orient & 1 else p
        r = 7 - r if orient & 2 else r
        source = (8 * p + r).reshape(64)
        for half in range(2):
            out[half * 64 + source, orient * 128 + half * 64 + np.arange(64)] = 1.0
    return out


def deriv_table():
    d = cheb_matrix()
    along_b = np.kron(np.eye(2), np.kron(d, np.eye(8))).T
    along_c = np.kron(np.eye(16), d).T
    return np.concatenate([along_b, along_c], axis=0).astype(np.float32)


def code_table(rows):
    out = np.zeros((16, 128 * len(rows)), np.float32)
    for block, weights in enumerate(rows):
        for row, weight in weights.items():
            out[row, block * 128 : (block + 1) * 128] = weight
    return out


def dot(a, b, ca=1, cb=0):
    return lax.dot_general(a, b, (((ca,), (cb,)), ((), ())), preferred_element_type=f32)


def split2(x):
    hi = x.astype(bf16)
    return hi, (x - hi.astype(f32)).astype(bf16)


def split3(x):
    hi = x.astype(bf16)
    rest = x - hi.astype(f32)
    mid = rest.astype(bf16)
    return hi, mid, (rest - mid.astype(f32)).astype(bf16)


def lane_low(shape):
    return lax.broadcasted_iota(jnp.int32, shape, len(shape) - 1) % 128 < 64


def swap(x):
    return pltpu.roll(x, 64, 1)


def join_pair(low, a, b):
    return jnp.where(low, a, swap(b))


def by_element(ref, shape):
    row = lax.broadcasted_iota(jnp.int32, shape, 0)
    out = jnp.full(shape, ref[0], f32) if ref.dtype == f32 else jnp.full(shape, ref[0].astype(f32), f32)
    for e in range(1, 8):
        out = jnp.where(row == e, ref[e].astype(f32), out)
    return out


def project_blocks(proj_ref):
    zero = jnp.zeros((64, 64), f32)
    blocks = []
    for s in range(4):
        p = proj_ref[s]
        top = jnp.concatenate([p, zero], axis=1)
        bottom = jnp.concatenate([zero, p], axis=1)
        blocks.append(jnp.concatenate([top, bottom], axis=0))
    return blocks


def slot_material(mat_ref, element):
    out = jnp.zeros(element.shape, f32)
    for e in range(8):
        out = jnp.where(element == e, mat_ref[e].astype(f32), out)
    return out


def code_rows(rows):
    pad = [jnp.zeros((1, SLOTS), f32)] * (16 - len(rows))
    return jnp.concatenate(rows + pad, axis=0).astype(bf16)


def trace_kernel(state_ref, mat_ref, map_ref, proj_ref, sel_ref, orient_ref, code_ref, out_ref, face_ref):
    low = lane_low((8, 128))
    flat = state_ref[...].reshape(48, 512)
    picked = dot(jnp.concatenate(split3(flat), axis=0), sel_ref[...])
    picked = picked[0:48] + picked[48:96] + picked[96:144]
    pairs = []
    for v in range(6):
        x = state_ref[v]
        pairs.append(
            [
                jnp.where(low, x[:, 0:128], x[:, 384:512]),
                picked[8 * v : 8 * v + 8, 0:128],
                picked[8 * v : 8 * v + 8, 128:256],
            ]
        )
    rows = []
    for j in range(3):
        for d in range(3):
            first, second = pairs[2 * j][d], pairs[2 * j + 1][d]
            rows.append(jnp.where(low, first, swap(second)))
            rows.append(jnp.where(low, swap(first), second))
    faces = jnp.concatenate(rows, axis=0)
    face_ref[...] = faces
    hi, lo = split2(faces)
    table = dot(jnp.concatenate([hi, lo], axis=0), orient_ref[...]).astype(bf16)
    info = map_ref[...]
    element, face, sub, orient = (info[i : i + 1] for i in range(4))
    material = slot_material(mat_ref, element)
    codes = code_rows([element.astype(f32), face.astype(f32), sub.astype(f32), orient.astype(f32), material])
    spread = dot(codes, code_ref[...], 0, 0)
    index = spread[:, 0:128].astype(jnp.int32)
    sub_of = spread[:, 128:256].astype(jnp.int32)
    lane = lax.broadcasted_iota(jnp.int32, (SLOTS, 128), 1)
    one_hot = jnp.concatenate(
        [jnp.where(index == lane + 128 * t, 1.0, 0.0).astype(bf16) for t in range(3)], axis=1
    )
    columns = []
    for part in range(6):
        block = table[48 * part : 48 * part + 48]
        columns.append(jnp.concatenate([block[:, 128 * o : 128 * o + 128] for o in range(8)], axis=0))
    gathered = dot(one_hot, jnp.concatenate(columns, axis=1))
    x_hi = jnp.concatenate([gathered[:, 128 * j : 128 * j + 128] for j in range(3)], axis=0)
    x_lo = jnp.concatenate([gathered[:, 384 + 128 * j : 512 + 128 * j] for j in range(3)], axis=0)
    b_hi, b_lo = split2(jnp.concatenate(project_blocks(proj_ref), axis=0))
    h = x_hi.astype(bf16)
    wide = dot(
        jnp.concatenate([h, x_lo.astype(bf16)], axis=1), jnp.concatenate([b_hi, b_hi], axis=1), 1, 1
    ) + dot(h, b_lo, 1, 1)
    for j in range(3):
        r = slice(128 * j, 128 * j + 128)
        w = x_hi[r] + x_lo[r]
        for s in range(4):
            w = jnp.where(sub_of == s + 1, wide[r, 128 * s : 128 * s + 128], w)
        out_ref[:, 128 * j : 128 * j + 128] = w
    out_ref[:, 384:512] = 1.4 + 0.27 * spread[:, 256:384]


def hllc_correction(u, g, normal, own):
    inv = 1.0 / u[0]
    vel = [u[1] * inv, u[2] * inv, u[3] * inv]
    p = (g - 1.0) * (u[4] - 0.5 * (u[1] * vel[0] + u[2] * vel[1] + u[3] * vel[2]))
    s = normal[0] * vel[0] + normal[1] * vel[1] + normal[2] * vel[2]
    c = jnp.sqrt(g * p * inv)
    lower, upper = s - c, s + c
    left = jnp.minimum(lower, swap(lower))
    right = jnp.maximum(upper, swap(upper))
    wave = jnp.where(own, left, right)
    relative = wave - s
    mass = u[0] * relative
    part = mass * s - p
    middle = (part - swap(part)) / (mass - swap(mass))
    chi = mass / (wave - middle)
    shift = middle - s
    star = [
        chi,
        chi * (vel[0] + shift * normal[0]),
        chi * (vel[1] + shift * normal[1]),
        chi * (vel[2] + shift * normal[2]),
        chi * (u[4] * inv + shift * (middle + p / mass)),
        chi * (u[5] * inv),
    ]
    flux = [
        u[0] * s,
        u[1] * s + p * normal[0],
        u[2] * s + p * normal[1],
        u[3] * s + p * normal[2],
        (u[4] + p) * s,
        u[5] * s,
    ]
    use_star = jnp.where(own, -wave, wave) > 0.0
    take_own = (left >= 0.0) | (middle >= 0.0)
    out = []
    for v in range(6):
        side = jnp.where(use_star, wave * (star[v] - u[v]), 0.0)
        out.append(jnp.where(take_own, -side, flux[v] - swap(flux[v] + side)))
    return out


def paired(own, mine, theirs):
    return jnp.where(own, mine, swap(theirs)), jnp.where(own, swap(mine), theirs)


def local_kernel(state_ref, mat_ref, metric_ref, near_ref, face_ref, deriv_ref, base_ref, local_ref):
    heat = 1.4 + 0.27 * by_element(mat_ref, (8, 512))
    u = [state_ref[v] for v in range(6)]
    inv = 1.0 / u[0]
    vel = [u[1] * inv, u[2] * inv, u[3] * inv]
    p = (heat - 1.0) * (u[4] - 0.5 * (u[1] * vel[0] + u[2] * vel[1] + u[3] * vel[2]))
    fluxes = []
    for d in range(3):
        s = vel[d]
        f = [u[0] * s, u[1] * s, u[2] * s, u[3] * s, (u[4] + p) * s, u[5] * s]
        f[1 + d] = f[1 + d] + p
        fluxes.append(f)
    rows = []
    for v in range(6):
        for t in range(4):
            r = slice(128 * t, 128 * t + 128)
            rows.append(jnp.concatenate([fluxes[1][v][:, r], fluxes[2][v][:, r]], axis=1))
    hi, lo = split2(jnp.concatenate(rows, axis=0))
    d_hi, d_lo = deriv_ref[:, 0:128], deriv_ref[:, 128:256]
    main = dot(jnp.concatenate([hi, lo], axis=0), d_hi)
    bc = main[0:192] + main[192:384] + dot(hi, d_lo)
    low = lane_low((8, 128))
    deriv = cheb_matrix()
    scale = STEP * by_element(metric_ref, (8, 128))
    for v in range(6):
        x = [fluxes[0][v][:, 128 * t : 128 * t + 128] for t in range(4)]
        xs = [swap(a) for a in x]
        for t in range(4):
            acc = bc[32 * v + 8 * t : 32 * v + 8 * t + 8]
            for k in range(4):
                same = jnp.where(low, float(deriv[2 * t, 2 * k]), float(deriv[2 * t + 1, 2 * k + 1]))
                cross = jnp.where(low, float(deriv[2 * t, 2 * k + 1]), float(deriv[2 * t + 1, 2 * k]))
                acc = acc + same * x[k] + cross * xs[k]
            r = slice(128 * t, 128 * t + 128)
            base_ref[v, :, r] = u[v][:, r] - scale * acc
    faces = face_ref[...]
    lane = lax.broadcasted_iota(jnp.int32, (8, 256), 1)
    hot, live = [], []
    for k in range(6):
        near = jnp.broadcast_to(near_ref[:, k : k + 1], (8, 256))
        live.append((near >= 0)[:, 0:128])
        target = 8 * (k ^ 1) + near
        hit = (jnp.bitwise_and(lane, 63) == target) & (near >= 0) & (lane < 192)
        hot.append(jnp.where(hit, 1.0, 0.0))
    hot = jnp.concatenate(hot, axis=0).astype(bf16)
    heat_rows = jnp.concatenate([heat[:, 0:128]] * 6, axis=0)
    table = jnp.concatenate([faces[0:48], faces[48:96], faces[96:144], heat_rows], axis=1)
    gap = jnp.zeros((16, 512), bf16)
    terms = []
    for term in split3(table):
        terms += [term, gap]
    terms.append(jnp.zeros((64, 512), bf16))
    theirs = dot(hot, jnp.concatenate(terms, axis=0))
    own = lane_low((48, 128))
    row = lax.broadcasted_iota(jnp.int32, (48, 128), 0)
    sign = jnp.where(jnp.bitwise_and(row, 8) != 0, 1.0, -1.0)
    normal = [jnp.where(lax.shift_right_logical(row, 4) == d, sign, 0.0) for d in range(3)]
    states = []
    for j in range(3):
        states += paired(own, faces[48 * j : 48 * j + 48], theirs[:, 128 * j : 128 * j + 128])
    g = jnp.where(own, heat_rows, theirs[:, 384:512])
    corr = hllc_correction(states, g, normal, own)
    for j in range(3):
        packed = join_pair(own, corr[2 * j], corr[2 * j + 1])
        for k in range(6):
            local_ref[48 * j + 8 * k : 48 * j + 8 * k + 8, :] = jnp.where(
                live[k], packed[8 * k : 8 * k + 8], 0.0
            )


def mortar_kernel(
    mine_ref, grp_ref, above_ref, below_ref, mat_ref, metric_ref, count_ref, map_ref, proj_ref,
    sel_ref, orient_ref, code_ref, base_ref, local_ref, out_ref,
):
    info = map_ref[...]
    element, face, sub, orient = (info[i : i + 1] for i in range(4))
    slot = lax.broadcasted_iota(jnp.int32, (1, SLOTS), 1)
    group = jnp.where(
        slot < 64, lax.shift_right_logical(slot, 3), 6 + lax.shift_right_logical(slot, 5)
    )
    position = jnp.where(slot < 64, jnp.bitwise_and(slot, 7), jnp.bitwise_and(slot, 31))
    limit = jnp.zeros((1, SLOTS), jnp.int32)
    for n in range(10):
        limit = jnp.where(group == n, count_ref[n], limit)
    alive = jnp.where(position < limit, 1.0, 0.0)
    sign = jnp.where(jnp.bitwise_and(face, 1) == 1, 1.0, -1.0)
    axis = lax.shift_right_logical(face, 1)
    codes = code_rows(
        [sub.astype(f32), alive] + [jnp.where(axis == d, sign, 0.0) for d in range(3)]
    )
    spread = dot(codes, code_ref[...], 0, 0)
    chunk = 32
    own = lane_low((chunk, 128))
    packed = [[], [], []]
    for start in range(0, SLOTS, chunk):
        r = slice(start, start + chunk)
        if start < 64:
            theirs_ref, at = grp_ref, start
        elif start < 96:
            theirs_ref, at = above_ref, start - 64
        else:
            theirs_ref, at = below_ref, start - 96
        q = slice(at, at + chunk)
        states = []
        for j in range(3):
            lanes = slice(128 * j, 128 * j + 128)
            states += paired(own, mine_ref[r, lanes], theirs_ref[q, lanes])
        g = jnp.where(own, mine_ref[r, 384:512], theirs_ref[q, 384:512])
        live = spread[r, 128:256] > 0.5
        normal = [spread[r, 256 + 128 * d : 384 + 128 * d] for d in range(3)]
        corr = hllc_correction(states, g, normal, own)
        for j in range(3):
            packed[j].append(jnp.where(live, join_pair(own, corr[2 * j], corr[2 * j + 1]), 0.0))
    corr = jnp.concatenate(packed[0] + packed[1] + packed[2], axis=0)
    b_hi, b_lo = split2(jnp.concatenate(project_blocks(proj_ref), axis=1))
    hi, lo = split2(corr)
    wide = dot(jnp.concatenate([hi, lo], axis=1), jnp.concatenate([b_hi, b_hi], axis=0)) + dot(hi, b_lo)
    sub_of = spread[:, 0:128].astype(jnp.int32)
    back = []
    for j in range(3):
        r = slice(128 * j, 128 * j + 128)
        y = corr[r]
        for s in range(4):
            y = jnp.where(sub_of == s + 1, wide[r, 128 * s : 128 * s + 128], y)
        back.append(y)
    hi, lo = split2(jnp.concatenate(back, axis=1))
    index = 48 * orient + 8 * face + element
    row = lax.broadcasted_iota(jnp.int32, (384, SLOTS), 0)
    beta = jnp.where(sub == 0, 1.0, 0.25)
    hot = jnp.where(row == index, beta, 0.0).astype(bf16)
    summed = dot(jnp.concatenate([hot, hot], axis=1), jnp.concatenate([hi, lo], axis=0))
    rows = []
    for j in range(3):
        lanes = slice(128 * j, 128 * j + 128)
        rows.append(jnp.concatenate([summed[48 * o : 48 * o + 48, lanes] for o in range(8)], axis=1))
    hi, lo = split2(jnp.concatenate(rows, axis=0))
    turned = dot(jnp.concatenate([hi, lo], axis=0), orient_ref[...], 1, 1)
    total = turned[0:144] + turned[144:288] + local_ref[...]
    low = lane_low((8, 128))
    lift = []
    for v in range(6):
        at = 48 * (v // 2)
        parts = []
        for d in range(3):
            first = total[at + 16 * d : at + 16 * d + 8]
            second = total[at + 16 * d + 8 : at + 16 * d + 16]
            if v % 2 == 0:
                parts.append(jnp.where(low, first, swap(second)))
            else:
                parts.append(jnp.where(low, swap(first), second))
        lift.append(parts)
    side = jnp.concatenate(
        [jnp.concatenate([lift[v][1] for v in range(6)], axis=0), jnp.concatenate([lift[v][2] for v in range(6)], axis=0)],
        axis=1,
    )
    hi, lo = split2(side)
    placed = dot(jnp.concatenate([hi, lo], axis=0), sel_ref[...], 1, 1)
    placed = placed[0:48] + placed[48:96]
    scale = (STEP * LIFT) * by_element(metric_ref, (8, 128))
    for v in range(6):
        for t in range(4):
            lanes = slice(128 * t, 128 * t + 128)
            value = placed[8 * v : 8 * v + 8, lanes]
            if t == 0:
                value = value + jnp.where(low, lift[v][0], 0.0)
            if t == 3:
                value = value + jnp.where(low, 0.0, lift[v][0])
            out_ref[v, :, lanes] = base_ref[v, :, lanes] + scale * value


SM = pl.BlockSpec(memory_space=pltpu.SMEM)
VM = pl.BlockSpec(memory_space=pltpu.VMEM)


def call(kernel, outs, specs, name):
    return pl.pallas_call(
        kernel,
        out_shape=[jax.ShapeDtypeStruct(s, f32) for s in outs],
        in_specs=specs,
        out_specs=[VM] * len(outs),
        name=name,
    )


def shards(state, material, metric, mortar_proj, mortar_map, mortar_count, neighbours):
    groups = lax.axis_size("grp")
    n_elem = lax.axis_size("elem")
    elements = jnp.transpose(state, (1, 0, 2))
    info = mortar_map[0]
    counts = mortar_count[0]
    select = jnp.asarray(face_select(), bf16)
    orients = jnp.asarray(orient_table(), bf16)
    deriv = deriv_table()
    d_hi = deriv.astype(bf16)
    d_lo = (deriv - d_hi.astype(np.float32)).astype(bf16)
    derivs = jnp.asarray(np.concatenate([d_hi, d_lo], axis=1))
    codes_a = jnp.asarray(code_table([{0: 1, 1: 8, 3: 48}, {2: 1}, {4: 1}]), bf16)
    codes_c = jnp.asarray(code_table([{n: 1} for n in range(5)]), bf16)

    mine, faces = call(
        trace_kernel, [(SLOTS, 512), (144, 128)], [VM, SM, VM, VM, VM, VM, VM], "traces"
    )(elements, material, info, mortar_proj, select, orients, codes_a)
    split = groups * CAPG
    arrived = lax.all_to_all(
        mine[:split].reshape(groups, CAPG, 512), "grp", split_axis=0, concat_axis=0, tiled=True
    ).reshape(split, 512)
    up = [(i, i + 1) for i in range(n_elem - 1)]
    down = [(i + 1, i) for i in range(n_elem - 1)]
    from_above = lax.ppermute(mine[split + CAPS :], "elem", down)
    from_below = lax.ppermute(mine[split : split + CAPS], "elem", up)
    base, local = call(
        local_kernel, [(6, 8, 512), (144, 128)], [VM, SM, SM, VM, VM, VM], "local"
    )(elements, material, metric, neighbours, faces, derivs)
    (new,) = call(
        mortar_kernel,
        [(6, 8, 512)],
        [VM, VM, VM, VM, SM, SM, SM, VM, VM, VM, VM, VM, VM, VM],
        "mortar",
    )(
        mine, arrived, from_above, from_below, material, metric, counts, info, mortar_proj,
        select, orients, codes_c, base, local,
    )
    return jnp.transpose(new, (1, 0, 2))


def solution(mesh):
    return jax.shard_map(
        shards,
        mesh=mesh,
        in_specs=(
            P(("elem", "grp"), None, None),
            P(("elem", "grp")),
            P(("elem", "grp")),
            P(),
            P(("elem", "grp"), None, None),
            P(("elem", "grp"), None),
            P(("elem", "grp"), None),
        ),
        out_specs=P(("elem", "grp"), None, None),
        check_vma=False,
    )
```

time: 135 us -> 33.3 us (0.25)
  matrix products: 44.4 us -> 0 us
  other arithmetic: 35.5 us -> 0 us
  local copies, waits for them, and re-layouts: 28.5 us -> 2.32 us
  Pallas kernels: 0 us -> 8.89 us
  starting transfers between devices: 23.2 us -> 20 us
    dot_general x8 -> x0, matrix products: 44.4 us -> none  [the longest x1 21 us: volume_term(): jnp.einsum('kc,evabc->evabk', deriv, fluxes[2], precision=highest)]
    sub x4 -> x0, other arithmetic: 12.9 us -> none  [state_parts(): heat_ratio[:, None] - 1.0]
    pallas_call x0 -> x3, Pallas kernels: none -> 8.89 us  [the longest x1 3.64 us: shards(): call(mortar_kernel, [(6, 8, 512)], [VM, VM, VM, VM, SM, SM, SM, VM, VM, V...]
    concatenate x21 -> x0, local copies, waits for them, and re-layouts: 8.57 us -> none  [the longest x20 8.49 us: state_parts(): jnp.concatenate([(density * speed_n)[:, None], momentum * speed_n[:, None...]
    ppermute x3 -> x2, starting transfers between devices: 7.89 us -> 2.59 us  [the longest x1 1.29 us: shards(): from_below = lax.ppermute(mine[split:split + CAPS], 'elem', up)]
    select_n x14 -> x0, other arithmetic: 5.27 us -> none  [the longest x1 1.39 us: mortar_traces(): picked = face_rows[mortar_info[0] * 6 + mortar_info[1]]]
    scatter-add x1 -> x0, other arithmetic: 4.97 us -> none  [section_update(): jax.ops.segment_sum(projected, mortar_info[0] * 6 + mortar_info[1], num_s...]
    gather x4 -> x0, local copies, waits for them, and re-layouts: 4.85 us -> none  [the longest x1 2.79 us: slot_operators(): return combos[mortar_info[2] * 8 + mortar_info[3]]]
  transfers between devices with their start and end apart: 4 -> 3, of which waited for: 1 -> 1; matrix products, arithmetic and copies ran while one was open for 62% -> 0% of each run, Pallas kernels for 0% -> 7%
where the time goes in v1:
time: 33.3 us; the launch traced here: 33 us
  starting transfers between devices  20 us (60%)
  Pallas kernels  8.89 us (27%)
  local copies, waits for them, and re-layouts  2.32 us (7%)
  waiting for transfers between devices  1.8 us (5%)
    all_to_all x1, starting transfers between devices, shards(): lax.all_to_all(mine[:split].reshape(groups, CAPG, 512), 'grp', split_axis...  17.4 us
    pallas_call x1, Pallas kernels, shards(): call(mortar_kernel, [(6, 8, 512)], [VM, VM, VM, VM, SM, SM, SM, VM, VM, V...  3.64 us
    pallas_call x1, Pallas kernels, shards(): call(trace_kernel, [(SLOTS, 512), (144, 128)], [VM, SM, VM, VM, VM, VM, V...  2.93 us
    pallas_call x1, Pallas kernels, shards(): call(local_kernel, [(6, 8, 512), (144, 128)], [VM, SM, SM, VM, VM, VM], '...  2.32 us
    ppermute x1, waiting for transfers between devices, shards(): from_above = lax.ppermute(mine[split + CAPS:], 'elem', down)  1.8 us
    reshape x1, local copies, waits for them, and re-layouts, shards(): mine[:split].reshape(groups, CAPG, 512)  1.64 us
    ppermute x1, starting transfers between devices, shards(): from_below = lax.ppermute(mine[split:split + CAPS], 'elem', up)  1.29 us
    ppermute x1, starting transfers between devices, shards(): from_above = lax.ppermute(mine[split + CAPS:], 'elem', down)  1.29 us
  transfers between devices with their start and end apart: 3, of which 1 were waited for; matrix products, arithmetic and copies ran while one was open for 0% of the time, Pallas kernels for 7%

profile of v1, /device:TPU:1, one launch (start us, length us, event | category | flops | bytes accessed | tf_op | source)
XLA Modules:
  0.0 33.0 jit_solution(10116386241956335657)
XLA Ops:
  0.0 2.9 %traces.1 = (f32[128,512]{1,0:T(8,128)}, f32[144,128]{1,0:T(8,128)}) custom-call(f32[6,8,512]{2,1,0:T(8,128)} %bitcast.8, s32[8]{0:T(128)} %mat_ref.5, s32[4,128]{1,0:T(4,128)} %bitcast.10, f32[4,64,64]{2,1,0:T(8,128)} %proj_ref.3, bf16[512,256]{1,0:T(8,128)(2,1)} %constant.10.clone.sel_ref, bf16[128,1024]{1,0:T(8,128)(2,1)} %constant.11.clone.orient_ref, ...), custom_call_target="tpu_custom_call" | custom-call | tf_op jit(solution)/shard_map/traces/pallas_call | solution.py:427
  2.9 0.0 copy-start
  2.9 1.6 %slice_bitcast_fusion = f32[8,8,512]{2,1,0:T(8,128)} fusion(f32[128,512]{1,0:T(8,128)} %get-tuple-element.9.mine_ref), kind=kLoop, calls=%fused_computation | loop fusion | bytes 262144 | tf_op jit(solution)/shard_map/reshape | solution.py:432
  4.6 17.4 %all-to-all-start = ((f32[8,8,512]{2,1,0:T(8,128)}), f32[8,8,512]{2,1,0:T(8,128)S(1)}, u32[]{:S(2)}, u32[]{:S(2)}) async-start(f32[8,8,512]{2,1,0:T(8,128)} %slice_bitcast_fusion), calls=%async_computation | async-start | bytes 262144 | tf_op jit(solution)/shard_map/all_to_all | solution.py:431
  22.0 0.0 copy-done
  22.0 1.3 %collective-permute-start.1 = (f32[32,512]{1,0:T(8,128)S(1)}, f32[32,512]{1,0:T(8,128)S(1)}, u32[]{:S(2)}, u32[]{:S(2)}) collective-permute-start(f32[32,512]{1,0:T(8,128)S(1)} %get-tuple-element.13), channel_id=1, source_target_pairs={{0,8},{8,16},{16,24},{24,32},{32,40},{40,48},{48,56},{56,64},{64,7... | collective-permute-start | bytes 196616 | tf_op jit(solution)/shard_map/ppermute | solution.py:437
  23.3 1.3 %collective-permute-start = (f32[32,512]{1,0:T(8,128)S(1)}, f32[32,512]{1,0:T(8,128)S(1)}, u32[]{:S(2)}, u32[]{:S(2)}) collective-permute-start(f32[32,512]{1,0:T(8,128)S(1)} %get-tuple-element.14), channel_id=1, source_target_pairs={{8,0},{16,8},{24,16},{32,24},{40,32},{48,40},{56,48},{64,56},{72,6... | collective-permute-start | bytes 196616 | tf_op jit(solution)/shard_map/ppermute | solution.py:436
  24.6 2.3 %local.1 = (f32[6,8,512]{2,1,0:T(8,128)}, f32[144,128]{1,0:T(8,128)}) custom-call(f32[6,8,512]{2,1,0:T(8,128)} %bitcast.9, s32[8]{0:T(128)} %mat_ref.5, f32[8]{0:T(128)} %metric_ref.3, s32[8,6]{1,0:T(8,128)} %near_ref.1, f32[144,128]{1,0:T(8,128)} %get-tuple-element.10.face_ref, bf16[256,256]{1,0:T(8,128)(2,1)} %constant.12.clone.deriv_ref), custom_call_target="tpu_custom_call" | custom-call | tf_op jit(solution)/shard_map/local/pallas_call | solution.py:438
  26.9 0.0 collective-permute-done.1.below_ref
  26.9 0.0 copy-start.2
  26.9 1.8 %collective-permute-done.above_ref = f32[32,512]{1,0:T(8,128)S(1)} collective-permute-done((f32[32,512]{1,0:T(8,128)S(1)}, f32[32,512]{1,0:T(8,128)S(1)}, u32[]{:S(2)}, u32[]{:S(2)}) %collective-permute-start) | collective-permute-done | bytes 65568 | tf_op jit(solution)/shard_map/ppermute | solution.py:436
  28.7 0.0 copy-start.3
  28.7 0.0 all-to-all-done
  28.7 0.0 copy-start.1
  28.7 0.0 copy-done.2
  28.7 0.6 %copy-done.3 = f32[32,512]{1,0:T(8,128)} copy-done((f32[32,512]{1,0:T(8,128)}, f32[32,512]{1,0:T(8,128)S(1)}, u32[]{:S(2)}) %copy-start.3) | copy-done | bytes 65560
  29.3 0.1 copy-done.1
  29.4 3.6 %mortar.1 = f32[6,8,512]{2,1,0:T(8,128)} custom-call(f32[128,512]{1,0:T(8,128)} %get-tuple-element.9.mine_ref, f32[64,512]{1,0:T(8,128)} %bitcast.7, f32[32,512]{1,0:T(8,128)} %copy-done.3, f32[32,512]{1,0:T(8,128)} %copy-done.2, s32[8]{0:T(128)} %mat_ref.5, f32[8]{0:T(128)} %metric_ref.3, s32[10]{0:T(128)} %bitcast.12, s32[4,128]{1,0:T(4,128)} %bitcast.11, ...), custom_call_target="tpu_custom_call" | custom-call | tf_op jit(solution)/shard_map/mortar/pallas_call | solution.py:441
  (1 shorter events, 0.0 us)
Async XLA Ops:
  2.9 19.0 %copy-start = (f32[128,512]{1,0:T(8,128)S(1)}, f32[128,512]{1,0:T(8,128)}, u32[]{:S(2)}) copy-start(f32[128,512]{1,0:T(8,128)} %get-tuple-element.9.mine_ref) | copy-start | bytes 786436
  4.6 24.1 %all-to-all-start = ((f32[8,8,512]{2,1,0:T(8,128)}), f32[8,8,512]{2,1,0:T(8,128)S(1)}, u32[]{:S(2)}, u32[]{:S(2)}) async-start(f32[8,8,512]{2,1,0:T(8,128)} %slice_bitcast_fusion), calls=%async_computation | async-start | bytes 262144 | tf_op jit(solution)/shard_map/all_to_all | solution.py:431
  22.0 4.9 %collective-permute-start.1 = (f32[32,512]{1,0:T(8,128)S(1)}, f32[32,512]{1,0:T(8,128)S(1)}, u32[]{:S(2)}, u32[]{:S(2)}) collective-permute-start(f32[32,512]{1,0:T(8,128)S(1)} %get-tuple-element.13), channel_id=1, source_target_pairs={{0,8},{8,16},{16,24},{24,32},{32,40},{40,48},{48,56},{56,64},{64,7... | collective-permute-start | bytes 196616 | tf_op jit(solution)/shard_map/ppermute | solution.py:437
  23.3 5.4 %collective-permute-start = (f32[32,512]{1,0:T(8,128)S(1)}, f32[32,512]{1,0:T(8,128)S(1)}, u32[]{:S(2)}, u32[]{:S(2)}) collective-permute-start(f32[32,512]{1,0:T(8,128)S(1)} %get-tuple-element.14), channel_id=1, source_target_pairs={{8,0},{16,8},{24,16},{32,24},{40,32},{48,40},{56,48},{64,56},{72,6... | collective-permute-start | bytes 196616 | tf_op jit(solution)/shard_map/ppermute | solution.py:436
  26.9 1.8 %copy-start.2 = (f32[32,512]{1,0:T(8,128)}, f32[32,512]{1,0:T(8,128)S(1)}, u32[]{:S(2)}) copy-start(f32[32,512]{1,0:T(8,128)S(1)} %collective-permute-done.1.below_ref) | copy-start | bytes 196612
  28.7 0.6 %copy-start.3 = (f32[32,512]{1,0:T(8,128)}, f32[32,512]{1,0:T(8,128)S(1)}, u32[]{:S(2)}) copy-start(f32[32,512]{1,0:T(8,128)S(1)} %collective-permute-done.above_ref) | copy-start | bytes 196612
  28.7 0.7 %copy-start.1 = (f32[8,8,512]{2,1,0:T(8,128)}, f32[8,8,512]{2,1,0:T(8,128)S(1)}, u32[]{:S(2)}) copy-start(f32[8,8,512]{2,1,0:T(8,128)S(1)} %all-to-all-done) | copy-start | bytes 393220

commit v2 on v1

--- a/solution.py
+++ b/solution.py
@@ -7,6 +7,7 @@
 from jax.experimental import pallas as pl
 from jax.experimental.pallas import tpu as pltpu
 from jax.sharding import PartitionSpec as P
+
 
 CAPG = 8
 CAPS = 32
@@ -123,7 +124,9 @@
     return jnp.concatenate(rows + pad, axis=0).astype(bf16)
 
 
-def trace_kernel(state_ref, mat_ref, map_ref, proj_ref, sel_ref, orient_ref, code_ref, out_ref, face_ref):
+def trace_kernel(
+    state_ref, mat_ref, map_ref, proj_ref, sel_ref, orient_ref, code_ref, grp_ref, up_ref, down_ref, face_ref, mine_ref, info_ref,
+):
     low = lane_low((8, 128))
     flat = state_ref[...].reshape(48, 512)
     picked = dot(jnp.concatenate(split3(flat), axis=0), sel_ref[...])
@@ -149,6 +152,7 @@
     hi, lo = split2(faces)
     table = dot(jnp.concatenate([hi, lo], axis=0), orient_ref[...]).astype(bf16)
     info = map_ref[...]
+    info_ref[...] = jnp.concatenate([info, info], axis=0)
     element, face, sub, orient = (info[i : i + 1] for i in range(4))
     material = slot_material(mat_ref, element)
     codes = code_rows([element.astype(f32), face.astype(f32), sub.astype(f32), orient.astype(f32), material])
@@ -171,13 +175,22 @@
     wide = dot(
         jnp.concatenate([h, x_lo.astype(bf16)], axis=1), jnp.concatenate([b_hi, b_hi], axis=1), 1, 1
     ) + dot(h, b_lo, 1, 1)
+
+    def put(at, value):
+        lanes = slice(at, at + 128)
+        for g in range(8):
+            grp_ref[g, :, lanes] = value[8 * g : 8 * g + 8]
+            mine_ref[g, :, lanes] = value[8 * g : 8 * g + 8]
+        up_ref[:, lanes] = value[64:96]
+        down_ref[:, lanes] = value[96:128]
+
     for j in range(3):
         r = slice(128 * j, 128 * j + 128)
         w = x_hi[r] + x_lo[r]
         for s in range(4):
             w = jnp.where(sub_of == s + 1, wide[r, 128 * s : 128 * s + 128], w)
-        out_ref[:, 128 * j : 128 * j + 128] = w
-    out_ref[:, 384:512] = 1.4 + 0.27 * spread[:, 256:384]
+        put(128 * j, w)
+    put(384, 1.4 + 0.27 * spread[:, 256:384])
 
 
 def hllc_correction(u, g, normal, own):
@@ -225,7 +238,37 @@
     return jnp.where(own, mine, swap(theirs)), jnp.where(own, swap(mine), theirs)
 
 
-def local_kernel(state_ref, mat_ref, metric_ref, near_ref, face_ref, deriv_ref, base_ref, local_ref):
+def local_kernel(
+    state_ref, mat_ref, metric_ref, count_ref, near_ref, face_ref, deriv_ref, info_ref, proj_ref, code_ref,
+    base_ref, local_ref, spread_ref, hot_ref, back_ref,
+):
+    info = info_ref[...]
+    element, face, sub, orient = (info[i : i + 1] for i in range(4))
+    slot = lax.broadcasted_iota(jnp.int32, (1, SLOTS), 1)
+    group = jnp.where(
+        slot < 64, lax.shift_right_logical(slot, 3), 6 + lax.shift_right_logical(slot, 5)
+    )
+    position = jnp.where(slot < 64, jnp.bitwise_and(slot, 7), jnp.bitwise_and(slot, 31))
+    limit = jnp.zeros((1, SLOTS), jnp.int32)
+    for n in range(10):
+        limit = jnp.where(group == n, count_ref[n], limit)
+    alive = jnp.where(position < limit, 1.0, 0.0)
+    sign = jnp.where(jnp.bitwise_and(face, 1) == 1, 1.0, -1.0)
+    axis = lax.shift_right_logical(face, 1)
+    codes = code_rows(
+        [sub.astype(f32), alive] + [jnp.where(axis == d, sign, 0.0) for d in range(3)]
+    )
+    spread_ref[...] = dot(codes, code_ref[...], 0, 0)
+    index = 48 * orient + 8 * face + element
+    row = lax.broadcasted_iota(jnp.int32, (384, SLOTS), 0)
+    beta = jnp.where(sub == 0, 1.0, 0.25)
+    hot = jnp.where(row == index, beta, 0.0).astype(bf16)
+    hot_ref[:, 0:128] = hot
+    hot_ref[:, 128:256] = hot
+    b_hi, b_lo = split2(jnp.concatenate(project_blocks(proj_ref), axis=1))
+    back_ref[0:128, :] = b_hi
+    back_ref[128:256, :] = b_hi
+    back_ref[256:384, :] = b_lo
     heat = 1.4 + 0.27 * by_element(mat_ref, (8, 512))
     u = [state_ref[v] for v in range(6)]
     inv = 1.0 / u[0]
@@ -296,53 +339,36 @@
 
 
 def mortar_kernel(
-    mine_ref, grp_ref, above_ref, below_ref, mat_ref, metric_ref, count_ref, map_ref, proj_ref,
-    sel_ref, orient_ref, code_ref, base_ref, local_ref, out_ref,
+    grp_ref, up_ref, down_ref, from_grp_ref, above_ref, below_ref, metric_ref,
+    sel_ref, orient_ref, base_ref, local_ref, spread_ref, hot_ref, back_ref, out_ref,
 ):
-    info = map_ref[...]
-    element, face, sub, orient = (info[i : i + 1] for i in range(4))
-    slot = lax.broadcasted_iota(jnp.int32, (1, SLOTS), 1)
-    group = jnp.where(
-        slot < 64, lax.shift_right_logical(slot, 3), 6 + lax.shift_right_logical(slot, 5)
-    )
-    position = jnp.where(slot < 64, jnp.bitwise_and(slot, 7), jnp.bitwise_and(slot, 31))
-    limit = jnp.zeros((1, SLOTS), jnp.int32)
-    for n in range(10):
-        limit = jnp.where(group == n, count_ref[n], limit)
-    alive = jnp.where(position < limit, 1.0, 0.0)
-    sign = jnp.where(jnp.bitwise_and(face, 1) == 1, 1.0, -1.0)
-    axis = lax.shift_right_logical(face, 1)
-    codes = code_rows(
-        [sub.astype(f32), alive] + [jnp.where(axis == d, sign, 0.0) for d in range(3)]
-    )
-    spread = dot(codes, code_ref[...], 0, 0)
     chunk = 32
     own = lane_low((chunk, 128))
     packed = [[], [], []]
     for start in range(0, SLOTS, chunk):
         r = slice(start, start + chunk)
-        if start < 64:
-            theirs_ref, at = grp_ref, start
-        elif start < 96:
-            theirs_ref, at = above_ref, start - 64
-        else:
-            theirs_ref, at = below_ref, start - 96
-        q = slice(at, at + chunk)
+
+        def rows(grp, up, down, at):
+            lanes = slice(at, at + 128)
+            if start < 64:
+                return jnp.concatenate([grp[start // 8 + n, :, lanes] for n in range(chunk // 8)], axis=0)
+            return (up if start < 96 else down)[:, lanes]
+
+        mine = functools.partial(rows, grp_ref, up_ref, down_ref)
+        theirs = functools.partial(rows, from_grp_ref, above_ref, below_ref)
         states = []
         for j in range(3):
-            lanes = slice(128 * j, 128 * j + 128)
-            states += paired(own, mine_ref[r, lanes], theirs_ref[q, lanes])
-        g = jnp.where(own, mine_ref[r, 384:512], theirs_ref[q, 384:512])
-        live = spread[r, 128:256] > 0.5
-        normal = [spread[r, 256 + 128 * d : 384 + 128 * d] for d in range(3)]
+            states += paired(own, mine(128 * j), theirs(128 * j))
+        g = jnp.where(own, mine(384), theirs(384))
+        live = spread_ref[r, 128:256] > 0.5
+        normal = [spread_ref[r, 256 + 128 * d : 384 + 128 * d] for d in range(3)]
         corr = hllc_correction(states, g, normal, own)
         for j in range(3):
             packed[j].append(jnp.where(live, join_pair(own, corr[2 * j], corr[2 * j + 1]), 0.0))
     corr = jnp.concatenate(packed[0] + packed[1] + packed[2], axis=0)
-    b_hi, b_lo = split2(jnp.concatenate(project_blocks(proj_ref), axis=1))
     hi, lo = split2(corr)
-    wide = dot(jnp.concatenate([hi, lo], axis=1), jnp.concatenate([b_hi, b_hi], axis=0)) + dot(hi, b_lo)
-    sub_of = spread[:, 0:128].astype(jnp.int32)
+    wide = dot(jnp.concatenate([hi, lo, hi], axis=1), back_ref[...])
+    sub_of = spread_ref[:, 0:128].astype(jnp.int32)
     back = []
     for j in range(3):
         r = slice(128 * j, 128 * j + 128)
@@ -351,11 +377,7 @@
             y = jnp.where(sub_of == s + 1, wide[r, 128 * s : 128 * s + 128], y)
         back.append(y)
     hi, lo = split2(jnp.concatenate(back, axis=1))
-    index = 48 * orient + 8 * face + element
-    row = lax.broadcasted_iota(jnp.int32, (384, SLOTS), 0)
-    beta = jnp.where(sub == 0, 1.0, 0.25)
-    hot = jnp.where(row == index, beta, 0.0).astype(bf16)
-    summed = dot(jnp.concatenate([hot, hot], axis=1), jnp.concatenate([hi, lo], axis=0))
+    summed = dot(hot_ref[...], jnp.concatenate([hi, lo], axis=0))
     rows = []
     for j in range(3):
         lanes = slice(128 * j, 128 * j + 128)
@@ -399,17 +421,21 @@
 VM = pl.BlockSpec(memory_space=pltpu.VMEM)
 
 
-def call(kernel, outs, specs, name):
+def call(kernel, outs, scalars, args, first=False, free=()):
+    outs = [s if isinstance(s[0], tuple) else (s, f32) for s in outs]
+    held = [
+        a if first or n in scalars else pltpu.with_memory_space_constraint(a, pltpu.VMEM)
+        for n, a in enumerate(args)
+    ]
     return pl.pallas_call(
         kernel,
-        out_shape=[jax.ShapeDtypeStruct(s, f32) for s in outs],
-        in_specs=specs,
+        out_shape=[jax.ShapeDtypeStruct(*s) if n in free else pltpu.VMEM(*s) for n, s in enumerate(outs)],
+        in_specs=[SM if n in scalars else VM for n in range(len(args))],
         out_specs=[VM] * len(outs),
-        name=name,
-    )
-
-
-def shards(state, material, metric, mortar_proj, mortar_map, mortar_count, neighbours):
+    )(*held)
+
+
+def section(state, material, metric, mortar_proj, mortar_map, mortar_count, neighbours):
     groups = lax.axis_size("grp")
     n_elem = lax.axis_size("elem")
     elements = jnp.transpose(state, (1, 0, 2))
@@ -424,35 +450,36 @@
     codes_a = jnp.asarray(code_table([{0: 1, 1: 8, 3: 48}, {2: 1}, {4: 1}]), bf16)
     codes_c = jnp.asarray(code_table([{n: 1} for n in range(5)]), bf16)
 
-    mine, faces = call(
-        trace_kernel, [(SLOTS, 512), (144, 128)], [VM, SM, VM, VM, VM, VM, VM], "traces"
-    )(elements, material, info, mortar_proj, select, orients, codes_a)
-    split = groups * CAPG
-    arrived = lax.all_to_all(
-        mine[:split].reshape(groups, CAPG, 512), "grp", split_axis=0, concat_axis=0, tiled=True
-    ).reshape(split, 512)
-    up = [(i, i + 1) for i in range(n_elem - 1)]
-    down = [(i + 1, i) for i in range(n_elem - 1)]
-    from_above = lax.ppermute(mine[split + CAPS :], "elem", down)
-    from_below = lax.ppermute(mine[split : split + CAPS], "elem", up)
-    base, local = call(
-        local_kernel, [(6, 8, 512), (144, 128)], [VM, SM, SM, VM, VM, VM], "local"
-    )(elements, material, metric, neighbours, faces, derivs)
+    grp, up, down, faces, mine, kept = call(
+        trace_kernel,
+        [(groups, CAPG, 512), (CAPS, 512), (CAPS, 512), (144, 128), (groups, CAPG, 512), ((8, SLOTS), jnp.int32)],
+        {1},
+        (elements, material, info, mortar_proj, select, orients, codes_a),
+        first=True,
+        free=(0,),
+    )
+    above = lax.ppermute(down, "elem", [(i + 1, i) for i in range(n_elem - 1)])
+    below = lax.ppermute(up, "elem", [(i, i + 1) for i in range(n_elem - 1)])
+    held = call(
+        local_kernel,
+        [(6, 8, 512), (144, 128), (SLOTS, 640), ((384, 256), bf16), ((384, 512), bf16)],
+        {1, 2, 3},
+        (elements, material, metric, counts, neighbours, faces, derivs, kept, mortar_proj, codes_c),
+    )
+    arrived = lax.all_to_all(grp, "grp", split_axis=0, concat_axis=0, tiled=True)
     (new,) = call(
         mortar_kernel,
         [(6, 8, 512)],
-        [VM, VM, VM, VM, SM, SM, SM, VM, VM, VM, VM, VM, VM, VM],
-        "mortar",
-    )(
-        mine, arrived, from_above, from_below, material, metric, counts, info, mortar_proj,
-        select, orients, codes_c, base, local,
+        {6},
+        (mine, up, down, arrived, above, below, metric, select, orients, *held),
+        free=(0,),
     )
     return jnp.transpose(new, (1, 0, 2))
 
 
 def solution(mesh):
     return jax.shard_map(
-        shards,
+        section,
         mesh=mesh,
         in_specs=(
             P(("elem", "grp"), None, None),

time: 33.3 us -> 30.4 us (0.913)
  local copies, waits for them, and re-layouts: 2.32 us -> 0.03 us
  Pallas kernels: 8.89 us -> 7.24 us
  waiting for transfers between devices: 1.8 us -> 2.57 us
    pallas_call x3, Pallas kernels: 8.89 us -> 7.24 us  [call(): pl.pallas_call(kernel, out_shape=[jax.ShapeDtypeStruct(*s) if n in free e...]
    reshape x1 -> x0, local copies, waits for them, and re-layouts: 1.64 us -> none  [shards(): mine[:split].reshape(groups, CAPG, 512)]
    ppermute x2, waiting for transfers between devices: 1.8 us -> 2.57 us  [the longest x1 2.57 us: section(): above = lax.ppermute(down, 'elem', [(i + 1, i) for i in range(n_elem - 1)])]
    unnamed x8 -> x14, local copies, waits for them, and re-layouts: 0.67 us -> 0.03 us
  transfers between devices with their start and end apart: 3 -> 3, of which waited for: 1 -> 1; matrix products, arithmetic and copies ran while one was open for 0% -> 0% of each run, Pallas kernels for 7% -> 5%
where the time goes in v2:
time: 30.4 us; the launch traced here: 30.1 us
  starting transfers between devices  20.2 us (66%)
  Pallas kernels  7.24 us (24%)
  waiting for transfers between devices  2.57 us (8%)
    all_to_all x1, starting transfers between devices, section(): lax.all_to_all(grp, 'grp', split_axis=0, concat_axis=0, tiled=True)  17.5 us
    pallas_call x3, Pallas kernels, call(): pl.pallas_call(kernel, out_shape=[jax.ShapeDtypeStruct(*s) if n in free e...  7.24 us
    ppermute x1, waiting for transfers between devices, section(): above = lax.ppermute(down, 'elem', [(i + 1, i) for i in range(n_elem - 1)])  2.57 us
    ppermute x1, starting transfers between devices, section(): below = lax.ppermute(up, 'elem', [(i, i + 1) for i in range(n_elem - 1)])  1.41 us
    ppermute x1, starting transfers between devices, section(): above = lax.ppermute(down, 'elem', [(i + 1, i) for i in range(n_elem - 1)])  1.29 us
  transfers between devices with their start and end apart: 3, of which 1 were waited for; matrix products, arithmetic and copies ran while one was open for 0% of the time, Pallas kernels for 5%

profile of v2, /device:TPU:1, one launch (start us, length us, event | category | flops | bytes accessed | tf_op | source)
XLA Modules:
  0.0 30.1 jit_solution(12395016318770872301)
XLA Ops:
  0.0 0.0 copy-start.2
  0.0 0.0 copy-start.3
  0.0 0.0 copy-start.4
  0.0 2.9 %shard_map.118 = (f32[8,8,512]{2,1,0:T(8,128)}, f32[32,512]{1,0:T(8,128)S(1)}, f32[32,512]{1,0:T(8,128)S(1)}, f32[144,128]{1,0:T(8,128)S(1)}, f32[8,8,512]{2,1,0:T(8,128)S(1)}, /*index=5*/s32[8,128]{1,0:T(8,128)S(1)}) custom-call(f32[6,8,512]{2,1,0:T(8,128)} %bitcast.4, s32[8]{0:T(128)} %mat_ref.3, s32[4,128]{1,0:T(4,128)} %bitcast.6, ...), custom_call_target="tpu_custom_call" | custom-call | tf_op jit(solution)/shard_map/pallas_call | solution.py:430
  2.9 0.0 copy-start.5
  2.9 0.0 copy-start.6
  2.9 0.0 copy-start.1
  2.9 17.5 %all-to-all-start = ((f32[8,8,512]{2,1,0:T(8,128)}), f32[8,8,512]{2,1,0:T(8,128)S(1)}, u32[]{:S(2)}, u32[]{:S(2)}) async-start(f32[8,8,512]{2,1,0:T(8,128)} %get-tuple-element.19), calls=%async_computation | async-start | bytes 262144 | tf_op jit(solution)/shard_map/all_to_all | solution.py:469
  20.4 0.0 copy-start
  20.4 1.4 %collective-permute-start.1 = (f32[32,512]{1,0:T(8,128)S(1)}, f32[32,512]{1,0:T(8,128)S(1)}, u32[]{:S(2)}, u32[]{:S(2)}) collective-permute-start(f32[32,512]{1,0:T(8,128)S(1)} %get-tuple-element.17.up_ref), channel_id=1, source_target_pairs={{0,8},{8,16},{16,24},{24,32},{32,40},{40,48},{48,56},{56,64},{64,7... | collective-permute-start | bytes 196616 | tf_op jit(solution)/shard_map/ppermute | solution.py:462
  21.9 1.3 %collective-permute-start = (f32[32,512]{1,0:T(8,128)S(1)}, f32[32,512]{1,0:T(8,128)S(1)}, u32[]{:S(2)}, u32[]{:S(2)}) collective-permute-start(f32[32,512]{1,0:T(8,128)S(1)} %get-tuple-element.18.down_ref), channel_id=1, source_target_pairs={{8,0},{16,8},{24,16},{32,24},{40,32},{48,40},{56,48},{64,56},{72,6... | collective-permute-start | bytes 196616 | tf_op jit(solution)/shard_map/ppermute | solution.py:461
  23.2 0.0 copy-done.2
  23.2 0.0 copy-done.3
  23.2 0.0 copy-done.4
  23.2 0.0 copy-done.5
  23.2 0.0 copy-done.6
  23.2 1.5 %shard_map.119 = (f32[6,8,512]{2,1,0:T(8,128)S(1)}, f32[144,128]{1,0:T(8,128)S(1)}, f32[128,640]{1,0:T(8,128)S(1)}, bf16[384,256]{1,0:T(8,128)(2,1)S(1)}, bf16[384,512]{1,0:T(8,128)(2,1)S(1)}) custom-call(f32[6,8,512]{2,1,0:T(8,128)S(1)} %bitcast.5, s32[8]{0:T(128)} %mat_ref.3, f32[8]{0:T(128)} %metric_ref.3, s32[10]{0:T(128)} %bitcast.7, ...), custom_call_target="tpu_custom_call" | custom-call | tf_op jit(solution)/shard_map/pallas_call | solution.py:430
  24.7 0.0 collective-permute-done.1.below_ref
  24.7 2.6 %collective-permute-done.above_ref = f32[32,512]{1,0:T(8,128)S(1)} collective-permute-done((f32[32,512]{1,0:T(8,128)S(1)}, f32[32,512]{1,0:T(8,128)S(1)}, u32[]{:S(2)}, u32[]{:S(2)}) %collective-permute-start) | collective-permute-done | bytes 65568 | tf_op jit(solution)/shard_map/ppermute | solution.py:461
  27.3 0.0 all-to-all-done.from_grp_ref
  27.3 0.0 copy-done.1
  27.3 0.0 copy-done
  27.3 2.9 %shard_map.120 = f32[6,8,512]{2,1,0:T(8,128)} custom-call(f32[8,8,512]{2,1,0:T(8,128)S(1)} %get-tuple-element.16.grp_ref, f32[32,512]{1,0:T(8,128)S(1)} %get-tuple-element.17.up_ref, f32[32,512]{1,0:T(8,128)S(1)} %get-tuple-element.18.down_ref, f32[8,8,512]{2,1,0:T(8,128)S(1)} %all-to-all-done.from_grp_ref, f32[32,512]{1,0:T(8,128)S(1)} %collective-permute-done.above_ref, ...), custom_call_target="tpu_custom_call" | custom-call | tf_op jit(solution)/shard_map/pallas_call | solution.py:430
Async XLA Ops:
  0.0 23.2 %copy-start.2 = (f32[4,64,64]{2,1,0:T(8,128)S(1)}, f32[4,64,64]{2,1,0:T(8,128)}, u32[]{:S(2)}) copy-start(f32[4,64,64]{2,1,0:T(8,128)} %proj_ref.3) | copy-start | bytes 196612
  0.0 23.2 %copy-start.3 = (f32[8,6,512]{2,0,1:T(8,128)S(1)}, f32[8,6,512]{2,0,1:T(8,128)}, u32[]{:S(2)}) copy-start(f32[8,6,512]{2,0,1:T(8,128)} %param.12) | copy-start | bytes 294916
  0.0 23.2 %copy-start.4 = (bf16[256,256]{1,0:T(8,128)(2,1)S(1)}, bf16[256,256]{1,0:T(8,128)(2,1)}, u32[]{:S(2)}) copy-start(bf16[256,256]{1,0:T(8,128)(2,1)} %constant.12.clone.deriv_ref) | copy-start | bytes 393220
  2.9 20.3 %copy-start.5 = (bf16[16,640]{1,0:T(8,128)(2,1)S(1)}, bf16[16,640]{1,0:T(8,128)(2,1)}, u32[]{:S(2)}) copy-start(bf16[16,640]{1,0:T(8,128)(2,1)} %constant.14.clone.code_ref) | copy-start | bytes 61444
  2.9 20.3 %copy-start.6 = (s32[8,6]{1,0:T(8,128)S(1)}, s32[8,6]{1,0:T(8,128)}, u32[]{:S(2)}) copy-start(s32[8,6]{1,0:T(8,128)} %near_ref.1) | copy-start | bytes 580
  2.9 24.4 %copy-start.1 = (bf16[512,256]{1,0:T(8,128)(2,1)S(1)}, bf16[512,256]{1,0:T(8,128)(2,1)}, u32[]{:S(2)}) copy-start(bf16[512,256]{1,0:T(8,128)(2,1)} %constant.10.clone.sel_ref) | copy-start | bytes 786436
  2.9 24.4 %all-to-all-start = ((f32[8,8,512]{2,1,0:T(8,128)}), f32[8,8,512]{2,1,0:T(8,128)S(1)}, u32[]{:S(2)}, u32[]{:S(2)}) async-start(f32[8,8,512]{2,1,0:T(8,128)} %get-tuple-element.19), calls=%async_computation | async-start | bytes 262144 | tf_op jit(solution)/shard_map/all_to_all | solution.py:469
  20.4 6.8 %copy-start = (bf16[128,1024]{1,0:T(8,128)(2,1)S(1)}, bf16[128,1024]{1,0:T(8,128)(2,1)}, u32[]{:S(2)}) copy-start(bf16[128,1024]{1,0:T(8,128)(2,1)} %constant.11.clone.orient_ref) | copy-start | bytes 786436
  20.4 4.3 %collective-permute-start.1 = (f32[32,512]{1,0:T(8,128)S(1)}, f32[32,512]{1,0:T(8,128)S(1)}, u32[]{:S(2)}, u32[]{:S(2)}) collective-permute-start(f32[32,512]{1,0:T(8,128)S(1)} %get-tuple-element.17.up_ref), channel_id=1, source_target_pairs={{0,8},{8,16},{16,24},{24,32},{32,40},{40,48},{48,56},{56,64},{64,7... | collective-permute-start | bytes 196616 | tf_op jit(solution)/shard_map/ppermute | solution.py:462
  21.9 5.4 %collective-permute-start = (f32[32,512]{1,0:T(8,128)S(1)}, f32[32,512]{1,0:T(8,128)S(1)}, u32[]{:S(2)}, u32[]{:S(2)}) collective-permute-start(f32[32,512]{1,0:T(8,128)S(1)} %get-tuple-element.18.down_ref), channel_id=1, source_target_pairs={{8,0},{16,8},{24,16},{32,24},{40,32},{48,40},{56,48},{64,56},{72,6... | collective-permute-start | bytes 196616 | tf_op jit(solution)/shard_map/ppermute | solution.py:461

commit v3 on v2

--- a/solution.py
+++ b/solution.py
@@ -125,7 +125,7 @@
 
 
 def trace_kernel(
-    state_ref, mat_ref, map_ref, proj_ref, sel_ref, orient_ref, code_ref, grp_ref, up_ref, down_ref, face_ref, mine_ref, info_ref,
+    state_ref, mat_ref, map_ref, proj_ref, sel_ref, orient_ref, code_ref, grp_ref, even_ref, odd_ref, face_ref, mine_ref, info_ref,
 ):
     low = lane_low((8, 128))
     flat = state_ref[...].reshape(48, 512)
@@ -151,8 +151,12 @@
     face_ref[...] = faces
     hi, lo = split2(faces)
     table = dot(jnp.concatenate([hi, lo], axis=0), orient_ref[...]).astype(bf16)
-    info = map_ref[...]
-    info_ref[...] = jnp.concatenate([info, info], axis=0)
+    info = jnp.concatenate([map_ref[...]] * 2, axis=0)
+    slot = lax.broadcasted_iota(jnp.int32, (8, SLOTS), 1)
+    turned = jnp.where(slot < 96, pltpu.roll(info, 96, 1), pltpu.roll(info, 32, 1))
+    odd = jnp.bitwise_and(lax.axis_index("elem"), 1) == 1
+    info = jnp.where((slot >= 64) & odd, turned, info)
+    info_ref[...] = info
     element, face, sub, orient = (info[i : i + 1] for i in range(4))
     material = slot_material(mat_ref, element)
     codes = code_rows([element.astype(f32), face.astype(f32), sub.astype(f32), orient.astype(f32), material])
@@ -181,8 +185,8 @@
         for g in range(8):
             grp_ref[g, :, lanes] = value[8 * g : 8 * g + 8]
             mine_ref[g, :, lanes] = value[8 * g : 8 * g + 8]
-        up_ref[:, lanes] = value[64:96]
-        down_ref[:, lanes] = value[96:128]
+        even_ref[:, lanes] = value[64:96]
+        odd_ref[:, lanes] = value[96:128]
 
     for j in range(3):
         r = slice(128 * j, 128 * j + 128)
@@ -245,9 +249,9 @@
     info = info_ref[...]
     element, face, sub, orient = (info[i : i + 1] for i in range(4))
     slot = lax.broadcasted_iota(jnp.int32, (1, SLOTS), 1)
-    group = jnp.where(
-        slot < 64, lax.shift_right_logical(slot, 3), 6 + lax.shift_right_logical(slot, 5)
-    )
+    odd = jnp.bitwise_and(lax.axis_index("elem"), 1)
+    side = jnp.bitwise_xor(jnp.bitwise_and(lax.shift_right_logical(slot, 5), 1), odd)
+    group = jnp.where(slot < 64, lax.shift_right_logical(slot, 3), 8 + side)
     position = jnp.where(slot < 64, jnp.bitwise_and(slot, 7), jnp.bitwise_and(slot, 31))
     limit = jnp.zeros((1, SLOTS), jnp.int32)
     for n in range(10):
@@ -339,7 +343,7 @@
 
 
 def mortar_kernel(
-    grp_ref, up_ref, down_ref, from_grp_ref, above_ref, below_ref, metric_ref,
+    grp_ref, even_ref, odd_ref, from_grp_ref, from_even_ref, from_odd_ref, metric_ref,
     sel_ref, orient_ref, base_ref, local_ref, spread_ref, hot_ref, back_ref, out_ref,
 ):
     chunk = 32
@@ -348,14 +352,14 @@
     for start in range(0, SLOTS, chunk):
         r = slice(start, start + chunk)
 
-        def rows(grp, up, down, at):
+        def rows(grp, even, odd, at):
             lanes = slice(at, at + 128)
             if start < 64:
                 return jnp.concatenate([grp[start // 8 + n, :, lanes] for n in range(chunk // 8)], axis=0)
-            return (up if start < 96 else down)[:, lanes]
-
-        mine = functools.partial(rows, grp_ref, up_ref, down_ref)
-        theirs = functools.partial(rows, from_grp_ref, above_ref, below_ref)
+            return (even if start < 96 else odd)[:, lanes]
+
+        mine = functools.partial(rows, grp_ref, even_ref, odd_ref)
+        theirs = functools.partial(rows, from_grp_ref, from_even_ref, from_odd_ref)
         states = []
         for j in range(3):
             states += paired(own, mine(128 * j), theirs(128 * j))
@@ -450,7 +454,7 @@
     codes_a = jnp.asarray(code_table([{0: 1, 1: 8, 3: 48}, {2: 1}, {4: 1}]), bf16)
     codes_c = jnp.asarray(code_table([{n: 1} for n in range(5)]), bf16)
 
-    grp, up, down, faces, mine, kept = call(
+    grp, even, odd, faces, mine, kept = call(
         trace_kernel,
         [(groups, CAPG, 512), (CAPS, 512), (CAPS, 512), (144, 128), (groups, CAPG, 512), ((8, SLOTS), jnp.int32)],
         {1},
@@ -458,20 +462,21 @@
         first=True,
         free=(0,),
     )
-    above = lax.ppermute(down, "elem", [(i + 1, i) for i in range(n_elem - 1)])
-    below = lax.ppermute(up, "elem", [(i, i + 1) for i in range(n_elem - 1)])
+    pairs = [[(i + n, i + 1 - n) for i in range(first, n_elem - 1, 2) for n in range(2)] for first in range(2)]
+    from_odd = lax.ppermute(odd, "elem", pairs[1])
+    arrived = lax.all_to_all(grp, "grp", split_axis=0, concat_axis=0, tiled=True)
+    from_even = lax.ppermute(even, "elem", pairs[0])
     held = call(
         local_kernel,
         [(6, 8, 512), (144, 128), (SLOTS, 640), ((384, 256), bf16), ((384, 512), bf16)],
         {1, 2, 3},
         (elements, material, metric, counts, neighbours, faces, derivs, kept, mortar_proj, codes_c),
     )
-    arrived = lax.all_to_all(grp, "grp", split_axis=0, concat_axis=0, tiled=True)
     (new,) = call(
         mortar_kernel,
         [(6, 8, 512)],
         {6},
-        (mine, up, down, arrived, above, below, metric, select, orients, *held),
+        (mine, even, odd, arrived, from_even, from_odd, metric, select, orients, *held),
         free=(0,),
     )
     return jnp.transpose(new, (1, 0, 2))

time: 30.4 us -> 31.3 us (1.030)
  the two profiles are of different devices: /device:TPU:1 before, /device:TPU:10 now
where the time goes in v3:
time: 31.3 us; the launch traced here: 31 us
  starting transfers between devices  21 us (67%)
  Pallas kernels  7.23 us (23%)
  waiting for transfers between devices  2.7 us (9%)
    ppermute x1, starting transfers between devices, section(): from_even = lax.ppermute(even, 'elem', pairs[0])  14 us
    pallas_call x3, Pallas kernels, call(): pl.pallas_call(kernel, out_shape=[jax.ShapeDtypeStruct(*s) if n in free e...  7.23 us
    all_to_all x1, starting transfers between devices, section(): lax.all_to_all(grp, 'grp', split_axis=0, concat_axis=0, tiled=True)  5.07 us
    ppermute x1, waiting for transfers between devices, section(): from_odd = lax.ppermute(odd, 'elem', pairs[1])  2.69 us
    ppermute x1, starting transfers between devices, section(): from_odd = lax.ppermute(odd, 'elem', pairs[1])  1.92 us
  transfers between devices with their start and end apart: 3, of which 1 were waited for; matrix products, arithmetic and copies ran while one was open for 0% of the time, Pallas kernels for 5%

profile of v3, /device:TPU:10, one launch (start us, length us, event | category | flops | bytes accessed | tf_op | source)
XLA Modules:
  0.0 31.0 jit_solution(4686277404400110524)
XLA Ops:
  0.0 0.0 copy-start.2
  0.0 0.0 copy-start.3
  0.0 0.0 copy-start.4
  0.0 2.9 %shard_map.118 = (f32[8,8,512]{2,1,0:T(8,128)}, f32[32,512]{1,0:T(8,128)S(1)}, f32[32,512]{1,0:T(8,128)S(1)}, f32[144,128]{1,0:T(8,128)S(1)}, f32[8,8,512]{2,1,0:T(8,128)S(1)}, /*index=5*/s32[8,128]{1,0:T(8,128)S(1)}) custom-call(f32[6,8,512]{2,1,0:T(8,128)} %bitcast.4, s32[8]{0:T(128)} %mat_ref.3, s32[4,128]{1,0:T(4,128)} %bitcast.6, ...), custom_call_target="tpu_custom_call" | custom-call | tf_op jit(solution)/shard_map/pallas_call | solution.py:434
  2.9 0.0 copy-start.5
  2.9 0.0 copy-start.6
  2.9 0.0 copy-start.1
  2.9 5.1 %all-to-all-start = ((f32[8,8,512]{2,1,0:T(8,128)}), f32[8,8,512]{2,1,0:T(8,128)S(1)}, u32[]{:S(2)}, u32[]{:S(2)}) async-start(f32[8,8,512]{2,1,0:T(8,128)} %get-tuple-element.19), calls=%async_computation | async-start | bytes 262144 | tf_op jit(solution)/shard_map/all_to_all | solution.py:467
  8.0 0.0 copy-start
  8.0 14.0 %collective-permute-start = (f32[32,512]{1,0:T(8,128)S(1)}, f32[32,512]{1,0:T(8,128)S(1)}, u32[]{:S(2)}, u32[]{:S(2)}) collective-permute-start(f32[32,512]{1,0:T(8,128)S(1)} %get-tuple-element.17.even_ref), channel_id=1, source_target_pairs={{0,8},{8,0},{16,24},{24,16},{32,40},{40,32},{48,56},{56,48},{64,72... | collective-permute-start | bytes 196616 | tf_op jit(solution)/shard_map/ppermute | solution.py:468
  22.0 1.9 %collective-permute-start.1 = (f32[32,512]{1,0:T(8,128)S(1)}, f32[32,512]{1,0:T(8,128)S(1)}, u32[]{:S(2)}, u32[]{:S(2)}) collective-permute-start(f32[32,512]{1,0:T(8,128)S(1)} %get-tuple-element.18.odd_ref), channel_id=1, source_target_pairs={{8,16},{16,8},{24,32},{32,24},{40,48},{48,40},{56,64},{64,56},{72,... | collective-permute-start | bytes 196616 | tf_op jit(solution)/shard_map/ppermute | solution.py:466
  23.9 0.0 copy-done.2
  23.9 0.0 copy-done.3
  23.9 0.0 copy-done.4
  23.9 0.0 copy-done.5
  23.9 0.0 copy-done.6
  23.9 1.5 %shard_map.119 = (f32[6,8,512]{2,1,0:T(8,128)S(1)}, f32[144,128]{1,0:T(8,128)S(1)}, f32[128,640]{1,0:T(8,128)S(1)}, bf16[384,256]{1,0:T(8,128)(2,1)S(1)}, bf16[384,512]{1,0:T(8,128)(2,1)S(1)}) custom-call(f32[6,8,512]{2,1,0:T(8,128)S(1)} %bitcast.5, s32[8]{0:T(128)} %mat_ref.3, f32[8]{0:T(128)} %metric_ref.3, s32[10]{0:T(128)} %bitcast.7, ...), custom_call_target="tpu_custom_call" | custom-call | tf_op jit(solution)/shard_map/pallas_call | solution.py:434
  25.4 0.0 collective-permute-done.from_even_ref
  25.4 2.7 %collective-permute-done.1.from_odd_ref = f32[32,512]{1,0:T(8,128)S(1)} collective-permute-done((f32[32,512]{1,0:T(8,128)S(1)}, f32[32,512]{1,0:T(8,128)S(1)}, u32[]{:S(2)}, u32[]{:S(2)}) %collective-permute-start.1) | collective-permute-done | bytes 65568 | tf_op jit(solution)/shard_map/ppermute | solution.py:466
  28.1 0.0 all-to-all-done.from_grp_ref
  28.1 0.0 copy-done.1
  28.1 0.0 copy-done
  28.1 2.9 %shard_map.120 = f32[6,8,512]{2,1,0:T(8,128)} custom-call(f32[8,8,512]{2,1,0:T(8,128)S(1)} %get-tuple-element.16.grp_ref, f32[32,512]{1,0:T(8,128)S(1)} %get-tuple-element.17.even_ref, f32[32,512]{1,0:T(8,128)S(1)} %get-tuple-element.18.odd_ref, f32[8,8,512]{2,1,0:T(8,128)S(1)} %all-to-all-done.from_grp_ref, ...), custom_call_target="tpu_custom_call" | custom-call | tf_op jit(solution)/shard_map/pallas_call | solution.py:434
Async XLA Ops:
  0.0 23.9 %copy-start.2 = (f32[4,64,64]{2,1,0:T(8,128)S(1)}, f32[4,64,64]{2,1,0:T(8,128)}, u32[]{:S(2)}) copy-start(f32[4,64,64]{2,1,0:T(8,128)} %proj_ref.3) | copy-start | bytes 196612
  0.0 23.9 %copy-start.3 = (f32[8,6,512]{2,0,1:T(8,128)S(1)}, f32[8,6,512]{2,0,1:T(8,128)}, u32[]{:S(2)}) copy-start(f32[8,6,512]{2,0,1:T(8,128)} %param.12) | copy-start | bytes 294916
  0.0 23.9 %copy-start.4 = (bf16[256,256]{1,0:T(8,128)(2,1)S(1)}, bf16[256,256]{1,0:T(8,128)(2,1)}, u32[]{:S(2)}) copy-start(bf16[256,256]{1,0:T(8,128)(2,1)} %constant.12.clone.deriv_ref) | copy-start | bytes 393220
  2.9 21.0 %copy-start.5 = (bf16[16,640]{1,0:T(8,128)(2,1)S(1)}, bf16[16,640]{1,0:T(8,128)(2,1)}, u32[]{:S(2)}) copy-start(bf16[16,640]{1,0:T(8,128)(2,1)} %constant.14.clone.code_ref) | copy-start | bytes 61444
  2.9 21.0 %copy-start.6 = (s32[8,6]{1,0:T(8,128)S(1)}, s32[8,6]{1,0:T(8,128)}, u32[]{:S(2)}) copy-start(s32[8,6]{1,0:T(8,128)} %near_ref.1) | copy-start | bytes 580
  2.9 25.2 %copy-start.1 = (bf16[512,256]{1,0:T(8,128)(2,1)S(1)}, bf16[512,256]{1,0:T(8,128)(2,1)}, u32[]{:S(2)}) copy-start(bf16[512,256]{1,0:T(8,128)(2,1)} %constant.10.clone.sel_ref) | copy-start | bytes 786436
  2.9 25.2 %all-to-all-start = ((f32[8,8,512]{2,1,0:T(8,128)}), f32[8,8,512]{2,1,0:T(8,128)S(1)}, u32[]{:S(2)}, u32[]{:S(2)}) async-start(f32[8,8,512]{2,1,0:T(8,128)} %get-tuple-element.19), calls=%async_computation | async-start | bytes 262144 | tf_op jit(solution)/shard_map/all_to_all | solution.py:467
  8.0 20.2 %copy-start = (bf16[128,1024]{1,0:T(8,128)(2,1)S(1)}, bf16[128,1024]{1,0:T(8,128)(2,1)}, u32[]{:S(2)}) copy-start(bf16[128,1024]{1,0:T(8,128)(2,1)} %constant.11.clone.orient_ref) | copy-start | bytes 786436
  8.0 17.5 %collective-permute-start = (f32[32,512]{1,0:T(8,128)S(1)}, f32[32,512]{1,0:T(8,128)S(1)}, u32[]{:S(2)}, u32[]{:S(2)}) collective-permute-start(f32[32,512]{1,0:T(8,128)S(1)} %get-tuple-element.17.even_ref), channel_id=1, source_target_pairs={{0,8},{8,0},{16,24},{24,16},{32,40},{40,32},{48,56},{56,48},{64,72... | collective-permute-start | bytes 196616 | tf_op jit(solution)/shard_map/ppermute | solution.py:468
  22.0 6.2 %collective-permute-start.1 = (f32[32,512]{1,0:T(8,128)S(1)}, f32[32,512]{1,0:T(8,128)S(1)}, u32[]{:S(2)}, u32[]{:S(2)}) collective-permute-start(f32[32,512]{1,0:T(8,128)S(1)} %get-tuple-element.18.odd_ref), channel_id=1, source_target_pairs={{8,16},{16,8},{24,32},{32,24},{40,48},{48,40},{56,64},{64,56},{72,... | collective-permute-start | bytes 196616 | tf_op jit(solution)/shard_map/ppermute | solution.py:466

commit v4 on v3

--- a/solution.py
+++ b/solution.py
@@ -1,5 +1,3 @@
-import functools
-
 import jax
 import jax.numpy as jnp
 import numpy as np
@@ -124,9 +122,50 @@
     return jnp.concatenate(rows + pad, axis=0).astype(bf16)
 
 
+def selection():
+    lane = lax.broadcasted_iota(jnp.int32, (1, 256), 1)
+    far = jnp.bitwise_and(lax.shift_right_logical(lane, 6), 1)
+    p = jnp.bitwise_and(lax.shift_right_logical(lane, 3), 7)
+    r = jnp.bitwise_and(lane, 7)
+    node = 64 * p + jnp.where(lane < 128, r + 56 * far, 8 * r + 7 * far)
+    row = lax.broadcasted_iota(jnp.int32, (512, 256), 0)
+    return jnp.where(row == node, 1.0, 0.0).astype(bf16)
+
+
+def orientations():
+    lane = lax.broadcasted_iota(jnp.int32, (1, 1024), 1)
+    half = jnp.bitwise_and(lane, 64)
+    p = jnp.bitwise_and(lax.shift_right_logical(lane, 3), 7)
+    r = jnp.bitwise_and(lane, 7)
+    turn = jnp.bitwise_and(lane, 512) != 0
+    p, r = jnp.where(turn, r, p), jnp.where(turn, p, r)
+    p = jnp.where(jnp.bitwise_and(lane, 128) != 0, 7 - p, p)
+    r = jnp.where(jnp.bitwise_and(lane, 256) != 0, 7 - r, r)
+    row = lax.broadcasted_iota(jnp.int32, (128, 1024), 0)
+    return jnp.where(row == half + 8 * p + r, 1.0, 0.0).astype(bf16)
+
+
 def trace_kernel(
-    state_ref, mat_ref, map_ref, proj_ref, sel_ref, orient_ref, code_ref, grp_ref, even_ref, odd_ref, face_ref, mine_ref, info_ref,
+    state_hbm, mat_hbm, map_hbm, proj_hbm, grp_hbm, even_ref, odd_ref, face_ref, mine_ref, info_ref,
+    state_ref, mat_ref, map_ref, proj_ref, sel_ref, orient_ref, in_sem, out_sem,
 ):
+    loads = [
+        pltpu.make_async_copy(src, dst, in_sem.at[n])
+        for n, (src, dst) in enumerate(
+            [(state_hbm, state_ref), (mat_hbm, mat_ref), (map_hbm, map_ref), (proj_hbm, proj_ref)]
+        )
+    ]
+    for load in loads:
+        load.start()
+    sel_ref[...] = selection()
+    orient_ref[...] = orientations()
+    code_row = lax.broadcasted_iota(jnp.int32, (16, 128), 0)
+    weights = jnp.where(code_row == 0, 1.0, jnp.where(code_row == 1, 8.0, jnp.where(code_row == 3, 48.0, 0.0)))
+    spreads = jnp.concatenate(
+        [weights, jnp.where(code_row == 2, 1.0, 0.0), jnp.where(code_row == 4, 1.0, 0.0)], axis=1
+    ).astype(bf16)
+    for load in loads:
+        load.wait()
     low = lane_low((8, 128))
     flat = state_ref[...].reshape(48, 512)
     picked = dot(jnp.concatenate(split3(flat), axis=0), sel_ref[...])
@@ -160,7 +199,7 @@
     element, face, sub, orient = (info[i : i + 1] for i in range(4))
     material = slot_material(mat_ref, element)
     codes = code_rows([element.astype(f32), face.astype(f32), sub.astype(f32), orient.astype(f32), material])
-    spread = dot(codes, code_ref[...], 0, 0)
+    spread = dot(codes, spreads, 0, 0)
     index = spread[:, 0:128].astype(jnp.int32)
     sub_of = spread[:, 128:256].astype(jnp.int32)
     lane = lax.broadcasted_iota(jnp.int32, (SLOTS, 128), 1)
@@ -179,72 +218,75 @@
     wide = dot(
         jnp.concatenate([h, x_lo.astype(bf16)], axis=1), jnp.concatenate([b_hi, b_hi], axis=1), 1, 1
     ) + dot(h, b_lo, 1, 1)
+    stores = []
 
     def put(at, value):
         lanes = slice(at, at + 128)
         for g in range(8):
-            grp_ref[g, :, lanes] = value[8 * g : 8 * g + 8]
             mine_ref[g, :, lanes] = value[8 * g : 8 * g + 8]
         even_ref[:, lanes] = value[64:96]
         odd_ref[:, lanes] = value[96:128]
-
+        store = pltpu.make_async_copy(mine_ref.at[:, :, lanes], grp_hbm.at[:, :, lanes], out_sem.at[at // 128])
+        store.start()
+        stores.append(store)
+
+    put(384, 1.4 + 0.27 * spread[:, 256:384])
     for j in range(3):
         r = slice(128 * j, 128 * j + 128)
         w = x_hi[r] + x_lo[r]
         for s in range(4):
             w = jnp.where(sub_of == s + 1, wide[r, 128 * s : 128 * s + 128], w)
         put(128 * j, w)
-    put(384, 1.4 + 0.27 * spread[:, 256:384])
-
-
-def hllc_correction(u, g, normal, own):
+    for store in stores:
+        store.wait()
+
+
+def primitives(u, g, n):
     inv = 1.0 / u[0]
-    vel = [u[1] * inv, u[2] * inv, u[3] * inv]
-    p = (g - 1.0) * (u[4] - 0.5 * (u[1] * vel[0] + u[2] * vel[1] + u[3] * vel[2]))
-    s = normal[0] * vel[0] + normal[1] * vel[1] + normal[2] * vel[2]
-    c = jnp.sqrt(g * p * inv)
-    lower, upper = s - c, s + c
-    left = jnp.minimum(lower, swap(lower))
-    right = jnp.maximum(upper, swap(upper))
-    wave = jnp.where(own, left, right)
-    relative = wave - s
-    mass = u[0] * relative
-    part = mass * s - p
-    middle = (part - swap(part)) / (mass - swap(mass))
-    chi = mass / (wave - middle)
-    shift = middle - s
-    star = [
-        chi,
-        chi * (vel[0] + shift * normal[0]),
-        chi * (vel[1] + shift * normal[1]),
-        chi * (vel[2] + shift * normal[2]),
-        chi * (u[4] * inv + shift * (middle + p / mass)),
-        chi * (u[5] * inv),
+    p = (g - 1.0) * (u[4] - 0.5 * inv * (u[1] * u[1] + u[2] * u[2] + u[3] * u[3]))
+    s = (n[0] * u[1] + n[1] * u[2] + n[2] * u[3]) * inv
+    return p, s, jnp.sqrt(g * p * inv)
+
+
+def flux_of(u, p, s, n):
+    return [u[0] * s, u[1] * s + p * n[0], u[2] * s + p * n[1], u[3] * s + p * n[2], (u[4] + p) * s, u[5] * s]
+
+
+def hllc(u_l, u_r, prim_l, prim_r, n):
+    (p_l, s_l, c_l), (p_r, s_r, c_r) = prim_l, prim_r
+    left = jnp.minimum(s_l - c_l, s_r - c_r)
+    right = jnp.maximum(s_l + c_l, s_r + c_r)
+    mass_l = u_l[0] * (left - s_l)
+    mass_r = u_r[0] * (right - s_r)
+    middle = (p_r - p_l + mass_l * s_l - mass_r * s_r) / (mass_l - mass_r)
+    take = (left >= 0.0) | (middle >= 0.0)
+    u = [jnp.where(take, x, y) for x, y in zip(u_l, u_r)]
+    p = jnp.where(take, p_l, p_r)
+    s = jnp.where(take, s_l, s_r)
+    mass = jnp.where(take, mass_l, mass_r)
+    wave = jnp.where(take, left, right)
+    use_star = jnp.where(take, -left, right) > 0.0
+    a = jnp.where(use_star, wave * (middle - s) / (wave - middle), 0.0)
+    speed = s + a
+    push = a * mass
+    lift = p + push
+    return [
+        u[0] * speed,
+        u[1] * speed + lift * n[0],
+        u[2] * speed + lift * n[1],
+        u[3] * speed + lift * n[2],
+        (u[4] + p) * speed + push * middle,
+        u[5] * speed,
     ]
-    flux = [
-        u[0] * s,
-        u[1] * s + p * normal[0],
-        u[2] * s + p * normal[1],
-        u[3] * s + p * normal[2],
-        (u[4] + p) * s,
-        u[5] * s,
-    ]
-    use_star = jnp.where(own, -wave, wave) > 0.0
-    take_own = (left >= 0.0) | (middle >= 0.0)
-    out = []
-    for v in range(6):
-        side = jnp.where(use_star, wave * (star[v] - u[v]), 0.0)
-        out.append(jnp.where(take_own, -side, flux[v] - swap(flux[v] + side)))
-    return out
-
-
-def paired(own, mine, theirs):
-    return jnp.where(own, mine, swap(theirs)), jnp.where(own, swap(mine), theirs)
+
+
+def two_halves(low, first, second):
+    return jnp.where(low, first, swap(second)), jnp.where(low, swap(first), second)
 
 
 def local_kernel(
     state_ref, mat_ref, metric_ref, count_ref, near_ref, face_ref, deriv_ref, info_ref, proj_ref, code_ref,
-    base_ref, local_ref, spread_ref, hot_ref, back_ref,
+    mine_ref, even_ref, odd_ref, base_ref, local_ref, sub_ref, own_ref, scale_ref, hot_ref, back_ref,
 ):
     info = info_ref[...]
     element, face, sub, orient = (info[i : i + 1] for i in range(4))
@@ -262,7 +304,8 @@
     codes = code_rows(
         [sub.astype(f32), alive] + [jnp.where(axis == d, sign, 0.0) for d in range(3)]
     )
-    spread_ref[...] = dot(codes, code_ref[...], 0, 0)
+    spread = dot(codes, code_ref[...], 0, 0)
+    sub_ref[...] = spread[:, 0:128]
     index = 48 * orient + 8 * face + element
     row = lax.broadcasted_iota(jnp.int32, (384, SLOTS), 0)
     beta = jnp.where(sub == 0, 1.0, 0.25)
@@ -325,54 +368,83 @@
         terms += [term, gap]
     terms.append(jnp.zeros((64, 512), bf16))
     theirs = dot(hot, jnp.concatenate(terms, axis=0))
-    own = lane_low((48, 128))
+    low = lane_low((48, 128))
     row = lax.broadcasted_iota(jnp.int32, (48, 128), 0)
     sign = jnp.where(jnp.bitwise_and(row, 8) != 0, 1.0, -1.0)
     normal = [jnp.where(lax.shift_right_logical(row, 4) == d, sign, 0.0) for d in range(3)]
-    states = []
-    for j in range(3):
-        states += paired(own, faces[48 * j : 48 * j + 48], theirs[:, 128 * j : 128 * j + 128])
-    g = jnp.where(own, heat_rows, theirs[:, 384:512])
-    corr = hllc_correction(states, g, normal, own)
-    for j in range(3):
-        packed = join_pair(own, corr[2 * j], corr[2 * j + 1])
+    mine, other = [], []
+    for j in range(3):
+        x, y = faces[48 * j : 48 * j + 48], theirs[:, 128 * j : 128 * j + 128]
+        mine += [x, swap(x)]
+        other += [y, swap(y)]
+    prim = primitives(mine, heat_rows, normal)
+    flux = flux_of(mine, prim[0], prim[1], normal)
+    through = hllc(mine, other, prim, primitives(other, theirs[:, 384:512], normal), normal)
+    corr = [f - h for f, h in zip(flux, through)]
+    for j in range(3):
+        packed = join_pair(low, corr[2 * j], corr[2 * j + 1])
         for k in range(6):
             local_ref[48 * j + 8 * k : 48 * j + 8 * k + 8, :] = jnp.where(
                 live[k], packed[8 * k : 8 * k + 8], 0.0
             )
+    low = lane_low((64, 128))
+
+    def rows(at):
+        lanes = slice(at, at + 128)
+        return (
+            jnp.concatenate([mine_ref[g, :, lanes] for g in range(8)], axis=0),
+            jnp.concatenate([even_ref[:, lanes], odd_ref[:, lanes]], axis=0),
+        )
+
+    states = []
+    for j in range(3):
+        states += two_halves(low, *rows(128 * j))
+    g = jnp.where(low, *rows(384))
+    slots = [
+        jnp.where(low, spread[0:64, 128 * n : 128 * n + 128], spread[64:128, 128 * n : 128 * n + 128])
+        for n in range(1, 5)
+    ]
+    prim = primitives(states, g, slots[1:])
+    kept = [*states, *prim, *flux_of(states, prim[0], prim[1], slots[1:]), *slots]
+    for n, x in enumerate(kept):
+        own_ref[n] = x
+    scale_ref[...] = (STEP * LIFT) * by_element(metric_ref, (8, 128))
 
 
 def mortar_kernel(
-    grp_ref, even_ref, odd_ref, from_grp_ref, from_even_ref, from_odd_ref, metric_ref,
-    sel_ref, orient_ref, base_ref, local_ref, spread_ref, hot_ref, back_ref, out_ref,
+    from_grp_ref, from_even_ref, from_odd_ref, sel_ref, orient_ref,
+    base_ref, local_ref, sub_ref, own_ref, scale_ref, hot_ref, back_ref, out_ref,
 ):
-    chunk = 32
-    own = lane_low((chunk, 128))
-    packed = [[], [], []]
-    for start in range(0, SLOTS, chunk):
-        r = slice(start, start + chunk)
-
-        def rows(grp, even, odd, at):
-            lanes = slice(at, at + 128)
-            if start < 64:
-                return jnp.concatenate([grp[start // 8 + n, :, lanes] for n in range(chunk // 8)], axis=0)
-            return (even if start < 96 else odd)[:, lanes]
-
-        mine = functools.partial(rows, grp_ref, even_ref, odd_ref)
-        theirs = functools.partial(rows, from_grp_ref, from_even_ref, from_odd_ref)
-        states = []
+    chunk = 16
+    low = lane_low((chunk, 128))
+    first, second = [[], [], []], [[], [], []]
+    for at in range(0, 64, chunk):
+        r = slice(at, at + chunk)
+
+        def rows(lane):
+            lanes = slice(lane, lane + 128)
+            elem_ref, start = (from_even_ref, at) if at < 32 else (from_odd_ref, at - 32)
+            grp = [from_grp_ref[at // 8 + n, :, lanes] for n in range(chunk // 8)]
+            return jnp.concatenate(grp, axis=0), elem_ref[start : start + chunk, lanes]
+
+        theirs = []
         for j in range(3):
-            states += paired(own, mine(128 * j), theirs(128 * j))
-        g = jnp.where(own, mine(384), theirs(384))
-        live = spread_ref[r, 128:256] > 0.5
-        normal = [spread_ref[r, 256 + 128 * d : 384 + 128 * d] for d in range(3)]
-        corr = hllc_correction(states, g, normal, own)
+            theirs += two_halves(low, *rows(128 * j))
+        g = jnp.where(low, *rows(384))
+        mine = [own_ref[n, r] for n in range(6)]
+        normal = [own_ref[n, r] for n in range(16, 19)]
+        live = own_ref[15, r] > 0.5
+        prim = tuple(own_ref[n, r] for n in range(6, 9))
+        through = hllc(mine, theirs, prim, primitives(theirs, g, normal), normal)
+        corr = [jnp.where(live, own_ref[9 + n, r] - through[n], 0.0) for n in range(6)]
         for j in range(3):
-            packed[j].append(jnp.where(live, join_pair(own, corr[2 * j], corr[2 * j + 1]), 0.0))
-    corr = jnp.concatenate(packed[0] + packed[1] + packed[2], axis=0)
+            x, y = two_halves(low, corr[2 * j], corr[2 * j + 1])
+            first[j].append(x)
+            second[j].append(y)
+    corr = jnp.concatenate([x for j in range(3) for x in first[j] + second[j]], axis=0)
     hi, lo = split2(corr)
     wide = dot(jnp.concatenate([hi, lo, hi], axis=1), back_ref[...])
-    sub_of = spread_ref[:, 0:128].astype(jnp.int32)
+    sub_of = sub_ref[...].astype(jnp.int32)
     back = []
     for j in range(3):
         r = slice(128 * j, 128 * j + 128)
@@ -409,7 +481,7 @@
     hi, lo = split2(side)
     placed = dot(jnp.concatenate([hi, lo], axis=0), sel_ref[...], 1, 1)
     placed = placed[0:48] + placed[48:96]
-    scale = (STEP * LIFT) * by_element(metric_ref, (8, 128))
+    scale = scale_ref[...]
     for v in range(6):
         for t in range(4):
             lanes = slice(128 * t, 128 * t + 128)
@@ -425,10 +497,10 @@
 VM = pl.BlockSpec(memory_space=pltpu.VMEM)
 
 
-def call(kernel, outs, scalars, args, first=False, free=()):
+def call(kernel, outs, scalars, args, free=()):
     outs = [s if isinstance(s[0], tuple) else (s, f32) for s in outs]
     held = [
-        a if first or n in scalars else pltpu.with_memory_space_constraint(a, pltpu.VMEM)
+        a if n in scalars else pltpu.with_memory_space_constraint(a, pltpu.VMEM)
         for n, a in enumerate(args)
     ]
     return pl.pallas_call(
@@ -436,6 +508,7 @@
         out_shape=[jax.ShapeDtypeStruct(*s) if n in free else pltpu.VMEM(*s) for n, s in enumerate(outs)],
         in_specs=[SM if n in scalars else VM for n in range(len(args))],
         out_specs=[VM] * len(outs),
+        compiler_params=pltpu.CompilerParams(vmem_limit_bytes=16 << 20),
     )(*held)
 
 
@@ -451,33 +524,52 @@
     d_hi = deriv.astype(bf16)
     d_lo = (deriv - d_hi.astype(np.float32)).astype(bf16)
     derivs = jnp.asarray(np.concatenate([d_hi, d_lo], axis=1))
-    codes_a = jnp.asarray(code_table([{0: 1, 1: 8, 3: 48}, {2: 1}, {4: 1}]), bf16)
     codes_c = jnp.asarray(code_table([{n: 1} for n in range(5)]), bf16)
 
-    grp, even, odd, faces, mine, kept = call(
+    far = pl.BlockSpec(memory_space=pl.ANY)
+    grp, even, odd, faces, mine, kept = pl.pallas_call(
         trace_kernel,
-        [(groups, CAPG, 512), (CAPS, 512), (CAPS, 512), (144, 128), (groups, CAPG, 512), ((8, SLOTS), jnp.int32)],
-        {1},
-        (elements, material, info, mortar_proj, select, orients, codes_a),
-        first=True,
-        free=(0,),
-    )
+        out_shape=[
+            jax.ShapeDtypeStruct((groups, CAPG, 512), f32),
+            pltpu.VMEM((CAPS, 512), f32),
+            pltpu.VMEM((CAPS, 512), f32),
+            pltpu.VMEM((144, 128), f32),
+            pltpu.VMEM((groups, CAPG, 512), f32),
+            pltpu.VMEM((8, SLOTS), jnp.int32),
+        ],
+        in_specs=[far] * 4,
+        out_specs=[far] + [VM] * 5,
+        scratch_shapes=[
+            pltpu.VMEM((6, 8, 512), f32),
+            pltpu.SMEM((8,), jnp.int32),
+            pltpu.VMEM((4, SLOTS), jnp.int32),
+            pltpu.VMEM((4, 64, 64), f32),
+            pltpu.VMEM((512, 256), bf16),
+            pltpu.VMEM((128, 1024), bf16),
+            pltpu.SemaphoreType.DMA((4,)),
+            pltpu.SemaphoreType.DMA((4,)),
+        ],
+        name="traces",
+        compiler_params=pltpu.CompilerParams(vmem_limit_bytes=16 << 20),
+    )(*(pltpu.with_memory_space_constraint(a, pltpu.HBM) for a in (elements, material, info, mortar_proj)))
     pairs = [[(i + n, i + 1 - n) for i in range(first, n_elem - 1, 2) for n in range(2)] for first in range(2)]
     from_odd = lax.ppermute(odd, "elem", pairs[1])
     arrived = lax.all_to_all(grp, "grp", split_axis=0, concat_axis=0, tiled=True)
     from_even = lax.ppermute(even, "elem", pairs[0])
     held = call(
         local_kernel,
-        [(6, 8, 512), (144, 128), (SLOTS, 640), ((384, 256), bf16), ((384, 512), bf16)],
+        [
+            (6, 8, 512), (144, 128), (SLOTS, 128), (19, 64, 128), (8, 128),
+            ((384, 256), bf16), ((384, 512), bf16),
+        ],
         {1, 2, 3},
-        (elements, material, metric, counts, neighbours, faces, derivs, kept, mortar_proj, codes_c),
+        (
+            elements, material, metric, counts, neighbours, faces, derivs, kept, mortar_proj, codes_c,
+            mine, even, odd,
+        ),
     )
     (new,) = call(
-        mortar_kernel,
-        [(6, 8, 512)],
-        {6},
-        (mine, even, odd, arrived, from_even, from_odd, metric, select, orients, *held),
-        free=(0,),
+        mortar_kernel, [(6, 8, 512)], set(), (arrived, from_even, from_odd, select, orients, *held), free=(0,)
     )
     return jnp.transpose(new, (1, 0, 2))
 

time: 31.3 us -> 30 us (0.958)
  Pallas kernels: 7.23 us -> 5.7 us
  local copies, waits for them, and re-layouts: 0.03 us -> 0.65 us
  waiting for transfers between devices: 2.7 us -> 2.38 us
    pallas_call x3 -> x2, Pallas kernels: 7.23 us -> 3.01 us  [call(): pl.pallas_call(kernel, out_shape=[jax.ShapeDtypeStruct(*s) if n in free e...]
    pallas_call x0 -> x1, Pallas kernels: none -> 2.69 us  [section(): pl.pallas_call(trace_kernel, out_shape=[jax.ShapeDtypeStruct((groups, CAP...]
    unnamed x14 -> x20, local copies, waits for them, and re-layouts: 0.03 us -> 0.65 us
    ppermute x1, waiting for transfers between devices: 2.69 us -> 2.37 us  [section(): from_odd = lax.ppermute(odd, 'elem', pairs[1])]
  transfers between devices with their start and end apart: 3 -> 3, of which waited for: 1 -> 1; matrix products, arithmetic and copies ran while one was open for 0% -> 0% of each run, Pallas kernels for 5% -> 4%
where the time goes in v4:
time: 30 us; the launch traced here: 29.7 us
  starting transfers between devices  20.9 us (70%)
  Pallas kernels  5.7 us (19%)
  waiting for transfers between devices  2.38 us (8%)
  local copies, waits for them, and re-layouts  0.65 us (2%)
    ppermute x1, starting transfers between devices, section(): from_even = lax.ppermute(even, 'elem', pairs[0])  13.9 us
    all_to_all x1, starting transfers between devices, section(): lax.all_to_all(grp, 'grp', split_axis=0, concat_axis=0, tiled=True)  5.06 us
    pallas_call x2, Pallas kernels, call(): pl.pallas_call(kernel, out_shape=[jax.ShapeDtypeStruct(*s) if n in free e...  3.01 us
    pallas_call x1, Pallas kernels, section(): pl.pallas_call(trace_kernel, out_shape=[jax.ShapeDtypeStruct((groups, CAP...  2.69 us
    ppermute x1, waiting for transfers between devices, section(): from_odd = lax.ppermute(odd, 'elem', pairs[1])  2.37 us
    ppermute x1, starting transfers between devices, section(): from_odd = lax.ppermute(odd, 'elem', pairs[1])  1.92 us
    unnamed x20, local copies, waits for them, and re-layouts  0.65 us
  transfers between devices with their start and end apart: 3, of which 1 were waited for; matrix products, arithmetic and copies ran while one was open for 0% of the time, Pallas kernels for 4%

profile of v4, /device:TPU:10, one launch (start us, length us, event | category | flops | bytes accessed | tf_op | source)
XLA Modules:
  0.0 29.7 jit_solution(9740708589628048582)
XLA Ops:
  0.0 0.0 copy-start.4
  0.0 2.7 %traces.1 = (f32[8,8,512]{2,1,0:T(8,128)}, f32[32,512]{1,0:T(8,128)S(1)}, f32[32,512]{1,0:T(8,128)S(1)}, f32[144,128]{1,0:T(8,128)S(1)}, f32[8,8,512]{2,1,0:T(8,128)S(1)}, /*index=5*/s32[8,128]{1,0:T(8,128)S(1)}) custom-call(f32[6,8,512]{2,1,0:T(8,128)} %bitcast.4, s32[8]{0:T(128)} %mat_ref.1, s32[4,128]{1,0:T(4,128)} %bitcast.7, f32[4,64,64]{2,1,0:T(8,128)} %proj_ref.1), custom_call_target="tpu_custom_call" | custom-call | tf_op jit(solution)/shard_map/traces/pallas_call | solution.py:530
  2.7 0.0 copy-start
  2.7 0.0 copy-start.1
  2.7 0.0 copy-start.5
  2.7 5.1 %all-to-all-start = ((f32[8,8,512]{2,1,0:T(8,128)}), f32[8,8,512]{2,1,0:T(8,128)S(1)}, u32[]{:S(2)}, u32[]{:S(2)}) async-start(f32[8,8,512]{2,1,0:T(8,128)} %get-tuple-element.18), calls=%async_computation | async-start | bytes 262144 | tf_op jit(solution)/shard_map/all_to_all | solution.py:557
  7.8 13.9 %collective-permute-start = (f32[32,512]{1,0:T(8,128)S(1)}, f32[32,512]{1,0:T(8,128)S(1)}, u32[]{:S(2)}, u32[]{:S(2)}) collective-permute-start(f32[32,512]{1,0:T(8,128)S(1)} %get-tuple-element.19.even_ref), channel_id=1, source_target_pairs={{0,8},{8,0},{16,24},{24,16},{32,40},{40,32},{48,56},{56,48},{64,72... | collective-permute-start | bytes 196616 | tf_op jit(solution)/shard_map/ppermute | solution.py:558
  21.7 0.0 copy-start.6
  21.7 1.9 %collective-permute-start.1 = (f32[32,512]{1,0:T(8,128)S(1)}, f32[32,512]{1,0:T(8,128)S(1)}, u32[]{:S(2)}, u32[]{:S(2)}) collective-permute-start(f32[32,512]{1,0:T(8,128)S(1)} %get-tuple-element.20.odd_ref), channel_id=1, source_target_pairs={{8,16},{16,8},{24,32},{32,24},{40,48},{48,40},{56,64},{64,56},{72,... | collective-permute-start | bytes 196616 | tf_op jit(solution)/shard_map/ppermute | solution.py:556
  23.6 0.0 copy-start.7
  23.6 0.0 copy-start.8
  23.6 0.0 copy-start.9
  23.7 0.0 copy-done.4
  23.7 0.0 copy-done
  23.7 0.0 copy-done.1
  23.7 0.0 copy-done.5
  23.7 0.0 copy-done.6
  23.7 0.6 %copy-done.7 = s32[8]{0:T(128)S(1)} copy-done((s32[8]{0:T(128)S(1)}, s32[8]{0:T(128)}, u32[]{:S(2)}) %copy-start.7) | copy-done | bytes 56
  24.3 0.0 copy-done.8
  24.3 0.0 copy-done.9
  24.3 0.0 copy-start.2
  24.3 0.0 copy-start.3
  24.3 1.1 %shard_map.109 = (f32[6,8,512]{2,1,0:T(8,128)S(1)}, f32[144,128]{1,0:T(8,128)S(1)}, f32[128,128]{1,0:T(8,128)S(1)}, f32[19,64,128]{2,1,0:T(8,128)S(1)}, f32[8,12...) custom-call(f32[6,8,512]{2,1,0:T(8,128)S(1)} %bitcast.5, s32[8]{0:T(128)S(1)} %copy-done.7, ...), custom_call_target="tpu_custom_call" | custom-call | tf_op jit(solution)/shard_map/pallas_call | solution.py:506
  25.5 0.0 collective-permute-done.from_even_ref
  25.5 2.4 %collective-permute-done.1.from_odd_ref = f32[32,512]{1,0:T(8,128)S(1)} collective-permute-done((f32[32,512]{1,0:T(8,128)S(1)}, f32[32,512]{1,0:T(8,128)S(1)}, u32[]{:S(2)}, u32[]{:S(2)}) %collective-permute-start.1) | collective-permute-done | bytes 65568 | tf_op jit(solution)/shard_map/ppermute | solution.py:556
  27.9 0.0 all-to-all-done.from_grp_ref
  27.9 0.0 copy-done.2
  27.9 0.0 copy-done.3
  27.9 1.9 %shard_map.110 = f32[6,8,512]{2,1,0:T(8,128)} custom-call(f32[8,8,512]{2,1,0:T(8,128)S(1)} %all-to-all-done.from_grp_ref, f32[32,512]{1,0:T(8,128)S(1)} %collective-permute-done.from_even_ref, f32[32,512]{1,0:T(8,128)S(1)} %collective-permute-done.1.from_odd_ref, bf16[512,256]{1,0:T(8,128)(2,1)S(1)} %copy-done.2, bf16[128,1024]{1,0:T(8,128)(2,1)S(1)} %copy-done.3, ...), custom_call_target="tpu_custom_call" | custom-call | tf_op jit(solution)/shard_map/pallas_call | solution.py:506
Async XLA Ops:
  0.0 23.7 %copy-start.4 = (bf16[256,256]{1,0:T(8,128)(2,1)S(1)}, bf16[256,256]{1,0:T(8,128)(2,1)}, u32[]{:S(2)}) copy-start(bf16[256,256]{1,0:T(8,128)(2,1)} %constant.10.clone.deriv_ref) | copy-start | bytes 393220
  2.7 21.0 %copy-start = (f32[4,64,64]{2,1,0:T(8,128)S(1)}, f32[4,64,64]{2,1,0:T(8,128)}, u32[]{:S(2)}) copy-start(f32[4,64,64]{2,1,0:T(8,128)} %proj_ref.1) | copy-start | bytes 196612
  2.7 21.0 %copy-start.1 = (f32[8,6,512]{2,0,1:T(8,128)S(1)}, f32[8,6,512]{2,0,1:T(8,128)}, u32[]{:S(2)}) copy-start(f32[8,6,512]{2,0,1:T(8,128)} %param.11) | copy-start | bytes 294916
  2.7 21.0 %copy-start.5 = (bf16[16,640]{1,0:T(8,128)(2,1)S(1)}, bf16[16,640]{1,0:T(8,128)(2,1)}, u32[]{:S(2)}) copy-start(bf16[16,640]{1,0:T(8,128)(2,1)} %constant.11.clone.code_ref) | copy-start | bytes 61444
  2.7 25.1 %all-to-all-start = ((f32[8,8,512]{2,1,0:T(8,128)}), f32[8,8,512]{2,1,0:T(8,128)S(1)}, u32[]{:S(2)}, u32[]{:S(2)}) async-start(f32[8,8,512]{2,1,0:T(8,128)} %get-tuple-element.18), calls=%async_computation | async-start | bytes 262144 | tf_op jit(solution)/shard_map/all_to_all | solution.py:557
  7.8 17.7 %collective-permute-start = (f32[32,512]{1,0:T(8,128)S(1)}, f32[32,512]{1,0:T(8,128)S(1)}, u32[]{:S(2)}, u32[]{:S(2)}) collective-permute-start(f32[32,512]{1,0:T(8,128)S(1)} %get-tuple-element.19.even_ref), channel_id=1, source_target_pairs={{0,8},{8,0},{16,24},{24,16},{32,40},{40,32},{48,56},{56,48},{64,72... | collective-permute-start | bytes 196616 | tf_op jit(solution)/shard_map/ppermute | solution.py:558
  21.7 2.0 %copy-start.6 = (s32[8,6]{1,0:T(8,128)S(1)}, s32[8,6]{1,0:T(8,128)}, u32[]{:S(2)}) copy-start(s32[8,6]{1,0:T(8,128)} %near_ref.1) | copy-start | bytes 580
  21.7 6.2 %collective-permute-start.1 = (f32[32,512]{1,0:T(8,128)S(1)}, f32[32,512]{1,0:T(8,128)S(1)}, u32[]{:S(2)}, u32[]{:S(2)}) collective-permute-start(f32[32,512]{1,0:T(8,128)S(1)} %get-tuple-element.20.odd_ref), channel_id=1, source_target_pairs={{8,16},{16,8},{24,32},{32,24},{40,48},{48,40},{56,64},{64,56},{72,... | collective-permute-start | bytes 196616 | tf_op jit(solution)/shard_map/ppermute | solution.py:556
  23.6 0.7 %copy-start.7 = (s32[8]{0:T(128)S(1)}, s32[8]{0:T(128)}, u32[]{:S(2)}) copy-start(s32[8]{0:T(128)} %mat_ref.1) | copy-start | bytes 100
  23.6 0.7 %copy-start.8 = (f32[8]{0:T(128)S(1)}, f32[8]{0:T(128)}, u32[]{:S(2)}) copy-start(f32[8]{0:T(128)} %metric_ref.1) | copy-start | bytes 100
  23.6 0.7 %copy-start.9 = (s32[1,10]{1,0:T(1,128)S(1)}, s32[1,10]{1,0:T(1,128)}, u32[]{:S(2)}) copy-start(s32[1,10]{1,0:T(1,128)} %param.16) | copy-start | bytes 124
  24.3 3.5 %copy-start.2 = (bf16[512,256]{1,0:T(8,128)(2,1)S(1)}, bf16[512,256]{1,0:T(8,128)(2,1)}, u32[]{:S(2)}) copy-start(bf16[512,256]{1,0:T(8,128)(2,1)} %constant.8.clone.sel_ref) | copy-start | bytes 786436
  24.3 3.5 %copy-start.3 = (bf16[128,1024]{1,0:T(8,128)(2,1)S(1)}, bf16[128,1024]{1,0:T(8,128)(2,1)}, u32[]{:S(2)}) copy-start(bf16[128,1024]{1,0:T(8,128)(2,1)} %constant.9.clone.orient_ref) | copy-start | bytes 786436

commit v5 on v4

--- a/solution.py
+++ b/solution.py
@@ -149,14 +149,15 @@
     state_hbm, mat_hbm, map_hbm, proj_hbm, grp_hbm, even_ref, odd_ref, face_ref, mine_ref, info_ref,
     state_ref, mat_ref, map_ref, proj_ref, sel_ref, orient_ref, in_sem, out_sem,
 ):
-    loads = [
-        pltpu.make_async_copy(src, dst, in_sem.at[n])
-        for n, (src, dst) in enumerate(
-            [(state_hbm, state_ref), (mat_hbm, mat_ref), (map_hbm, map_ref), (proj_hbm, proj_ref)]
-        )
-    ]
-    for load in loads:
-        load.start()
+    def load(src, dst, n):
+        copy = pltpu.make_async_copy(src, dst, in_sem.at[n])
+        copy.start()
+        return copy
+
+    map_load = load(map_hbm, map_ref, 0)
+    mat_load = load(mat_hbm, mat_ref, 1)
+    state_load = load(state_hbm, state_ref, 2)
+    proj_load = load(proj_hbm, proj_ref, 3)
     sel_ref[...] = selection()
     orient_ref[...] = orientations()
     code_row = lax.broadcasted_iota(jnp.int32, (16, 128), 0)
@@ -164,8 +165,26 @@
     spreads = jnp.concatenate(
         [weights, jnp.where(code_row == 2, 1.0, 0.0), jnp.where(code_row == 4, 1.0, 0.0)], axis=1
     ).astype(bf16)
-    for load in loads:
-        load.wait()
+    map_load.wait()
+    mat_load.wait()
+    info = jnp.concatenate([map_ref[...]] * 2, axis=0)
+    slot = lax.broadcasted_iota(jnp.int32, (8, SLOTS), 1)
+    turned = jnp.where(slot < 96, pltpu.roll(info, 96, 1), pltpu.roll(info, 32, 1))
+    odd = jnp.bitwise_and(lax.axis_index("elem"), 1) == 1
+    info = jnp.where((slot >= 64) & odd, turned, info)
+    info_ref[...] = info
+    element, face, sub, orient = (info[i : i + 1] for i in range(4))
+    material = slot_material(mat_ref, element)
+    codes = code_rows([element.astype(f32), face.astype(f32), sub.astype(f32), orient.astype(f32), material])
+    spread = dot(codes, spreads, 0, 0)
+    index = spread[:, 0:128].astype(jnp.int32)
+    sub_of = spread[:, 128:256].astype(jnp.int32)
+    lane = lax.broadcasted_iota(jnp.int32, (SLOTS, 128), 1)
+    one_hot = jnp.concatenate(
+        [jnp.where(index == lane + 128 * t, 1.0, 0.0).astype(bf16) for t in range(3)], axis=1
+    )
+    heat = 1.4 + 0.27 * spread[:, 256:384]
+    state_load.wait()
     low = lane_low((8, 128))
     flat = state_ref[...].reshape(48, 512)
     picked = dot(jnp.concatenate(split3(flat), axis=0), sel_ref[...])
@@ -190,53 +209,38 @@
     face_ref[...] = faces
     hi, lo = split2(faces)
     table = dot(jnp.concatenate([hi, lo], axis=0), orient_ref[...]).astype(bf16)
-    info = jnp.concatenate([map_ref[...]] * 2, axis=0)
-    slot = lax.broadcasted_iota(jnp.int32, (8, SLOTS), 1)
-    turned = jnp.where(slot < 96, pltpu.roll(info, 96, 1), pltpu.roll(info, 32, 1))
-    odd = jnp.bitwise_and(lax.axis_index("elem"), 1) == 1
-    info = jnp.where((slot >= 64) & odd, turned, info)
-    info_ref[...] = info
-    element, face, sub, orient = (info[i : i + 1] for i in range(4))
-    material = slot_material(mat_ref, element)
-    codes = code_rows([element.astype(f32), face.astype(f32), sub.astype(f32), orient.astype(f32), material])
-    spread = dot(codes, spreads, 0, 0)
-    index = spread[:, 0:128].astype(jnp.int32)
-    sub_of = spread[:, 128:256].astype(jnp.int32)
-    lane = lax.broadcasted_iota(jnp.int32, (SLOTS, 128), 1)
-    one_hot = jnp.concatenate(
-        [jnp.where(index == lane + 128 * t, 1.0, 0.0).astype(bf16) for t in range(3)], axis=1
-    )
     columns = []
     for part in range(6):
         block = table[48 * part : 48 * part + 48]
         columns.append(jnp.concatenate([block[:, 128 * o : 128 * o + 128] for o in range(8)], axis=0))
     gathered = dot(one_hot, jnp.concatenate(columns, axis=1))
-    x_hi = jnp.concatenate([gathered[:, 128 * j : 128 * j + 128] for j in range(3)], axis=0)
-    x_lo = jnp.concatenate([gathered[:, 384 + 128 * j : 512 + 128 * j] for j in range(3)], axis=0)
+    proj_load.wait()
     b_hi, b_lo = split2(jnp.concatenate(project_blocks(proj_ref), axis=0))
-    h = x_hi.astype(bf16)
-    wide = dot(
-        jnp.concatenate([h, x_lo.astype(bf16)], axis=1), jnp.concatenate([b_hi, b_hi], axis=1), 1, 1
-    ) + dot(h, b_lo, 1, 1)
+    b_twice = jnp.concatenate([b_hi, b_hi], axis=1)
+
+    def project(at):
+        q = slice(at, at + 64)
+        x_hi = jnp.concatenate([gathered[q, 128 * j : 128 * j + 128] for j in range(3)], axis=0)
+        x_lo = jnp.concatenate([gathered[q, 384 + 128 * j : 512 + 128 * j] for j in range(3)], axis=0)
+        h = x_hi.astype(bf16)
+        wide = dot(jnp.concatenate([h, x_lo.astype(bf16)], axis=1), b_twice, 1, 1) + dot(h, b_lo, 1, 1)
+        for j in range(3):
+            r = slice(64 * j, 64 * j + 64)
+            w = x_hi[r] + x_lo[r]
+            for s in range(4):
+                w = jnp.where(sub_of[q] == s + 1, wide[r, 128 * s : 128 * s + 128], w)
+            yield slice(128 * j, 128 * j + 128), w
+        yield slice(384, 512), heat[q]
+
     stores = []
-
-    def put(at, value):
-        lanes = slice(at, at + 128)
+    for n, (lanes, w) in enumerate(project(0)):
         for g in range(8):
-            mine_ref[g, :, lanes] = value[8 * g : 8 * g + 8]
-        even_ref[:, lanes] = value[64:96]
-        odd_ref[:, lanes] = value[96:128]
-        store = pltpu.make_async_copy(mine_ref.at[:, :, lanes], grp_hbm.at[:, :, lanes], out_sem.at[at // 128])
-        store.start()
-        stores.append(store)
-
-    put(384, 1.4 + 0.27 * spread[:, 256:384])
-    for j in range(3):
-        r = slice(128 * j, 128 * j + 128)
-        w = x_hi[r] + x_lo[r]
-        for s in range(4):
-            w = jnp.where(sub_of == s + 1, wide[r, 128 * s : 128 * s + 128], w)
-        put(128 * j, w)
+            mine_ref[g, :, lanes] = w[8 * g : 8 * g + 8]
+        stores.append(pltpu.make_async_copy(mine_ref.at[:, :, lanes], grp_hbm.at[:, :, lanes], out_sem.at[n]))
+        stores[-1].start()
+    for lanes, w in project(64):
+        even_ref[:, lanes] = w[0:32]
+        odd_ref[:, lanes] = w[32:64]
     for store in stores:
         store.wait()
 
@@ -412,8 +416,8 @@
 
 
 def mortar_kernel(
-    from_grp_ref, from_even_ref, from_odd_ref, sel_ref, orient_ref,
-    base_ref, local_ref, sub_ref, own_ref, scale_ref, hot_ref, back_ref, out_ref,
+    from_grp_ref, from_even_ref, from_late_ref, from_odd_ref, sel_ref, orient_ref,
+    base_ref, local_ref, sub_ref, own_ref, scale_ref, hot_ref, back_ref, out_hbm, new_ref, sem,
 ):
     chunk = 16
     low = lane_low((chunk, 128))
@@ -423,9 +427,10 @@
 
         def rows(lane):
             lanes = slice(lane, lane + 128)
-            elem_ref, start = (from_even_ref, at) if at < 32 else (from_odd_ref, at - 32)
-            grp = [from_grp_ref[at // 8 + n, :, lanes] for n in range(chunk // 8)]
-            return jnp.concatenate(grp, axis=0), elem_ref[start : start + chunk, lanes]
+            grp = jnp.concatenate([from_grp_ref[at // 8 + n, :, lanes] for n in range(chunk // 8)], axis=0)
+            if at < 32:
+                return grp, from_even_ref[r, lanes] + from_late_ref[r, lanes]
+            return grp, from_odd_ref[at - 32 : at - 32 + chunk, lanes]
 
         theirs = []
         for j in range(3):
@@ -482,6 +487,7 @@
     placed = dot(jnp.concatenate([hi, lo], axis=0), sel_ref[...], 1, 1)
     placed = placed[0:48] + placed[48:96]
     scale = scale_ref[...]
+    stores = []
     for v in range(6):
         for t in range(4):
             lanes = slice(128 * t, 128 * t + 128)
@@ -490,7 +496,13 @@
                 value = value + jnp.where(low, lift[v][0], 0.0)
             if t == 3:
                 value = value + jnp.where(low, 0.0, lift[v][0])
-            out_ref[v, :, lanes] = base_ref[v, :, lanes] + scale * value
+            new_ref[v, :, lanes] = base_ref[v, :, lanes] + scale * value
+        if v % 2 == 1:
+            pair = pl.ds(v - 1, 2)
+            stores.append(pltpu.make_async_copy(new_ref.at[pair], out_hbm.at[pair], sem.at[v // 2]))
+            stores[-1].start()
+    for store in stores:
+        store.wait()
 
 
 SM = pl.BlockSpec(memory_space=pltpu.SMEM)
@@ -552,10 +564,16 @@
         name="traces",
         compiler_params=pltpu.CompilerParams(vmem_limit_bytes=16 << 20),
     )(*(pltpu.with_memory_space_constraint(a, pltpu.HBM) for a in (elements, material, info, mortar_proj)))
-    pairs = [[(i + n, i + 1 - n) for i in range(first, n_elem - 1, 2) for n in range(2)] for first in range(2)]
-    from_odd = lax.ppermute(odd, "elem", pairs[1])
+    swaps = [
+        [((i + n) * groups + g, (i + 1 - n) * groups + g) for i in range(first, n_elem - 1, 2) for g in range(groups) for n in range(2)]
+        for first in range(2)
+    ]
+    late = [(0, groups), (groups, 0)]
+    axes = ("elem", "grp")
+    from_even = lax.ppermute(even, axes, [pair for pair in swaps[0] if pair not in late])
     arrived = lax.all_to_all(grp, "grp", split_axis=0, concat_axis=0, tiled=True)
-    from_even = lax.ppermute(even, "elem", pairs[0])
+    from_odd = lax.ppermute(odd, axes, swaps[1])
+    from_late = lax.ppermute(even, axes, late)
     held = call(
         local_kernel,
         [
@@ -568,9 +586,16 @@
             mine, even, odd,
         ),
     )
-    (new,) = call(
-        mortar_kernel, [(6, 8, 512)], set(), (arrived, from_even, from_odd, select, orients, *held), free=(0,)
-    )
+    operands = (arrived, from_even, from_late, from_odd, select, orients, *held)
+    new = pl.pallas_call(
+        mortar_kernel,
+        out_shape=jax.ShapeDtypeStruct((6, 8, 512), f32),
+        in_specs=[VM] * len(operands),
+        out_specs=far,
+        scratch_shapes=[pltpu.VMEM((6, 8, 512), f32), pltpu.SemaphoreType.DMA((3,))],
+        name="mortar",
+        compiler_params=pltpu.CompilerParams(vmem_limit_bytes=16 << 20),
+    )(*(pltpu.with_memory_space_constraint(a, pltpu.VMEM) for a in operands))
     return jnp.transpose(new, (1, 0, 2))
 
 

time: 30 us -> 31 us (1.033)
  starting transfers between devices: 20.9 us -> 21.5 us
  Pallas kernels: 5.7 us -> 6.03 us
    pallas_call x0 -> x1, Pallas kernels: none -> 1.9 us  [section(): pl.pallas_call(mortar_kernel, out_shape=jax.ShapeDtypeStruct((6, 8, 512),...]
    pallas_call x2 -> x1, Pallas kernels: 3.01 us -> 1.14 us  [call(): pl.pallas_call(kernel, out_shape=[jax.ShapeDtypeStruct(*s) if n in free e...]
    ppermute x2 -> x3, starting transfers between devices: 15.8 us -> 16.4 us  [the longest x1 13.9 us: section(): lax.ppermute(even, axes, [pair for pair in swaps[0] if pair not in late])]
    ppermute x2 -> x3, waiting for transfers between devices: 2.38 us -> 2.37 us  [the longest x1 2.36 us: section(): from_odd = lax.ppermute(odd, axes, swaps[1])]
  transfers between devices with their start and end apart: 3 -> 4, of which waited for: 1 -> 1; matrix products, arithmetic and copies ran while one was open for 0% -> 0% of each run, Pallas kernels for 4% -> 4%
where the time goes in v5:
time: 31 us; the launch traced here: 30.7 us
  starting transfers between devices  21.5 us (69%)
  Pallas kernels  6.03 us (19%)
  waiting for transfers between devices  2.37 us (8%)
  local copies, waits for them, and re-layouts  0.65 us (2%)
    ppermute x1, starting transfers between devices, section(): lax.ppermute(even, axes, [pair for pair in swaps[0] if pair not in late])  13.9 us
    all_to_all x1, starting transfers between devices, section(): lax.all_to_all(grp, 'grp', split_axis=0, concat_axis=0, tiled=True)  5.06 us
    pallas_call x1, Pallas kernels, section(): pl.pallas_call(trace_kernel, out_shape=[jax.ShapeDtypeStruct((groups, CAP...  2.99 us
    ppermute x1, waiting for transfers between devices, section(): from_odd = lax.ppermute(odd, axes, swaps[1])  2.36 us
    ppermute x1, starting transfers between devices, section(): from_odd = lax.ppermute(odd, axes, swaps[1])  1.92 us
    pallas_call x1, Pallas kernels, section(): pl.pallas_call(mortar_kernel, out_shape=jax.ShapeDtypeStruct((6, 8, 512),...  1.9 us
    pallas_call x1, Pallas kernels, call(): pl.pallas_call(kernel, out_shape=[jax.ShapeDtypeStruct(*s) if n in free e...  1.14 us
    ppermute x1, starting transfers between devices, section(): from_late = lax.ppermute(even, axes, late)  0.66 us
  transfers between devices with their start and end apart: 4, of which 1 were waited for; matrix products, arithmetic and copies ran while one was open for 0% of the time, Pallas kernels for 4%

profile of v5, /device:TPU:10, one launch (start us, length us, event | category | flops | bytes accessed | tf_op | source)
XLA Modules:
  0.0 30.7 jit_solution(7201146177611134246)
XLA Ops:
  0.0 0.0 copy-start.4
  0.0 3.0 %traces.1 = (f32[8,8,512]{2,1,0:T(8,128)}, f32[32,512]{1,0:T(8,128)S(1)}, f32[32,512]{1,0:T(8,128)S(1)}, f32[144,128]{1,0:T(8,128)S(1)}, f32[8,8,512]{2,1,0:T(8,128)S(1)}, /*index=5*/s32[8,128]{1,0:T(8,128)S(1)}) custom-call(f32[6,8,512]{2,1,0:T(8,128)} %bitcast.4, s32[8]{0:T(128)} %mat_ref.1, s32[4,128]{1,0:T(4,128)} %bitcast.7, f32[4,64,64]{2,1,0:T(8,128)} %proj_ref.1), custom_call_target="tpu_custom_call" | custom-call | tf_op jit(solution)/shard_map/traces/pallas_call | solution.py:542
  3.0 0.0 copy-start
  3.0 0.0 copy-start.1
  3.0 0.0 copy-start.5
  3.0 5.1 %all-to-all-start = ((f32[8,8,512]{2,1,0:T(8,128)}), f32[8,8,512]{2,1,0:T(8,128)S(1)}, u32[]{:S(2)}, u32[]{:S(2)}) async-start(f32[8,8,512]{2,1,0:T(8,128)} %get-tuple-element.18), calls=%async_computation | async-start | bytes 262144 | tf_op jit(solution)/shard_map/all_to_all | solution.py:574
  8.1 13.9 %collective-permute-start = (f32[32,512]{1,0:T(8,128)S(1)}, f32[32,512]{1,0:T(8,128)S(1)}, u32[]{:S(2)}, u32[]{:S(2)}) collective-permute-start(f32[32,512]{1,0:T(8,128)S(1)} %get-tuple-element.19.even_ref), channel_id=1, source_target_pairs={{1,9},{9,1},{2,10},{10,2},{3,11},{11,3},{4,12},{12,4},{5,13},{13,5... | collective-permute-start | bytes 196616 | tf_op jit(solution)/shard_map/ppermute | solution.py:573
  22.0 0.7 %collective-permute-start.1 = (f32[32,512]{1,0:T(8,128)S(1)}, f32[32,512]{1,0:T(8,128)S(1)}, u32[]{:S(2)}, u32[]{:S(2)}) collective-permute-start(f32[32,512]{1,0:T(8,128)S(1)} %get-tuple-element.19.even_ref), channel_id=1, source_target_pairs={{0,8},{8,0}} | collective-permute-start | bytes 196616 | tf_op jit(solution)/shard_map/ppermute | solution.py:576
  22.6 0.0 copy-start.6
  22.7 1.9 %collective-permute-start.2 = (f32[32,512]{1,0:T(8,128)S(1)}, f32[32,512]{1,0:T(8,128)S(1)}, u32[]{:S(2)}, u32[]{:S(2)}) collective-permute-start(f32[32,512]{1,0:T(8,128)S(1)} %get-tuple-element.20.odd_ref), channel_id=1, source_target_pairs={{8,16},{16,8},{9,17},{17,9},{10,18},{18,10},{11,19},{19,11},{12,20... | collective-permute-start | bytes 196616 | tf_op jit(solution)/shard_map/ppermute | solution.py:575
  24.6 0.0 copy-start.7
  24.6 0.0 copy-start.8
  24.6 0.0 copy-start.9
  24.6 0.0 copy-done.4
  24.6 0.0 copy-done
  24.6 0.0 copy-done.1
  24.6 0.0 copy-done.5
  24.7 0.0 copy-done.6
  24.7 0.6 %copy-done.7 = s32[8]{0:T(128)S(1)} copy-done((s32[8]{0:T(128)S(1)}, s32[8]{0:T(128)}, u32[]{:S(2)}) %copy-start.7) | copy-done | bytes 56
  25.2 0.0 copy-done.8
  25.3 0.0 copy-done.9
  25.3 0.0 copy-start.2
  25.3 0.0 copy-start.3
  25.3 1.1 %shard_map.109 = (f32[6,8,512]{2,1,0:T(8,128)S(1)}, f32[144,128]{1,0:T(8,128)S(1)}, f32[128,128]{1,0:T(8,128)S(1)}, f32[19,64,128]{2,1,0:T(8,128)S(1)}, f32[8,12...) custom-call(f32[6,8,512]{2,1,0:T(8,128)S(1)} %bitcast.5, s32[8]{0:T(128)S(1)} %copy-done.7, ...), custom_call_target="tpu_custom_call" | custom-call | tf_op jit(solution)/shard_map/pallas_call | solution.py:518
  26.4 0.0 collective-permute-done.from_even_ref
  26.4 0.0 collective-permute-done.1.from_late_ref
  26.4 2.4 %collective-permute-done.2.from_odd_ref = f32[32,512]{1,0:T(8,128)S(1)} collective-permute-done((f32[32,512]{1,0:T(8,128)S(1)}, f32[32,512]{1,0:T(8,128)S(1)}, u32[]{:S(2)}, u32[]{:S(2)}) %collective-permute-start.2) | collective-permute-done | bytes 65568 | tf_op jit(solution)/shard_map/ppermute | solution.py:575
  28.8 0.0 all-to-all-done.from_grp_ref
  28.8 0.0 copy-done.2
  28.8 0.0 copy-done.3
  28.8 1.9 %mortar.1 = f32[6,8,512]{2,1,0:T(8,128)} custom-call(f32[8,8,512]{2,1,0:T(8,128)S(1)} %all-to-all-done.from_grp_ref, f32[32,512]{1,0:T(8,128)S(1)} %collective-permute-done.from_even_ref, f32[32,512]{1,0:T(8,128)S(1)} %collective-permute-done.1.from_late_ref, f32[32,512]{1,0:T(8,128)S(1)} %collective-permute-done.2.from_odd_ref, ...), custom_call_target="tpu_custom_call" | custom-call | tf_op jit(solution)/shard_map/mortar/pallas_call | solution.py:590
Async XLA Ops:
  0.0 24.6 %copy-start.4 = (bf16[256,256]{1,0:T(8,128)(2,1)S(1)}, bf16[256,256]{1,0:T(8,128)(2,1)}, u32[]{:S(2)}) copy-start(bf16[256,256]{1,0:T(8,128)(2,1)} %constant.10.clone.deriv_ref) | copy-start | bytes 393220
  3.0 21.6 %copy-start = (f32[4,64,64]{2,1,0:T(8,128)S(1)}, f32[4,64,64]{2,1,0:T(8,128)}, u32[]{:S(2)}) copy-start(f32[4,64,64]{2,1,0:T(8,128)} %proj_ref.1) | copy-start | bytes 196612
  3.0 21.6 %copy-start.1 = (f32[8,6,512]{2,0,1:T(8,128)S(1)}, f32[8,6,512]{2,0,1:T(8,128)}, u32[]{:S(2)}) copy-start(f32[8,6,512]{2,0,1:T(8,128)} %param.11) | copy-start | bytes 294916
  3.0 21.6 %copy-start.5 = (bf16[16,640]{1,0:T(8,128)(2,1)S(1)}, bf16[16,640]{1,0:T(8,128)(2,1)}, u32[]{:S(2)}) copy-start(bf16[16,640]{1,0:T(8,128)(2,1)} %constant.11.clone.code_ref) | copy-start | bytes 61444
  3.0 25.8 %all-to-all-start = ((f32[8,8,512]{2,1,0:T(8,128)}), f32[8,8,512]{2,1,0:T(8,128)S(1)}, u32[]{:S(2)}, u32[]{:S(2)}) async-start(f32[8,8,512]{2,1,0:T(8,128)} %get-tuple-element.18), calls=%async_computation | async-start | bytes 262144 | tf_op jit(solution)/shard_map/all_to_all | solution.py:574
  8.1 18.3 %collective-permute-start = (f32[32,512]{1,0:T(8,128)S(1)}, f32[32,512]{1,0:T(8,128)S(1)}, u32[]{:S(2)}, u32[]{:S(2)}) collective-permute-start(f32[32,512]{1,0:T(8,128)S(1)} %get-tuple-element.19.even_ref), channel_id=1, source_target_pairs={{1,9},{9,1},{2,10},{10,2},{3,11},{11,3},{4,12},{12,4},{5,13},{13,5... | collective-permute-start | bytes 196616 | tf_op jit(solution)/shard_map/ppermute | solution.py:573
  22.0 4.5 %collective-permute-start.1 = (f32[32,512]{1,0:T(8,128)S(1)}, f32[32,512]{1,0:T(8,128)S(1)}, u32[]{:S(2)}, u32[]{:S(2)}) collective-permute-start(f32[32,512]{1,0:T(8,128)S(1)} %get-tuple-element.19.even_ref), channel_id=1, source_target_pairs={{0,8},{8,0}} | collective-permute-start | bytes 196616 | tf_op jit(solution)/shard_map/ppermute | solution.py:576
  22.6 2.0 %copy-start.6 = (s32[8,6]{1,0:T(8,128)S(1)}, s32[8,6]{1,0:T(8,128)}, u32[]{:S(2)}) copy-start(s32[8,6]{1,0:T(8,128)} %near_ref.1) | copy-start | bytes 580
  22.7 6.2 %collective-permute-start.2 = (f32[32,512]{1,0:T(8,128)S(1)}, f32[32,512]{1,0:T(8,128)S(1)}, u32[]{:S(2)}, u32[]{:S(2)}) collective-permute-start(f32[32,512]{1,0:T(8,128)S(1)} %get-tuple-element.20.odd_ref), channel_id=1, source_target_pairs={{8,16},{16,8},{9,17},{17,9},{10,18},{18,10},{11,19},{19,11},{12,20... | collective-permute-start | bytes 196616 | tf_op jit(solution)/shard_map/ppermute | solution.py:575
  24.6 0.7 %copy-start.7 = (s32[8]{0:T(128)S(1)}, s32[8]{0:T(128)}, u32[]{:S(2)}) copy-start(s32[8]{0:T(128)} %mat_ref.1) | copy-start | bytes 100
  24.6 0.7 %copy-start.8 = (f32[8]{0:T(128)S(1)}, f32[8]{0:T(128)}, u32[]{:S(2)}) copy-start(f32[8]{0:T(128)} %metric_ref.1) | copy-start | bytes 100
  24.6 0.7 %copy-start.9 = (s32[1,10]{1,0:T(1,128)S(1)}, s32[1,10]{1,0:T(1,128)}, u32[]{:S(2)}) copy-start(s32[1,10]{1,0:T(1,128)} %param.16) | copy-start | bytes 124
  25.3 3.5 %copy-start.2 = (bf16[512,256]{1,0:T(8,128)(2,1)S(1)}, bf16[512,256]{1,0:T(8,128)(2,1)}, u32[]{:S(2)}) copy-start(bf16[512,256]{1,0:T(8,128)(2,1)} %constant.8.clone.sel_ref) | copy-start | bytes 786436
  25.3 3.5 %copy-start.3 = (bf16[128,1024]{1,0:T(8,128)(2,1)S(1)}, bf16[128,1024]{1,0:T(8,128)(2,1)}, u32[]{:S(2)}) copy-start(bf16[128,1024]{1,0:T(8,128)(2,1)} %constant.9.clone.orient_ref) | copy-start | bytes 786436

commit v6 on v5

--- a/solution.py
+++ b/solution.py
@@ -10,6 +10,7 @@
 CAPG = 8
 CAPS = 32
 SLOTS = 128
+ROWS = 25
 STEP = 0.002
 LIFT = 49.0
 
@@ -35,19 +36,6 @@
     return (np.arange(512)[:, None] == nodes[None, :]).astype(np.float32)
 
 
-def orient_table():
-    first, second = np.meshgrid(np.arange(8), np.arange(8), indexing="ij")
-    out = np.zeros((128, 1024), np.float32)
-    for orient in range(8):
-        p, r = (second, first) if orient & 4 else (first, second)
-        p = 7 - p if orient & 1 else p
-        r = 7 - r if orient & 2 else r
-        source = (8 * p + r).reshape(64)
-        for half in range(2):
-            out[half * 64 + source, orient * 128 + half * 64 + np.arange(64)] = 1.0
-    return out
-
-
 def deriv_table():
     d = cheb_matrix()
     along_b = np.kron(np.eye(2), np.kron(d, np.eye(8))).T
@@ -132,22 +120,37 @@
     return jnp.where(row == node, 1.0, 0.0).astype(bf16)
 
 
-def orientations():
-    lane = lax.broadcasted_iota(jnp.int32, (1, 1024), 1)
-    half = jnp.bitwise_and(lane, 64)
+def lane_sources(orient, back):
+    lane = lax.broadcasted_iota(jnp.int32, orient.shape, 1)
     p = jnp.bitwise_and(lax.shift_right_logical(lane, 3), 7)
     r = jnp.bitwise_and(lane, 7)
-    turn = jnp.bitwise_and(lane, 512) != 0
-    p, r = jnp.where(turn, r, p), jnp.where(turn, p, r)
-    p = jnp.where(jnp.bitwise_and(lane, 128) != 0, 7 - p, p)
-    r = jnp.where(jnp.bitwise_and(lane, 256) != 0, 7 - r, r)
-    row = lax.broadcasted_iota(jnp.int32, (128, 1024), 0)
-    return jnp.where(row == half + 8 * p + r, 1.0, 0.0).astype(bf16)
+    turn = jnp.bitwise_and(orient, 4) != 0
+    flip_p = jnp.bitwise_and(orient, 1) != 0
+    flip_r = jnp.bitwise_and(orient, 2) != 0
+    if not back:
+        p, r = jnp.where(turn, r, p), jnp.where(turn, p, r)
+    p = jnp.where(flip_p, 7 - p, p)
+    r = jnp.where(flip_r, 7 - r, r)
+    if back:
+        p, r = jnp.where(turn, r, p), jnp.where(turn, p, r)
+    return jnp.bitwise_and(lane, 64) + 8 * p + r
+
+
+def reorder(x, source):
+    return jnp.take_along_axis(x, source, axis=1, mode="promise_in_bounds")
+
+
+def stacked(table):
+    gap = jnp.zeros((16, table.shape[1]), bf16)
+    terms = []
+    for term in split3(table):
+        terms += [term, gap]
+    return jnp.concatenate(terms + [jnp.zeros((64, table.shape[1]), bf16)], axis=0)
 
 
 def trace_kernel(
     state_hbm, mat_hbm, map_hbm, proj_hbm, grp_hbm, even_ref, odd_ref, face_ref, mine_ref, info_ref,
-    state_ref, mat_ref, map_ref, proj_ref, sel_ref, orient_ref, in_sem, out_sem,
+    state_ref, mat_ref, map_ref, proj_ref, sel_ref, pack_ref, in_sem, out_sem,
 ):
     def load(src, dst, n):
         copy = pltpu.make_async_copy(src, dst, in_sem.at[n])
@@ -159,12 +162,12 @@
     state_load = load(state_hbm, state_ref, 2)
     proj_load = load(proj_hbm, proj_ref, 3)
     sel_ref[...] = selection()
-    orient_ref[...] = orientations()
     code_row = lax.broadcasted_iota(jnp.int32, (16, 128), 0)
-    weights = jnp.where(code_row == 0, 1.0, jnp.where(code_row == 1, 8.0, jnp.where(code_row == 3, 48.0, 0.0)))
-    spreads = jnp.concatenate(
-        [weights, jnp.where(code_row == 2, 1.0, 0.0), jnp.where(code_row == 4, 1.0, 0.0)], axis=1
-    ).astype(bf16)
+    weights = jnp.where(code_row == 0, 1.0, jnp.where(code_row == 1, 8.0, 0.0))
+    spreads = jnp.concatenate([weights] + [jnp.where(code_row == n, 1.0, 0.0) for n in range(2, 5)], axis=1)
+    place = lax.broadcasted_iota(jnp.int32, (SLOTS, 128), 0)
+    lane = lax.broadcasted_iota(jnp.int32, (SLOTS, 128), 1)
+    fan = jnp.where(jnp.bitwise_and(place, 7) == lax.shift_right_logical(lane, 4), 1.0, 0.0).astype(bf16)
     map_load.wait()
     mat_load.wait()
     info = jnp.concatenate([map_ref[...]] * 2, axis=0)
@@ -176,14 +179,18 @@
     element, face, sub, orient = (info[i : i + 1] for i in range(4))
     material = slot_material(mat_ref, element)
     codes = code_rows([element.astype(f32), face.astype(f32), sub.astype(f32), orient.astype(f32), material])
-    spread = dot(codes, spreads, 0, 0)
+    spread = dot(codes, spreads.astype(bf16), 0, 0)
     index = spread[:, 0:128].astype(jnp.int32)
     sub_of = spread[:, 128:256].astype(jnp.int32)
-    lane = lax.broadcasted_iota(jnp.int32, (SLOTS, 128), 1)
+    source = lane_sources(spread[:, 256:384].astype(jnp.int32), False)
+    hit = jnp.bitwise_and(lane, 63) == index
     one_hot = jnp.concatenate(
-        [jnp.where(index == lane + 128 * t, 1.0, 0.0).astype(bf16) for t in range(3)], axis=1
-    )
-    heat = 1.4 + 0.27 * spread[:, 256:384]
+        [jnp.where(hit, 1.0, 0.0), jnp.where(hit & (lane < 64), 1.0, 0.0)], axis=1
+    ).astype(bf16)
+    heat = 1.4 + 0.27 * spread[:, 384:512]
+    peer = lax.broadcasted_iota(jnp.int32, (8, 128), 0)
+    by_peer = jnp.where(lax.shift_right_logical(slot, 3) == peer, material, 0.0)
+    heat_rows = dot(by_peer.astype(bf16), fan)
     state_load.wait()
     low = lane_low((8, 128))
     flat = state_ref[...].reshape(48, 512)
@@ -207,42 +214,38 @@
             rows.append(jnp.where(low, swap(first), second))
     faces = jnp.concatenate(rows, axis=0)
     face_ref[...] = faces
-    hi, lo = split2(faces)
-    table = dot(jnp.concatenate([hi, lo], axis=0), orient_ref[...]).astype(bf16)
-    columns = []
-    for part in range(6):
-        block = table[48 * part : 48 * part + 48]
-        columns.append(jnp.concatenate([block[:, 128 * o : 128 * o + 128] for o in range(8)], axis=0))
-    gathered = dot(one_hot, jnp.concatenate(columns, axis=1))
+    gathered = dot(one_hot, stacked(jnp.concatenate([faces[48 * j : 48 * j + 48] for j in range(3)], axis=1)))
+    x = [reorder(gathered[:, 128 * j : 128 * j + 128], source) for j in range(3)]
+    x = jnp.concatenate([x[j][at : at + 64] for at in (0, 64) for j in range(3)], axis=0)
     proj_load.wait()
     b_hi, b_lo = split2(jnp.concatenate(project_blocks(proj_ref), axis=0))
-    b_twice = jnp.concatenate([b_hi, b_hi], axis=1)
-
-    def project(at):
-        q = slice(at, at + 64)
-        x_hi = jnp.concatenate([gathered[q, 128 * j : 128 * j + 128] for j in range(3)], axis=0)
-        x_lo = jnp.concatenate([gathered[q, 384 + 128 * j : 512 + 128 * j] for j in range(3)], axis=0)
-        h = x_hi.astype(bf16)
-        wide = dot(jnp.concatenate([h, x_lo.astype(bf16)], axis=1), b_twice, 1, 1) + dot(h, b_lo, 1, 1)
-        for j in range(3):
-            r = slice(64 * j, 64 * j + 64)
-            w = x_hi[r] + x_lo[r]
-            for s in range(4):
-                w = jnp.where(sub_of[q] == s + 1, wide[r, 128 * s : 128 * s + 128], w)
-            yield slice(128 * j, 128 * j + 128), w
-        yield slice(384, 512), heat[q]
-
-    stores = []
-    for n, (lanes, w) in enumerate(project(0)):
+    hi, lo = split2(x)
+    wide = dot(jnp.concatenate([hi, lo], axis=1), jnp.concatenate([b_hi, b_hi], axis=1), 1, 1) + dot(hi, b_lo, 1, 1)
+
+    def projected(j, at):
+        r = slice(64 * j + 3 * at, 64 * j + 3 * at + 64)
+        w = x[r]
+        for n in range(4):
+            w = jnp.where(sub_of[at : at + 64] == n + 1, wide[r, 128 * n : 128 * n + 128], w)
+        return w
+
+    for j in range(3):
+        w = projected(j, 0)
         for g in range(8):
-            mine_ref[g, :, lanes] = w[8 * g : 8 * g + 8]
-        stores.append(pltpu.make_async_copy(mine_ref.at[:, :, lanes], grp_hbm.at[:, :, lanes], out_sem.at[n]))
-        stores[-1].start()
-    for lanes, w in project(64):
-        even_ref[:, lanes] = w[0:32]
-        odd_ref[:, lanes] = w[32:64]
-    for store in stores:
-        store.wait()
+            part = w[8 * g : 8 * g + 8]
+            mine_ref[g, :, 128 * j : 128 * j + 128] = part
+            pack_ref[ROWS * g + 8 * j : ROWS * g + 8 * j + 8, :] = part
+    for g in range(8):
+        pack_ref[ROWS * g + 24 : ROWS * g + 25, :] = heat_rows[g : g + 1]
+    store = pltpu.make_async_copy(pack_ref, grp_hbm, out_sem.at[0])
+    store.start()
+    for j in range(3):
+        w = projected(j, 64)
+        even_ref[:, 128 * j : 128 * j + 128] = w[0:32]
+        odd_ref[:, 128 * j : 128 * j + 128] = w[32:64]
+    even_ref[:, 384:512] = heat[64:96]
+    odd_ref[:, 384:512] = heat[96:128]
+    store.wait()
 
 
 def primitives(u, g, n):
@@ -290,7 +293,7 @@
 
 def local_kernel(
     state_ref, mat_ref, metric_ref, count_ref, near_ref, face_ref, deriv_ref, info_ref, proj_ref, code_ref,
-    mine_ref, even_ref, odd_ref, base_ref, local_ref, sub_ref, own_ref, scale_ref, hot_ref, back_ref,
+    mine_ref, even_ref, odd_ref, base_ref, local_ref, sub_ref, own_ref, scale_ref, hot_ref, back_ref, turn_ref,
 ):
     info = info_ref[...]
     element, face, sub, orient = (info[i : i + 1] for i in range(4))
@@ -306,14 +309,16 @@
     sign = jnp.where(jnp.bitwise_and(face, 1) == 1, 1.0, -1.0)
     axis = lax.shift_right_logical(face, 1)
     codes = code_rows(
-        [sub.astype(f32), alive] + [jnp.where(axis == d, sign, 0.0) for d in range(3)]
+        [sub.astype(f32), alive]
+        + [jnp.where(axis == d, sign, 0.0) for d in range(3)]
+        + [orient.astype(f32), slot_material(mat_ref, element)]
     )
     spread = dot(codes, code_ref[...], 0, 0)
     sub_ref[...] = spread[:, 0:128]
-    index = 48 * orient + 8 * face + element
-    row = lax.broadcasted_iota(jnp.int32, (384, SLOTS), 0)
+    turn_ref[...] = lane_sources(spread[:, 640:768].astype(jnp.int32), True)
+    row = lax.broadcasted_iota(jnp.int32, (48, SLOTS), 0)
     beta = jnp.where(sub == 0, 1.0, 0.25)
-    hot = jnp.where(row == index, beta, 0.0).astype(bf16)
+    hot = jnp.where(row == 8 * face + element, beta, 0.0).astype(bf16)
     hot_ref[:, 0:128] = hot
     hot_ref[:, 128:256] = hot
     b_hi, b_lo = split2(jnp.concatenate(project_blocks(proj_ref), axis=1))
@@ -366,12 +371,7 @@
     hot = jnp.concatenate(hot, axis=0).astype(bf16)
     heat_rows = jnp.concatenate([heat[:, 0:128]] * 6, axis=0)
     table = jnp.concatenate([faces[0:48], faces[48:96], faces[96:144], heat_rows], axis=1)
-    gap = jnp.zeros((16, 512), bf16)
-    terms = []
-    for term in split3(table):
-        terms += [term, gap]
-    terms.append(jnp.zeros((64, 512), bf16))
-    theirs = dot(hot, jnp.concatenate(terms, axis=0))
+    theirs = dot(hot, stacked(table))
     low = lane_low((48, 128))
     row = lax.broadcasted_iota(jnp.int32, (48, 128), 0)
     sign = jnp.where(jnp.bitwise_and(row, 8) != 0, 1.0, -1.0)
@@ -403,7 +403,8 @@
     states = []
     for j in range(3):
         states += two_halves(low, *rows(128 * j))
-    g = jnp.where(low, *rows(384))
+    heat = 1.4 + 0.27 * spread[:, 768:896]
+    g = jnp.where(low, heat[0:64], heat[64:128])
     slots = [
         jnp.where(low, spread[0:64, 128 * n : 128 * n + 128], spread[64:128, 128 * n : 128 * n + 128])
         for n in range(1, 5)
@@ -416,26 +417,33 @@
 
 
 def mortar_kernel(
-    from_grp_ref, from_even_ref, from_late_ref, from_odd_ref, sel_ref, orient_ref,
-    base_ref, local_ref, sub_ref, own_ref, scale_ref, hot_ref, back_ref, out_hbm, new_ref, sem,
+    from_grp_ref, from_even_ref, from_late_ref, from_odd_ref, sel_ref,
+    base_ref, local_ref, sub_ref, own_ref, scale_ref, hot_ref, back_ref, turn_ref, out_hbm, new_ref, sem,
 ):
     chunk = 16
     low = lane_low((chunk, 128))
     first, second = [[], [], []], [[], [], []]
+    spread = jnp.concatenate(
+        [jnp.broadcast_to(from_grp_ref[ROWS * n + 24 : ROWS * n + 25, :], (8, 128)) for n in range(8)], axis=0
+    )
+    row = lax.broadcasted_iota(jnp.int32, (64, 128), 0)
+    lane = lax.broadcasted_iota(jnp.int32, (64, 128), 1)
+    spread = jnp.where(lane == 16 * jnp.bitwise_and(row, 7), spread, 0.0).astype(bf16)
+    grp_heat = 1.4 + 0.27 * dot(spread, jnp.ones((128, 128), bf16))
     for at in range(0, 64, chunk):
         r = slice(at, at + chunk)
 
-        def rows(lane):
-            lanes = slice(lane, lane + 128)
-            grp = jnp.concatenate([from_grp_ref[at // 8 + n, :, lanes] for n in range(chunk // 8)], axis=0)
+        def from_elem(lanes):
             if at < 32:
-                return grp, from_even_ref[r, lanes] + from_late_ref[r, lanes]
-            return grp, from_odd_ref[at - 32 : at - 32 + chunk, lanes]
+                return from_even_ref[r, lanes] + from_late_ref[r, lanes]
+            return from_odd_ref[at - 32 : at - 32 + chunk, lanes]
 
         theirs = []
         for j in range(3):
-            theirs += two_halves(low, *rows(128 * j))
-        g = jnp.where(low, *rows(384))
+            starts = [ROWS * (at // 8 + n) + 8 * j for n in range(chunk // 8)]
+            grp = jnp.concatenate([from_grp_ref[x : x + 8, :] for x in starts], axis=0)
+            theirs += two_halves(low, grp, from_elem(slice(128 * j, 128 * j + 128)))
+        g = jnp.where(low, grp_heat[r], from_elem(slice(384, 512)))
         mine = [own_ref[n, r] for n in range(6)]
         normal = [own_ref[n, r] for n in range(16, 19)]
         live = own_ref[15, r] > 0.5
@@ -450,22 +458,17 @@
     hi, lo = split2(corr)
     wide = dot(jnp.concatenate([hi, lo, hi], axis=1), back_ref[...])
     sub_of = sub_ref[...].astype(jnp.int32)
+    turn = turn_ref[...]
     back = []
     for j in range(3):
         r = slice(128 * j, 128 * j + 128)
         y = corr[r]
         for s in range(4):
             y = jnp.where(sub_of == s + 1, wide[r, 128 * s : 128 * s + 128], y)
-        back.append(y)
+        back.append(reorder(y, turn))
     hi, lo = split2(jnp.concatenate(back, axis=1))
     summed = dot(hot_ref[...], jnp.concatenate([hi, lo], axis=0))
-    rows = []
-    for j in range(3):
-        lanes = slice(128 * j, 128 * j + 128)
-        rows.append(jnp.concatenate([summed[48 * o : 48 * o + 48, lanes] for o in range(8)], axis=1))
-    hi, lo = split2(jnp.concatenate(rows, axis=0))
-    turned = dot(jnp.concatenate([hi, lo], axis=0), orient_ref[...], 1, 1)
-    total = turned[0:144] + turned[144:288] + local_ref[...]
+    total = jnp.concatenate([summed[:, 128 * j : 128 * j + 128] for j in range(3)], axis=0) + local_ref[...]
     low = lane_low((8, 128))
     lift = []
     for v in range(6):
@@ -531,22 +534,21 @@
     info = mortar_map[0]
     counts = mortar_count[0]
     select = jnp.asarray(face_select(), bf16)
-    orients = jnp.asarray(orient_table(), bf16)
     deriv = deriv_table()
     d_hi = deriv.astype(bf16)
     d_lo = (deriv - d_hi.astype(np.float32)).astype(bf16)
     derivs = jnp.asarray(np.concatenate([d_hi, d_lo], axis=1))
-    codes_c = jnp.asarray(code_table([{n: 1} for n in range(5)]), bf16)
+    codes_c = jnp.asarray(code_table([{n: 1} for n in range(7)]), bf16)
 
     far = pl.BlockSpec(memory_space=pl.ANY)
     grp, even, odd, faces, mine, kept = pl.pallas_call(
         trace_kernel,
         out_shape=[
-            jax.ShapeDtypeStruct((groups, CAPG, 512), f32),
+            jax.ShapeDtypeStruct((groups * ROWS, 128), f32),
             pltpu.VMEM((CAPS, 512), f32),
             pltpu.VMEM((CAPS, 512), f32),
             pltpu.VMEM((144, 128), f32),
-            pltpu.VMEM((groups, CAPG, 512), f32),
+            pltpu.VMEM((groups, CAPG, 384), f32),
             pltpu.VMEM((8, SLOTS), jnp.int32),
         ],
         in_specs=[far] * 4,
@@ -557,9 +559,9 @@
             pltpu.VMEM((4, SLOTS), jnp.int32),
             pltpu.VMEM((4, 64, 64), f32),
             pltpu.VMEM((512, 256), bf16),
-            pltpu.VMEM((128, 1024), bf16),
+            pltpu.VMEM((groups * ROWS, 128), f32),
             pltpu.SemaphoreType.DMA((4,)),
-            pltpu.SemaphoreType.DMA((4,)),
+            pltpu.SemaphoreType.DMA((1,)),
         ],
         name="traces",
         compiler_params=pltpu.CompilerParams(vmem_limit_bytes=16 << 20),
@@ -571,14 +573,15 @@
     late = [(0, groups), (groups, 0)]
     axes = ("elem", "grp")
     from_even = lax.ppermute(even, axes, [pair for pair in swaps[0] if pair not in late])
-    arrived = lax.all_to_all(grp, "grp", split_axis=0, concat_axis=0, tiled=True)
+    blocks = grp.reshape(groups, ROWS, 1, 128)
+    arrived = lax.all_to_all(blocks, "grp", split_axis=0, concat_axis=0, tiled=True).reshape(groups * ROWS, 128)
     from_odd = lax.ppermute(odd, axes, swaps[1])
     from_late = lax.ppermute(even, axes, late)
     held = call(
         local_kernel,
         [
             (6, 8, 512), (144, 128), (SLOTS, 128), (19, 64, 128), (8, 128),
-            ((384, 256), bf16), ((384, 512), bf16),
+            ((48, 256), bf16), ((384, 512), bf16), ((SLOTS, 128), jnp.int32),
         ],
         {1, 2, 3},
         (
@@ -586,7 +589,7 @@
             mine, even, odd,
         ),
     )
-    operands = (arrived, from_even, from_late, from_odd, select, orients, *held)
+    operands = (arrived, from_even, from_late, from_odd, select, *held)
     new = pl.pallas_call(
         mortar_kernel,
         out_shape=jax.ShapeDtypeStruct((6, 8, 512), f32),

time: 31 us -> 30.7 us (level)
  Pallas kernels: 6.03 us -> 5.7 us
    unnamed x20 -> x18, local copies, waits for them, and re-layouts: 0.65 us -> 0.65 us
where the time goes in v6:
time: 30.7 us; the launch traced here: 30.4 us
  starting transfers between devices  21.5 us (70%)
  Pallas kernels  5.7 us (19%)
  waiting for transfers between devices  2.36 us (8%)
  local copies, waits for them, and re-layouts  0.65 us (2%)
    ppermute x1, starting transfers between devices, section(): lax.ppermute(even, axes, [pair for pair in swaps[0] if pair not in late])  13.9 us
    all_to_all x1, starting transfers between devices, section(): lax.all_to_all(blocks, 'grp', split_axis=0, concat_axis=0, tiled=True)  5.06 us
    pallas_call x1, Pallas kernels, section(): pl.pallas_call(trace_kernel, out_shape=[jax.ShapeDtypeStruct((groups * RO...  2.8 us
    ppermute x1, waiting for transfers between devices, section(): from_odd = lax.ppermute(odd, axes, swaps[1])  2.35 us
    ppermute x1, starting transfers between devices, section(): from_odd = lax.ppermute(odd, axes, swaps[1])  1.92 us
    pallas_call x1, Pallas kernels, section(): pl.pallas_call(mortar_kernel, out_shape=jax.ShapeDtypeStruct((6, 8, 512),...  1.74 us
    pallas_call x1, Pallas kernels, call(): pl.pallas_call(kernel, out_shape=[jax.ShapeDtypeStruct(*s) if n in free e...  1.16 us
    ppermute x1, starting transfers between devices, section(): from_late = lax.ppermute(even, axes, late)  0.66 us
  transfers between devices with their start and end apart: 4, of which 1 were waited for; matrix products, arithmetic and copies ran while one was open for 0% of the time, Pallas kernels for 4%

profile of v6, /device:TPU:10, one launch (start us, length us, event | category | flops | bytes accessed | tf_op | source)
XLA Modules:
  0.0 30.4 jit_solution(17368278925569979607)
XLA Ops:
  0.0 0.0 copy-start.1
  0.0 0.0 copy-start.3
  0.0 2.8 %traces.1 = (f32[200,128]{1,0:T(8,128)}, f32[32,512]{1,0:T(8,128)S(1)}, f32[32,512]{1,0:T(8,128)S(1)}, f32[144,128]{1,0:T(8,128)S(1)}, f32[8,8,384]{2,1,0:T(8,128)S(1)}, /*index=5*/s32[8,128]{1,0:T(8,128)S(1)}) custom-call(f32[6,8,512]{2,1,0:T(8,128)} %bitcast.7, s32[8]{0:T(128)} %mat_ref.1, s32[4,128]{1,0:T(4,128)} %bitcast.10, f32[4,64,64]{2,1,0:T(8,128)} %proj_ref.1), custom_call_target="tpu_custom_call" | custom-call | tf_op jit(solution)/shard_map/traces/pallas_call | solution.py:544
  2.8 0.0 copy-start
  2.8 0.0 copy-start.4
  2.8 5.1 %all-to-all-start = ((f32[8,25,1,128]{3,2,1,0:T(1,128)}), f32[8,25,1,128]{3,2,1,0:T(1,128)S(1)}, u32[]{:S(2)}, u32[]{:S(2)}) async-start(f32[8,25,1,128]{3,2,1,0:T(1,128)} %bitcast.2), calls=%async_computation | async-start | bytes 204800 | tf_op jit(solution)/shard_map/all_to_all | solution.py:577
  7.9 13.9 %collective-permute-start = (f32[32,512]{1,0:T(8,128)S(1)}, f32[32,512]{1,0:T(8,128)S(1)}, u32[]{:S(2)}, u32[]{:S(2)}) collective-permute-start(f32[32,512]{1,0:T(8,128)S(1)} %get-tuple-element.20.even_ref), channel_id=1, source_target_pairs={{1,9},{9,1},{2,10},{10,2},{3,11},{11,3},{4,12},{12,4},{5,13},{13,5... | collective-permute-start | bytes 196616 | tf_op jit(solution)/shard_map/ppermute | solution.py:575
  21.8 0.7 %collective-permute-start.1 = (f32[32,512]{1,0:T(8,128)S(1)}, f32[32,512]{1,0:T(8,128)S(1)}, u32[]{:S(2)}, u32[]{:S(2)}) collective-permute-start(f32[32,512]{1,0:T(8,128)S(1)} %get-tuple-element.20.even_ref), channel_id=1, source_target_pairs={{0,8},{8,0}} | collective-permute-start | bytes 196616 | tf_op jit(solution)/shard_map/ppermute | solution.py:579
  22.4 0.0 copy-start.5
  22.5 1.9 %collective-permute-start.2 = (f32[32,512]{1,0:T(8,128)S(1)}, f32[32,512]{1,0:T(8,128)S(1)}, u32[]{:S(2)}, u32[]{:S(2)}) collective-permute-start(f32[32,512]{1,0:T(8,128)S(1)} %get-tuple-element.21.odd_ref), channel_id=1, source_target_pairs={{8,16},{16,8},{9,17},{17,9},{10,18},{18,10},{11,19},{19,11},{12,20... | collective-permute-start | bytes 196616 | tf_op jit(solution)/shard_map/ppermute | solution.py:578
  24.4 0.0 copy-start.6
  24.4 0.0 copy-start.7
  24.4 0.0 copy-start.8
  24.4 0.0 copy-done.1
  24.4 0.0 copy-done.3
  24.4 0.0 copy-done
  24.4 0.0 copy-done.4
  24.5 0.0 copy-done.5
  24.5 0.6 %copy-done.6 = s32[8]{0:T(128)S(1)} copy-done((s32[8]{0:T(128)S(1)}, s32[8]{0:T(128)}, u32[]{:S(2)}) %copy-start.6) | copy-done | bytes 56
  25.0 0.0 copy-done.7
  25.1 0.0 copy-done.8
  25.1 0.0 copy-start.2
  25.1 1.2 %shard_map.100 = (f32[6,8,512]{2,1,0:T(8,128)S(1)}, f32[144,128]{1,0:T(8,128)S(1)}, f32[128,128]{1,0:T(8,128)S(1)}, f32[19,64,128]{2,1,0:T(8,128)S(1)}, f32[8,12...) custom-call(f32[6,8,512]{2,1,0:T(8,128)S(1)} %bitcast.8, ...), custom_call_target="tpu_custom_call" | custom-call | tf_op jit(solution)/shard_map/pallas_call | solution.py:521
  26.2 0.0 collective-permute-done.from_even_ref
  26.2 0.0 collective-permute-done.1.from_late_ref
  26.3 2.3 %collective-permute-done.2.from_odd_ref = f32[32,512]{1,0:T(8,128)S(1)} collective-permute-done((f32[32,512]{1,0:T(8,128)S(1)}, f32[32,512]{1,0:T(8,128)S(1)}, u32[]{:S(2)}, u32[]{:S(2)}) %collective-permute-start.2) | collective-permute-done | bytes 65568 | tf_op jit(solution)/shard_map/ppermute | solution.py:578
  28.6 0.0 all-to-all-done
  28.6 0.0 copy-done.2
  28.6 1.7 %mortar.1 = f32[6,8,512]{2,1,0:T(8,128)} custom-call(f32[200,128]{1,0:T(8,128)S(1)} %bitcast.6, f32[32,512]{1,0:T(8,128)S(1)} %collective-permute-done.from_even_ref, f32[32,512]{1,0:T(8,128)S(1)} %collective-permute-done.1.from_late_ref, f32[32,512]{1,0:T(8,128)S(1)} %collective-permute-done.2.from_odd_ref, bf16[512,256]{1,0:T(8,128)(2,1)S(1)} %copy-done.2, ...), custom_call_target="tpu_custom_call" | custom-call | tf_op jit(solution)/shard_map/mortar/pallas_call | solution.py:593
Async XLA Ops:
  0.0 24.4 %copy-start.1 = (f32[8,6,512]{2,0,1:T(8,128)S(1)}, f32[8,6,512]{2,0,1:T(8,128)}, u32[]{:S(2)}) copy-start(f32[8,6,512]{2,0,1:T(8,128)} %param.10) | copy-start | bytes 294916
  0.0 24.4 %copy-start.3 = (bf16[256,256]{1,0:T(8,128)(2,1)S(1)}, bf16[256,256]{1,0:T(8,128)(2,1)}, u32[]{:S(2)}) copy-start(bf16[256,256]{1,0:T(8,128)(2,1)} %constant.7.clone.deriv_ref) | copy-start | bytes 393220
  2.8 21.6 %copy-start = (f32[4,64,64]{2,1,0:T(8,128)S(1)}, f32[4,64,64]{2,1,0:T(8,128)}, u32[]{:S(2)}) copy-start(f32[4,64,64]{2,1,0:T(8,128)} %proj_ref.1) | copy-start | bytes 196612
  2.8 21.6 %copy-start.4 = (bf16[16,896]{1,0:T(8,128)(2,1)S(1)}, bf16[16,896]{1,0:T(8,128)(2,1)}, u32[]{:S(2)}) copy-start(bf16[16,896]{1,0:T(8,128)(2,1)} %constant.8.clone.code_ref) | copy-start | bytes 86020
  2.8 25.8 %all-to-all-start = ((f32[8,25,1,128]{3,2,1,0:T(1,128)}), f32[8,25,1,128]{3,2,1,0:T(1,128)S(1)}, u32[]{:S(2)}, u32[]{:S(2)}) async-start(f32[8,25,1,128]{3,2,1,0:T(1,128)} %bitcast.2), calls=%async_computation | async-start | bytes 204800 | tf_op jit(solution)/shard_map/all_to_all | solution.py:577
  7.9 18.3 %collective-permute-start = (f32[32,512]{1,0:T(8,128)S(1)}, f32[32,512]{1,0:T(8,128)S(1)}, u32[]{:S(2)}, u32[]{:S(2)}) collective-permute-start(f32[32,512]{1,0:T(8,128)S(1)} %get-tuple-element.20.even_ref), channel_id=1, source_target_pairs={{1,9},{9,1},{2,10},{10,2},{3,11},{11,3},{4,12},{12,4},{5,13},{13,5... | collective-permute-start | bytes 196616 | tf_op jit(solution)/shard_map/ppermute | solution.py:575
  21.8 4.5 %collective-permute-start.1 = (f32[32,512]{1,0:T(8,128)S(1)}, f32[32,512]{1,0:T(8,128)S(1)}, u32[]{:S(2)}, u32[]{:S(2)}) collective-permute-start(f32[32,512]{1,0:T(8,128)S(1)} %get-tuple-element.20.even_ref), channel_id=1, source_target_pairs={{0,8},{8,0}} | collective-permute-start | bytes 196616 | tf_op jit(solution)/shard_map/ppermute | solution.py:579
  22.4 2.0 %copy-start.5 = (s32[8,6]{1,0:T(8,128)S(1)}, s32[8,6]{1,0:T(8,128)}, u32[]{:S(2)}) copy-start(s32[8,6]{1,0:T(8,128)} %near_ref.1) | copy-start | bytes 580
  22.5 6.2 %collective-permute-start.2 = (f32[32,512]{1,0:T(8,128)S(1)}, f32[32,512]{1,0:T(8,128)S(1)}, u32[]{:S(2)}, u32[]{:S(2)}) collective-permute-start(f32[32,512]{1,0:T(8,128)S(1)} %get-tuple-element.21.odd_ref), channel_id=1, source_target_pairs={{8,16},{16,8},{9,17},{17,9},{10,18},{18,10},{11,19},{19,11},{12,20... | collective-permute-start | bytes 196616 | tf_op jit(solution)/shard_map/ppermute | solution.py:578
  24.4 0.7 %copy-start.6 = (s32[8]{0:T(128)S(1)}, s32[8]{0:T(128)}, u32[]{:S(2)}) copy-start(s32[8]{0:T(128)} %mat_ref.1) | copy-start | bytes 100
  24.4 0.7 %copy-start.7 = (f32[8]{0:T(128)S(1)}, f32[8]{0:T(128)}, u32[]{:S(2)}) copy-start(f32[8]{0:T(128)} %metric_ref.1) | copy-start | bytes 100
  24.4 0.7 %copy-start.8 = (s32[1,10]{1,0:T(1,128)S(1)}, s32[1,10]{1,0:T(1,128)}, u32[]{:S(2)}) copy-start(s32[1,10]{1,0:T(1,128)} %param.15) | copy-start | bytes 124
  25.1 3.5 %copy-start.2 = (bf16[512,256]{1,0:T(8,128)(2,1)S(1)}, bf16[512,256]{1,0:T(8,128)(2,1)}, u32[]{:S(2)}) copy-start(bf16[512,256]{1,0:T(8,128)(2,1)} %constant.6.clone.sel_ref) | copy-start | bytes 786436

commit v7 on v6

--- a/solution.py
+++ b/solution.py
@@ -111,12 +111,12 @@
 
 
 def selection():
-    lane = lax.broadcasted_iota(jnp.int32, (1, 256), 1)
-    far = jnp.bitwise_and(lax.shift_right_logical(lane, 6), 1)
+    lane = lax.broadcasted_iota(jnp.int32, (1, 512), 1)
+    far = jnp.bitwise_and(lax.shift_right_logical(lane, 7), 1)
     p = jnp.bitwise_and(lax.shift_right_logical(lane, 3), 7)
     r = jnp.bitwise_and(lane, 7)
-    node = 64 * p + jnp.where(lane < 128, r + 56 * far, 8 * r + 7 * far)
-    row = lax.broadcasted_iota(jnp.int32, (512, 256), 0)
+    node = 64 * p + jnp.where(lane < 256, r + 56 * far, 8 * r + 7 * far)
+    row = lax.broadcasted_iota(jnp.int32, (512, 512), 0)
     return jnp.where(row == node, 1.0, 0.0).astype(bf16)
 
 
@@ -170,6 +170,8 @@
     fan = jnp.where(jnp.bitwise_and(place, 7) == lax.shift_right_logical(lane, 4), 1.0, 0.0).astype(bf16)
     map_load.wait()
     mat_load.wait()
+    state_load.wait()
+    proj_load.wait()
     info = jnp.concatenate([map_ref[...]] * 2, axis=0)
     slot = lax.broadcasted_iota(jnp.int32, (8, SLOTS), 1)
     turned = jnp.where(slot < 96, pltpu.roll(info, 96, 1), pltpu.roll(info, 32, 1))
@@ -191,33 +193,23 @@
     peer = lax.broadcasted_iota(jnp.int32, (8, 128), 0)
     by_peer = jnp.where(lax.shift_right_logical(slot, 3) == peer, material, 0.0)
     heat_rows = dot(by_peer.astype(bf16), fan)
-    state_load.wait()
     low = lane_low((8, 128))
     flat = state_ref[...].reshape(48, 512)
     picked = dot(jnp.concatenate(split3(flat), axis=0), sel_ref[...])
     picked = picked[0:48] + picked[48:96] + picked[96:144]
-    pairs = []
-    for v in range(6):
-        x = state_ref[v]
-        pairs.append(
-            [
-                jnp.where(low, x[:, 0:128], x[:, 384:512]),
-                picked[8 * v : 8 * v + 8, 0:128],
-                picked[8 * v : 8 * v + 8, 128:256],
-            ]
-        )
     rows = []
     for j in range(3):
-        for d in range(3):
-            first, second = pairs[2 * j][d], pairs[2 * j + 1][d]
-            rows.append(jnp.where(low, first, swap(second)))
-            rows.append(jnp.where(low, swap(first), second))
+        x, y = state_ref[2 * j], state_ref[2 * j + 1]
+        rows.append(jnp.where(low, x[:, 0:128], swap(y[:, 0:128])))
+        rows.append(jnp.where(low, swap(x[:, 384:512]), y[:, 384:512]))
+        for k in range(4):
+            lanes = slice(128 * k, 128 * k + 128)
+            rows.append(jnp.where(low, picked[16 * j : 16 * j + 8, lanes], picked[16 * j + 8 : 16 * j + 16, lanes]))
     faces = jnp.concatenate(rows, axis=0)
     face_ref[...] = faces
     gathered = dot(one_hot, stacked(jnp.concatenate([faces[48 * j : 48 * j + 48] for j in range(3)], axis=1)))
     x = [reorder(gathered[:, 128 * j : 128 * j + 128], source) for j in range(3)]
     x = jnp.concatenate([x[j][at : at + 64] for at in (0, 64) for j in range(3)], axis=0)
-    proj_load.wait()
     b_hi, b_lo = split2(jnp.concatenate(project_blocks(proj_ref), axis=0))
     hi, lo = split2(x)
     wide = dot(jnp.concatenate([hi, lo], axis=1), jnp.concatenate([b_hi, b_hi], axis=1), 1, 1) + dot(hi, b_lo, 1, 1)
@@ -527,21 +519,9 @@
     )(*held)
 
 
-def section(state, material, metric, mortar_proj, mortar_map, mortar_count, neighbours):
-    groups = lax.axis_size("grp")
-    n_elem = lax.axis_size("elem")
-    elements = jnp.transpose(state, (1, 0, 2))
-    info = mortar_map[0]
-    counts = mortar_count[0]
-    select = jnp.asarray(face_select(), bf16)
-    deriv = deriv_table()
-    d_hi = deriv.astype(bf16)
-    d_lo = (deriv - d_hi.astype(np.float32)).astype(bf16)
-    derivs = jnp.asarray(np.concatenate([d_hi, d_lo], axis=1))
-    codes_c = jnp.asarray(code_table([{n: 1} for n in range(7)]), bf16)
-
+def traces(groups, elements, material, info, mortar_proj):
     far = pl.BlockSpec(memory_space=pl.ANY)
-    grp, even, odd, faces, mine, kept = pl.pallas_call(
+    return pl.pallas_call(
         trace_kernel,
         out_shape=[
             jax.ShapeDtypeStruct((groups * ROWS, 128), f32),
@@ -558,7 +538,7 @@
             pltpu.SMEM((8,), jnp.int32),
             pltpu.VMEM((4, SLOTS), jnp.int32),
             pltpu.VMEM((4, 64, 64), f32),
-            pltpu.VMEM((512, 256), bf16),
+            pltpu.VMEM((512, 512), bf16),
             pltpu.VMEM((groups * ROWS, 128), f32),
             pltpu.SemaphoreType.DMA((4,)),
             pltpu.SemaphoreType.DMA((1,)),
@@ -566,6 +546,22 @@
         name="traces",
         compiler_params=pltpu.CompilerParams(vmem_limit_bytes=16 << 20),
     )(*(pltpu.with_memory_space_constraint(a, pltpu.HBM) for a in (elements, material, info, mortar_proj)))
+
+
+def section(state, material, metric, mortar_proj, mortar_map, mortar_count, neighbours):
+    groups = lax.axis_size("grp")
+    n_elem = lax.axis_size("elem")
+    elements = jnp.transpose(state, (1, 0, 2))
+    info = mortar_map[0]
+    counts = mortar_count[0]
+    select = jnp.asarray(face_select(), bf16)
+    deriv = deriv_table()
+    d_hi = deriv.astype(bf16)
+    d_lo = (deriv - d_hi.astype(np.float32)).astype(bf16)
+    derivs = jnp.asarray(np.concatenate([d_hi, d_lo], axis=1))
+    codes_c = jnp.asarray(code_table([{n: 1} for n in range(7)]), bf16)
+
+    grp, even, odd, faces, mine, kept = traces(groups, elements, material, info, mortar_proj)
     swaps = [
         [((i + n) * groups + g, (i + 1 - n) * groups + g) for i in range(first, n_elem - 1, 2) for g in range(groups) for n in range(2)]
         for first in range(2)
@@ -594,7 +590,7 @@
         mortar_kernel,
         out_shape=jax.ShapeDtypeStruct((6, 8, 512), f32),
         in_specs=[VM] * len(operands),
-        out_specs=far,
+        out_specs=pl.BlockSpec(memory_space=pl.ANY),
         scratch_shapes=[pltpu.VMEM((6, 8, 512), f32), pltpu.SemaphoreType.DMA((3,))],
         name="mortar",
         compiler_params=pltpu.CompilerParams(vmem_limit_bytes=16 << 20),

time: 30.7 us -> 30.5 us (level)
  no operation moved by 1% of the time
where the time goes in v7:
time: 30.5 us; the launch traced here: 30.2 us
  starting transfers between devices  21.5 us (70%)
  Pallas kernels  5.54 us (18%)
  waiting for transfers between devices  2.35 us (8%)
  local copies, waits for them, and re-layouts  0.65 us (2%)
    ppermute x1, starting transfers between devices, section(): lax.ppermute(even, axes, [pair for pair in swaps[0] if pair not in late])  13.9 us
    all_to_all x1, starting transfers between devices, section(): lax.all_to_all(blocks, 'grp', split_axis=0, concat_axis=0, tiled=True)  5.06 us
    pallas_call x1, Pallas kernels, traces(): pl.pallas_call(trace_kernel, out_shape=[jax.ShapeDtypeStruct((groups * RO...  2.63 us
    ppermute x1, waiting for transfers between devices, section(): from_odd = lax.ppermute(odd, axes, swaps[1])  2.35 us
    ppermute x1, starting transfers between devices, section(): from_odd = lax.ppermute(odd, axes, swaps[1])  1.92 us
    pallas_call x1, Pallas kernels, section(): pl.pallas_call(mortar_kernel, out_shape=jax.ShapeDtypeStruct((6, 8, 512),...  1.74 us
    pallas_call x1, Pallas kernels, call(): pl.pallas_call(kernel, out_shape=[jax.ShapeDtypeStruct(*s) if n in free e...  1.17 us
    ppermute x1, starting transfers between devices, section(): from_late = lax.ppermute(even, axes, late)  0.66 us
  transfers between devices with their start and end apart: 4, of which 1 were waited for; matrix products, arithmetic and copies ran while one was open for 0% of the time, Pallas kernels for 4%

profile of v7, /device:TPU:10, one launch (start us, length us, event | category | flops | bytes accessed | tf_op | source)
XLA Modules:
  0.0 30.2 jit_solution(13433794986464505738)
XLA Ops:
  0.0 0.0 copy-start.1
  0.0 0.0 copy-start.3
  0.0 2.6 %traces.1 = (f32[200,128]{1,0:T(8,128)}, f32[32,512]{1,0:T(8,128)S(1)}, f32[32,512]{1,0:T(8,128)S(1)}, f32[144,128]{1,0:T(8,128)S(1)}, f32[8,8,384]{2,1,0:T(8,128)S(1)}, /*index=5*/s32[8,128]{1,0:T(8,128)S(1)}) custom-call(f32[6,8,512]{2,1,0:T(8,128)} %bitcast.7, s32[8]{0:T(128)} %mat_ref.1, s32[4,128]{1,0:T(4,128)} %bitcast.10, f32[4,64,64]{2,1,0:T(8,128)} %proj_ref.1), custom_call_target="tpu_custom_call" | custom-call | tf_op jit(solution)/shard_map/traces/pallas_call | solution.py:524
  2.6 0.0 copy-start
  2.7 0.0 copy-start.4
  2.7 5.1 %all-to-all-start = ((f32[8,25,1,128]{3,2,1,0:T(1,128)}), f32[8,25,1,128]{3,2,1,0:T(1,128)S(1)}, u32[]{:S(2)}, u32[]{:S(2)}) async-start(f32[8,25,1,128]{3,2,1,0:T(1,128)} %bitcast.2), calls=%async_computation | async-start | bytes 204800 | tf_op jit(solution)/shard_map/all_to_all | solution.py:573
  7.7 13.9 %collective-permute-start = (f32[32,512]{1,0:T(8,128)S(1)}, f32[32,512]{1,0:T(8,128)S(1)}, u32[]{:S(2)}, u32[]{:S(2)}) collective-permute-start(f32[32,512]{1,0:T(8,128)S(1)} %get-tuple-element.20.even_ref), channel_id=1, source_target_pairs={{1,9},{9,1},{2,10},{10,2},{3,11},{11,3},{4,12},{12,4},{5,13},{13,5... | collective-permute-start | bytes 196616 | tf_op jit(solution)/shard_map/ppermute | solution.py:571
  21.6 0.7 %collective-permute-start.1 = (f32[32,512]{1,0:T(8,128)S(1)}, f32[32,512]{1,0:T(8,128)S(1)}, u32[]{:S(2)}, u32[]{:S(2)}) collective-permute-start(f32[32,512]{1,0:T(8,128)S(1)} %get-tuple-element.20.even_ref), channel_id=1, source_target_pairs={{0,8},{8,0}} | collective-permute-start | bytes 196616 | tf_op jit(solution)/shard_map/ppermute | solution.py:575
  22.3 0.0 copy-start.5
  22.3 1.9 %collective-permute-start.2 = (f32[32,512]{1,0:T(8,128)S(1)}, f32[32,512]{1,0:T(8,128)S(1)}, u32[]{:S(2)}, u32[]{:S(2)}) collective-permute-start(f32[32,512]{1,0:T(8,128)S(1)} %get-tuple-element.21.odd_ref), channel_id=1, source_target_pairs={{8,16},{16,8},{9,17},{17,9},{10,18},{18,10},{11,19},{19,11},{12,20... | collective-permute-start | bytes 196616 | tf_op jit(solution)/shard_map/ppermute | solution.py:574
  24.2 0.0 copy-start.6
  24.2 0.0 copy-start.7
  24.2 0.0 copy-start.8
  24.2 0.0 copy-done.1
  24.3 0.0 copy-done.3
  24.3 0.0 copy-done
  24.3 0.0 copy-done.4
  24.3 0.0 copy-done.5
  24.3 0.6 %copy-done.6 = s32[8]{0:T(128)S(1)} copy-done((s32[8]{0:T(128)S(1)}, s32[8]{0:T(128)}, u32[]{:S(2)}) %copy-start.6) | copy-done | bytes 56
  24.9 0.0 copy-done.7
  24.9 0.0 copy-done.8
  24.9 0.0 copy-start.2
  24.9 1.2 %shard_map.100 = (f32[6,8,512]{2,1,0:T(8,128)S(1)}, f32[144,128]{1,0:T(8,128)S(1)}, f32[128,128]{1,0:T(8,128)S(1)}, f32[19,64,128]{2,1,0:T(8,128)S(1)}, f32[8,12...) custom-call(f32[6,8,512]{2,1,0:T(8,128)S(1)} %bitcast.8, ...), custom_call_target="tpu_custom_call" | custom-call | tf_op jit(solution)/shard_map/pallas_call | solution.py:513
  26.1 0.0 collective-permute-done.from_even_ref
  26.1 0.0 collective-permute-done.1.from_late_ref
  26.1 2.3 %collective-permute-done.2.from_odd_ref = f32[32,512]{1,0:T(8,128)S(1)} collective-permute-done((f32[32,512]{1,0:T(8,128)S(1)}, f32[32,512]{1,0:T(8,128)S(1)}, u32[]{:S(2)}, u32[]{:S(2)}) %collective-permute-start.2) | collective-permute-done | bytes 65568 | tf_op jit(solution)/shard_map/ppermute | solution.py:574
  28.4 0.0 all-to-all-done
  28.4 0.0 copy-done.2
  28.4 1.7 %mortar.1 = f32[6,8,512]{2,1,0:T(8,128)} custom-call(f32[200,128]{1,0:T(8,128)S(1)} %bitcast.6, f32[32,512]{1,0:T(8,128)S(1)} %collective-permute-done.from_even_ref, f32[32,512]{1,0:T(8,128)S(1)} %collective-permute-done.1.from_late_ref, f32[32,512]{1,0:T(8,128)S(1)} %collective-permute-done.2.from_odd_ref, bf16[512,256]{1,0:T(8,128)(2,1)S(1)} %copy-done.2, ...), custom_call_target="tpu_custom_call" | custom-call | tf_op jit(solution)/shard_map/mortar/pallas_call | solution.py:589
Async XLA Ops:
  0.0 24.2 %copy-start.1 = (f32[8,6,512]{2,0,1:T(8,128)S(1)}, f32[8,6,512]{2,0,1:T(8,128)}, u32[]{:S(2)}) copy-start(f32[8,6,512]{2,0,1:T(8,128)} %param.10) | copy-start | bytes 294916
  0.0 24.3 %copy-start.3 = (bf16[256,256]{1,0:T(8,128)(2,1)S(1)}, bf16[256,256]{1,0:T(8,128)(2,1)}, u32[]{:S(2)}) copy-start(bf16[256,256]{1,0:T(8,128)(2,1)} %constant.7.clone.deriv_ref) | copy-start | bytes 393220
  2.6 21.6 %copy-start = (f32[4,64,64]{2,1,0:T(8,128)S(1)}, f32[4,64,64]{2,1,0:T(8,128)}, u32[]{:S(2)}) copy-start(f32[4,64,64]{2,1,0:T(8,128)} %proj_ref.1) | copy-start | bytes 196612
  2.7 21.6 %copy-start.4 = (bf16[16,896]{1,0:T(8,128)(2,1)S(1)}, bf16[16,896]{1,0:T(8,128)(2,1)}, u32[]{:S(2)}) copy-start(bf16[16,896]{1,0:T(8,128)(2,1)} %constant.8.clone.code_ref) | copy-start | bytes 86020
  2.7 25.8 %all-to-all-start = ((f32[8,25,1,128]{3,2,1,0:T(1,128)}), f32[8,25,1,128]{3,2,1,0:T(1,128)S(1)}, u32[]{:S(2)}, u32[]{:S(2)}) async-start(f32[8,25,1,128]{3,2,1,0:T(1,128)} %bitcast.2), calls=%async_computation | async-start | bytes 204800 | tf_op jit(solution)/shard_map/all_to_all | solution.py:573
  7.7 18.3 %collective-permute-start = (f32[32,512]{1,0:T(8,128)S(1)}, f32[32,512]{1,0:T(8,128)S(1)}, u32[]{:S(2)}, u32[]{:S(2)}) collective-permute-start(f32[32,512]{1,0:T(8,128)S(1)} %get-tuple-element.20.even_ref), channel_id=1, source_target_pairs={{1,9},{9,1},{2,10},{10,2},{3,11},{11,3},{4,12},{12,4},{5,13},{13,5... | collective-permute-start | bytes 196616 | tf_op jit(solution)/shard_map/ppermute | solution.py:571
  21.6 4.5 %collective-permute-start.1 = (f32[32,512]{1,0:T(8,128)S(1)}, f32[32,512]{1,0:T(8,128)S(1)}, u32[]{:S(2)}, u32[]{:S(2)}) collective-permute-start(f32[32,512]{1,0:T(8,128)S(1)} %get-tuple-element.20.even_ref), channel_id=1, source_target_pairs={{0,8},{8,0}} | collective-permute-start | bytes 196616 | tf_op jit(solution)/shard_map/ppermute | solution.py:575
  22.3 2.0 %copy-start.5 = (s32[8,6]{1,0:T(8,128)S(1)}, s32[8,6]{1,0:T(8,128)}, u32[]{:S(2)}) copy-start(s32[8,6]{1,0:T(8,128)} %near_ref.1) | copy-start | bytes 580
  22.3 6.2 %collective-permute-start.2 = (f32[32,512]{1,0:T(8,128)S(1)}, f32[32,512]{1,0:T(8,128)S(1)}, u32[]{:S(2)}, u32[]{:S(2)}) collective-permute-start(f32[32,512]{1,0:T(8,128)S(1)} %get-tuple-element.21.odd_ref), channel_id=1, source_target_pairs={{8,16},{16,8},{9,17},{17,9},{10,18},{18,10},{11,19},{19,11},{12,20... | collective-permute-start | bytes 196616 | tf_op jit(solution)/shard_map/ppermute | solution.py:574
  24.2 0.7 %copy-start.6 = (s32[8]{0:T(128)S(1)}, s32[8]{0:T(128)}, u32[]{:S(2)}) copy-start(s32[8]{0:T(128)} %mat_ref.1) | copy-start | bytes 100
  24.2 0.7 %copy-start.7 = (f32[8]{0:T(128)S(1)}, f32[8]{0:T(128)}, u32[]{:S(2)}) copy-start(f32[8]{0:T(128)} %metric_ref.1) | copy-start | bytes 100
  24.2 0.7 %copy-start.8 = (s32[1,10]{1,0:T(1,128)S(1)}, s32[1,10]{1,0:T(1,128)}, u32[]{:S(2)}) copy-start(s32[1,10]{1,0:T(1,128)} %param.15) | copy-start | bytes 124
  24.9 3.5 %copy-start.2 = (bf16[512,256]{1,0:T(8,128)(2,1)S(1)}, bf16[512,256]{1,0:T(8,128)(2,1)}, u32[]{:S(2)}) copy-start(bf16[512,256]{1,0:T(8,128)(2,1)} %constant.6.clone.sel_ref) | copy-start | bytes 786436

commit v8 on v7

--- a/solution.py
+++ b/solution.py
@@ -8,7 +8,6 @@
 
 
 CAPG = 8
-CAPS = 32
 SLOTS = 128
 ROWS = 25
 STEP = 0.002
@@ -233,10 +232,15 @@
     store.start()
     for j in range(3):
         w = projected(j, 64)
-        even_ref[:, 128 * j : 128 * j + 128] = w[0:32]
-        odd_ref[:, 128 * j : 128 * j + 128] = w[32:64]
-    even_ref[:, 384:512] = heat[64:96]
-    odd_ref[:, 384:512] = heat[96:128]
+        for t in range(4):
+            even_ref[24 * t + 8 * j : 24 * t + 8 * j + 8, :] = w[8 * t : 8 * t + 8]
+            odd_ref[24 * t + 8 * j : 24 * t + 8 * j + 8, :] = w[32 + 8 * t : 40 + 8 * t]
+    quarter = lax.shift_right_logical(lax.broadcasted_iota(jnp.int32, (8, 128), 1), 5)
+    for ref, at in ((even_ref, 64), (odd_ref, 96)):
+        tile = heat[at : at + 8]
+        for t in range(1, 4):
+            tile = jnp.where(quarter == t, heat[at + 8 * t : at + 8 * t + 8], tile)
+        ref[96:104, :] = tile
     store.wait()
 
 
@@ -389,7 +393,10 @@
         lanes = slice(at, at + 128)
         return (
             jnp.concatenate([mine_ref[g, :, lanes] for g in range(8)], axis=0),
-            jnp.concatenate([even_ref[:, lanes], odd_ref[:, lanes]], axis=0),
+            jnp.concatenate(
+                [ref[24 * t + at // 16 : 24 * t + at // 16 + 8, :] for ref in (even_ref, odd_ref) for t in range(4)],
+                axis=0,
+            ),
         )
 
     states = []
@@ -409,7 +416,7 @@
 
 
 def mortar_kernel(
-    from_grp_ref, from_even_ref, from_late_ref, from_odd_ref, sel_ref,
+    from_grp_ref, from_even_ref, from_odd_ref, sel_ref,
     base_ref, local_ref, sub_ref, own_ref, scale_ref, hot_ref, back_ref, turn_ref, out_hbm, new_ref, sem,
 ):
     chunk = 16
@@ -425,17 +432,19 @@
     for at in range(0, 64, chunk):
         r = slice(at, at + chunk)
 
-        def from_elem(lanes):
-            if at < 32:
-                return from_even_ref[r, lanes] + from_late_ref[r, lanes]
-            return from_odd_ref[at - 32 : at - 32 + chunk, lanes]
+        elem_ref = from_even_ref if at < 32 else from_odd_ref
+        blocks = [(at % 32) // 8 + n for n in range(chunk // 8)]
 
         theirs = []
         for j in range(3):
             starts = [ROWS * (at // 8 + n) + 8 * j for n in range(chunk // 8)]
             grp = jnp.concatenate([from_grp_ref[x : x + 8, :] for x in starts], axis=0)
-            theirs += two_halves(low, grp, from_elem(slice(128 * j, 128 * j + 128)))
-        g = jnp.where(low, grp_heat[r], from_elem(slice(384, 512)))
+            elem = jnp.concatenate([elem_ref[24 * t + 8 * j : 24 * t + 8 * j + 8, :] for t in blocks], axis=0)
+            theirs += two_halves(low, grp, elem)
+        elem_heat = jnp.concatenate(
+            [jnp.broadcast_to(elem_ref[96:104, 32 * t : 32 * t + 1], (8, 128)) for t in blocks], axis=0
+        )
+        g = jnp.where(low, grp_heat[r], elem_heat)
         mine = [own_ref[n, r] for n in range(6)]
         normal = [own_ref[n, r] for n in range(16, 19)]
         live = own_ref[15, r] > 0.5
@@ -525,8 +534,8 @@
         trace_kernel,
         out_shape=[
             jax.ShapeDtypeStruct((groups * ROWS, 128), f32),
-            pltpu.VMEM((CAPS, 512), f32),
-            pltpu.VMEM((CAPS, 512), f32),
+            pltpu.VMEM((104, 128), f32),
+            pltpu.VMEM((104, 128), f32),
             pltpu.VMEM((144, 128), f32),
             pltpu.VMEM((groups, CAPG, 384), f32),
             pltpu.VMEM((8, SLOTS), jnp.int32),
@@ -562,17 +571,11 @@
     codes_c = jnp.asarray(code_table([{n: 1} for n in range(7)]), bf16)
 
     grp, even, odd, faces, mine, kept = traces(groups, elements, material, info, mortar_proj)
-    swaps = [
-        [((i + n) * groups + g, (i + 1 - n) * groups + g) for i in range(first, n_elem - 1, 2) for g in range(groups) for n in range(2)]
-        for first in range(2)
-    ]
-    late = [(0, groups), (groups, 0)]
-    axes = ("elem", "grp")
-    from_even = lax.ppermute(even, axes, [pair for pair in swaps[0] if pair not in late])
+    swaps = [[(i + n, i + 1 - n) for i in range(first, n_elem - 1, 2) for n in range(2)] for first in range(2)]
     blocks = grp.reshape(groups, ROWS, 1, 128)
     arrived = lax.all_to_all(blocks, "grp", split_axis=0, concat_axis=0, tiled=True).reshape(groups * ROWS, 128)
-    from_odd = lax.ppermute(odd, axes, swaps[1])
-    from_late = lax.ppermute(even, axes, late)
+    from_even = lax.ppermute(even, "elem", swaps[0])
+    from_odd = lax.ppermute(odd, "elem", swaps[1])
     held = call(
         local_kernel,
         [
@@ -585,7 +588,7 @@
             mine, even, odd,
         ),
     )
-    operands = (arrived, from_even, from_late, from_odd, select, *held)
+    operands = (arrived, from_even, from_odd, select, *held)
     new = pl.pallas_call(
         mortar_kernel,
         out_shape=jax.ShapeDtypeStruct((6, 8, 512), f32),

time: 30.5 us -> 29.7 us (0.974)
  starting transfers between devices: 21.5 us -> 20.8 us
    ppermute x3 -> x2, starting transfers between devices: 16.4 us -> 15.8 us  [the longest x1 13.8 us: section(): from_even = lax.ppermute(even, 'elem', swaps[0])]
    ppermute x3 -> x2, waiting for transfers between devices: 2.35 us -> 2.23 us  [the longest x1 2.23 us: section(): from_odd = lax.ppermute(odd, 'elem', swaps[1])]
  transfers between devices with their start and end apart: 4 -> 3, of which waited for: 1 -> 1; matrix products, arithmetic and copies ran while one was open for 0% -> 0% of each run, Pallas kernels for 4% -> 4%
where the time goes in v8:
time: 29.7 us; the launch traced here: 29.4 us
  starting transfers between devices  20.8 us (70%)
  Pallas kernels  5.54 us (19%)
  waiting for transfers between devices  2.23 us (8%)
  local copies, waits for them, and re-layouts  0.65 us (2%)
    ppermute x1, starting transfers between devices, section(): from_even = lax.ppermute(even, 'elem', swaps[0])  13.8 us
    all_to_all x1, starting transfers between devices, section(): lax.all_to_all(blocks, 'grp', split_axis=0, concat_axis=0, tiled=True)  5.06 us
    pallas_call x1, Pallas kernels, traces(): pl.pallas_call(trace_kernel, out_shape=[jax.ShapeDtypeStruct((groups * RO...  2.64 us
    ppermute x1, waiting for transfers between devices, section(): from_odd = lax.ppermute(odd, 'elem', swaps[1])  2.23 us
    ppermute x1, starting transfers between devices, section(): from_odd = lax.ppermute(odd, 'elem', swaps[1])  1.92 us
    pallas_call x1, Pallas kernels, section(): pl.pallas_call(mortar_kernel, out_shape=jax.ShapeDtypeStruct((6, 8, 512),...  1.73 us
    pallas_call x1, Pallas kernels, call(): pl.pallas_call(kernel, out_shape=[jax.ShapeDtypeStruct(*s) if n in free e...  1.16 us
    unnamed x18, local copies, waits for them, and re-layouts  0.65 us
  transfers between devices with their start and end apart: 3, of which 1 were waited for; matrix products, arithmetic and copies ran while one was open for 0% of the time, Pallas kernels for 4%

profile of v8, /device:TPU:10, one launch (start us, length us, event | category | flops | bytes accessed | tf_op | source)
XLA Modules:
  0.0 29.4 jit_solution(10216688354913383397)
XLA Ops:
  0.0 0.0 copy-start.1
  0.0 0.0 copy-start.3
  0.0 2.6 %traces.1 = (f32[200,128]{1,0:T(8,128)}, f32[104,128]{1,0:T(8,128)S(1)}, f32[104,128]{1,0:T(8,128)S(1)}, f32[144,128]{1,0:T(8,128)S(1)}, f32[8,8,384]{2,1,0:T(8,128)S(1)}, /*index=5*/s32[8,128]{1,0:T(8,128)S(1)}) custom-call(f32[6,8,512]{2,1,0:T(8,128)} %bitcast.7, s32[8]{0:T(128)} %mat_ref.1, s32[4,128]{1,0:T(4,128)} %bitcast.10, f32[4,64,64]{2,1,0:T(8,128)} %proj_ref.1), custom_call_target="tpu_custom_call" | custom-call | tf_op jit(solution)/shard_map/traces/pallas_call | solution.py:533
  2.7 0.0 copy-start
  2.7 0.0 copy-start.4
  2.7 5.1 %all-to-all-start = ((f32[8,25,1,128]{3,2,1,0:T(1,128)}), f32[8,25,1,128]{3,2,1,0:T(1,128)S(1)}, u32[]{:S(2)}, u32[]{:S(2)}) async-start(f32[8,25,1,128]{3,2,1,0:T(1,128)} %bitcast.2), calls=%async_computation | async-start | bytes 204800 | tf_op jit(solution)/shard_map/all_to_all | solution.py:576
  7.7 13.8 %collective-permute-start = (f32[104,128]{1,0:T(8,128)S(1)}, f32[104,128]{1,0:T(8,128)S(1)}, u32[]{:S(2)}, u32[]{:S(2)}) collective-permute-start(f32[104,128]{1,0:T(8,128)S(1)} %get-tuple-element.20.even_ref), channel_id=1, source_target_pairs={{0,8},{8,0},{16,24},{24,16},{32,40},{40,32},{48,56},{56,48},{64,72... | collective-permute-start | bytes 159752 | tf_op jit(solution)/shard_map/ppermute | solution.py:577
  21.6 0.0 copy-start.5
  21.6 1.9 %collective-permute-start.1 = (f32[104,128]{1,0:T(8,128)S(1)}, f32[104,128]{1,0:T(8,128)S(1)}, u32[]{:S(2)}, u32[]{:S(2)}) collective-permute-start(f32[104,128]{1,0:T(8,128)S(1)} %get-tuple-element.21.odd_ref), channel_id=1, source_target_pairs={{8,16},{16,8},{24,32},{32,24},{40,48},{48,40},{56,64},{64,56},{72,... | collective-permute-start | bytes 159752 | tf_op jit(solution)/shard_map/ppermute | solution.py:578
  23.5 0.0 copy-start.6
  23.5 0.0 copy-start.7
  23.6 0.0 copy-start.8
  23.6 0.0 copy-done.1
  23.6 0.0 copy-done.3
  23.6 0.0 copy-done
  23.6 0.0 copy-done.4
  23.6 0.0 copy-done.5
  23.6 0.6 %copy-done.6 = s32[8]{0:T(128)S(1)} copy-done((s32[8]{0:T(128)S(1)}, s32[8]{0:T(128)}, u32[]{:S(2)}) %copy-start.6) | copy-done | bytes 56
  24.2 0.0 copy-done.7
  24.2 0.0 copy-done.8
  24.2 0.0 copy-start.2
  24.2 1.2 %shard_map.100 = (f32[6,8,512]{2,1,0:T(8,128)S(1)}, f32[144,128]{1,0:T(8,128)S(1)}, f32[128,128]{1,0:T(8,128)S(1)}, f32[19,64,128]{2,1,0:T(8,128)S(1)}, f32[8,12...) custom-call(f32[6,8,512]{2,1,0:T(8,128)S(1)} %bitcast.8, ...), custom_call_target="tpu_custom_call" | custom-call | tf_op jit(solution)/shard_map/pallas_call | solution.py:522
  25.4 0.0 collective-permute-done.from_even_ref
  25.4 2.2 %collective-permute-done.1.from_odd_ref = f32[104,128]{1,0:T(8,128)S(1)} collective-permute-done((f32[104,128]{1,0:T(8,128)S(1)}, f32[104,128]{1,0:T(8,128)S(1)}, u32[]{:S(2)}, u32[]{:S(2)}) %collective-permute-start.1) | collective-permute-done | bytes 53280 | tf_op jit(solution)/shard_map/ppermute | solution.py:578
  27.6 0.0 all-to-all-done
  27.6 0.0 copy-done.2
  27.6 1.7 %mortar.1 = f32[6,8,512]{2,1,0:T(8,128)} custom-call(f32[200,128]{1,0:T(8,128)S(1)} %bitcast.6, f32[104,128]{1,0:T(8,128)S(1)} %collective-permute-done.from_even_ref, f32[104,128]{1,0:T(8,128)S(1)} %collective-permute-done.1.from_odd_ref, bf16[512,256]{1,0:T(8,128)(2,1)S(1)} %copy-done.2, f32[6,8,512]{2,1,0:T(8,128)S(1)} %get-tuple-element.25.base_ref, ...), custom_call_target="tpu_custom_call" | custom-call | tf_op jit(solution)/shard_map/mortar/pallas_call | solution.py:592
Async XLA Ops:
  0.0 23.6 %copy-start.1 = (f32[8,6,512]{2,0,1:T(8,128)S(1)}, f32[8,6,512]{2,0,1:T(8,128)}, u32[]{:S(2)}) copy-start(f32[8,6,512]{2,0,1:T(8,128)} %param.10) | copy-start | bytes 294916
  0.0 23.6 %copy-start.3 = (bf16[256,256]{1,0:T(8,128)(2,1)S(1)}, bf16[256,256]{1,0:T(8,128)(2,1)}, u32[]{:S(2)}) copy-start(bf16[256,256]{1,0:T(8,128)(2,1)} %constant.7.clone.deriv_ref) | copy-start | bytes 393220
  2.7 20.9 %copy-start = (f32[4,64,64]{2,1,0:T(8,128)S(1)}, f32[4,64,64]{2,1,0:T(8,128)}, u32[]{:S(2)}) copy-start(f32[4,64,64]{2,1,0:T(8,128)} %proj_ref.1) | copy-start | bytes 196612
  2.7 20.9 %copy-start.4 = (bf16[16,896]{1,0:T(8,128)(2,1)S(1)}, bf16[16,896]{1,0:T(8,128)(2,1)}, u32[]{:S(2)}) copy-start(bf16[16,896]{1,0:T(8,128)(2,1)} %constant.8.clone.code_ref) | copy-start | bytes 86020
  2.7 25.0 %all-to-all-start = ((f32[8,25,1,128]{3,2,1,0:T(1,128)}), f32[8,25,1,128]{3,2,1,0:T(1,128)S(1)}, u32[]{:S(2)}, u32[]{:S(2)}) async-start(f32[8,25,1,128]{3,2,1,0:T(1,128)} %bitcast.2), calls=%async_computation | async-start | bytes 204800 | tf_op jit(solution)/shard_map/all_to_all | solution.py:576
  7.7 17.7 %collective-permute-start = (f32[104,128]{1,0:T(8,128)S(1)}, f32[104,128]{1,0:T(8,128)S(1)}, u32[]{:S(2)}, u32[]{:S(2)}) collective-permute-start(f32[104,128]{1,0:T(8,128)S(1)} %get-tuple-element.20.even_ref), channel_id=1, source_target_pairs={{0,8},{8,0},{16,24},{24,16},{32,40},{40,32},{48,56},{56,48},{64,72... | collective-permute-start | bytes 159752 | tf_op jit(solution)/shard_map/ppermute | solution.py:577
  21.6 2.0 %copy-start.5 = (s32[8,6]{1,0:T(8,128)S(1)}, s32[8,6]{1,0:T(8,128)}, u32[]{:S(2)}) copy-start(s32[8,6]{1,0:T(8,128)} %near_ref.1) | copy-start | bytes 580
  21.6 6.0 %collective-permute-start.1 = (f32[104,128]{1,0:T(8,128)S(1)}, f32[104,128]{1,0:T(8,128)S(1)}, u32[]{:S(2)}, u32[]{:S(2)}) collective-permute-start(f32[104,128]{1,0:T(8,128)S(1)} %get-tuple-element.21.odd_ref), channel_id=1, source_target_pairs={{8,16},{16,8},{24,32},{32,24},{40,48},{48,40},{56,64},{64,56},{72,... | collective-permute-start | bytes 159752 | tf_op jit(solution)/shard_map/ppermute | solution.py:578
  23.5 0.7 %copy-start.6 = (s32[8]{0:T(128)S(1)}, s32[8]{0:T(128)}, u32[]{:S(2)}) copy-start(s32[8]{0:T(128)} %mat_ref.1) | copy-start | bytes 100
  23.5 0.7 %copy-start.7 = (f32[8]{0:T(128)S(1)}, f32[8]{0:T(128)}, u32[]{:S(2)}) copy-start(f32[8]{0:T(128)} %metric_ref.1) | copy-start | bytes 100
  23.6 0.7 %copy-start.8 = (s32[1,10]{1,0:T(1,128)S(1)}, s32[1,10]{1,0:T(1,128)}, u32[]{:S(2)}) copy-start(s32[1,10]{1,0:T(1,128)} %param.15) | copy-start | bytes 124
  24.2 3.4 %copy-start.2 = (bf16[512,256]{1,0:T(8,128)(2,1)S(1)}, bf16[512,256]{1,0:T(8,128)(2,1)}, u32[]{:S(2)}) copy-start(bf16[512,256]{1,0:T(8,128)(2,1)} %constant.6.clone.sel_ref) | copy-start | bytes 786436

commit v9 on v8

--- a/solution.py
+++ b/solution.py
@@ -419,7 +419,7 @@
     from_grp_ref, from_even_ref, from_odd_ref, sel_ref,
     base_ref, local_ref, sub_ref, own_ref, scale_ref, hot_ref, back_ref, turn_ref, out_hbm, new_ref, sem,
 ):
-    chunk = 16
+    chunk = 32
     low = lane_low((chunk, 128))
     first, second = [[], [], []], [[], [], []]
     spread = jnp.concatenate(
@@ -557,6 +557,18 @@
     )(*(pltpu.with_memory_space_constraint(a, pltpu.HBM) for a in (elements, material, info, mortar_proj)))
 
 
+def finish(*operands):
+    return pl.pallas_call(
+        mortar_kernel,
+        out_shape=jax.ShapeDtypeStruct((6, 8, 512), f32),
+        in_specs=[VM] * len(operands),
+        out_specs=pl.BlockSpec(memory_space=pl.ANY),
+        scratch_shapes=[pltpu.VMEM((6, 8, 512), f32), pltpu.SemaphoreType.DMA((3,))],
+        name="mortar",
+        compiler_params=pltpu.CompilerParams(vmem_limit_bytes=16 << 20),
+    )(*(pltpu.with_memory_space_constraint(a, pltpu.VMEM) for a in operands))
+
+
 def section(state, material, metric, mortar_proj, mortar_map, mortar_count, neighbours):
     groups = lax.axis_size("grp")
     n_elem = lax.axis_size("elem")
@@ -588,16 +600,7 @@
             mine, even, odd,
         ),
     )
-    operands = (arrived, from_even, from_odd, select, *held)
-    new = pl.pallas_call(
-        mortar_kernel,
-        out_shape=jax.ShapeDtypeStruct((6, 8, 512), f32),
-        in_specs=[VM] * len(operands),
-        out_specs=pl.BlockSpec(memory_space=pl.ANY),
-        scratch_shapes=[pltpu.VMEM((6, 8, 512), f32), pltpu.SemaphoreType.DMA((3,))],
-        name="mortar",
-        compiler_params=pltpu.CompilerParams(vmem_limit_bytes=16 << 20),
-    )(*(pltpu.with_memory_space_constraint(a, pltpu.VMEM) for a in operands))
+    new = finish(arrived, from_even, from_odd, select, *held)
     return jnp.transpose(new, (1, 0, 2))
 
 

time: 29.7 us -> 29.7 us (level)
  no operation moved by 1% of the time
where the time goes in v9:
time: 29.7 us; the launch traced here: 29.4 us
  starting transfers between devices  20.8 us (70%)
  Pallas kernels  5.54 us (19%)
  waiting for transfers between devices  2.23 us (8%)
  local copies, waits for them, and re-layouts  0.65 us (2%)
    ppermute x1, starting transfers between devices, section(): from_even = lax.ppermute(even, 'elem', swaps[0])  13.8 us
    all_to_all x1, starting transfers between devices, section(): lax.all_to_all(blocks, 'grp', split_axis=0, concat_axis=0, tiled=True)  5.06 us
    pallas_call x1, Pallas kernels, traces(): pl.pallas_call(trace_kernel, out_shape=[jax.ShapeDtypeStruct((groups * RO...  2.64 us
    ppermute x1, waiting for transfers between devices, section(): from_odd = lax.ppermute(odd, 'elem', swaps[1])  2.23 us
    ppermute x1, starting transfers between devices, section(): from_odd = lax.ppermute(odd, 'elem', swaps[1])  1.92 us
    pallas_call x1, Pallas kernels, finish(): pl.pallas_call(mortar_kernel, out_shape=jax.ShapeDtypeStruct((6, 8, 512),...  1.74 us
    pallas_call x1, Pallas kernels, call(): pl.pallas_call(kernel, out_shape=[jax.ShapeDtypeStruct(*s) if n in free e...  1.16 us
    unnamed x18, local copies, waits for them, and re-layouts  0.65 us
  transfers between devices with their start and end apart: 3, of which 1 were waited for; matrix products, arithmetic and copies ran while one was open for 0% of the time, Pallas kernels for 4%

profile of v9, /device:TPU:10, one launch (start us, length us, event | category | flops | bytes accessed | tf_op | source)
XLA Modules:
  0.0 29.4 jit_solution(12165267222783436034)
XLA Ops:
  0.0 0.0 copy-start.1
  0.0 0.0 copy-start.3
  0.0 2.6 %traces.1 = (f32[200,128]{1,0:T(8,128)}, f32[104,128]{1,0:T(8,128)S(1)}, f32[104,128]{1,0:T(8,128)S(1)}, f32[144,128]{1,0:T(8,128)S(1)}, f32[8,8,384]{2,1,0:T(8,128)S(1)}, /*index=5*/s32[8,128]{1,0:T(8,128)S(1)}) custom-call(f32[6,8,512]{2,1,0:T(8,128)} %bitcast.7, s32[8]{0:T(128)} %mat_ref.1, s32[4,128]{1,0:T(4,128)} %bitcast.10, f32[4,64,64]{2,1,0:T(8,128)} %proj_ref.1), custom_call_target="tpu_custom_call" | custom-call | tf_op jit(solution)/shard_map/traces/pallas_call | solution.py:533
  2.7 0.0 copy-start
  2.7 0.0 copy-start.4
  2.7 5.1 %all-to-all-start = ((f32[8,25,1,128]{3,2,1,0:T(1,128)}), f32[8,25,1,128]{3,2,1,0:T(1,128)S(1)}, u32[]{:S(2)}, u32[]{:S(2)}) async-start(f32[8,25,1,128]{3,2,1,0:T(1,128)} %bitcast.2), calls=%async_computation | async-start | bytes 204800 | tf_op jit(solution)/shard_map/all_to_all | solution.py:588
  7.7 13.8 %collective-permute-start = (f32[104,128]{1,0:T(8,128)S(1)}, f32[104,128]{1,0:T(8,128)S(1)}, u32[]{:S(2)}, u32[]{:S(2)}) collective-permute-start(f32[104,128]{1,0:T(8,128)S(1)} %get-tuple-element.20.even_ref), channel_id=1, source_target_pairs={{0,8},{8,0},{16,24},{24,16},{32,40},{40,32},{48,56},{56,48},{64,72... | collective-permute-start | bytes 159752 | tf_op jit(solution)/shard_map/ppermute | solution.py:589
  21.6 0.0 copy-start.5
  21.6 1.9 %collective-permute-start.1 = (f32[104,128]{1,0:T(8,128)S(1)}, f32[104,128]{1,0:T(8,128)S(1)}, u32[]{:S(2)}, u32[]{:S(2)}) collective-permute-start(f32[104,128]{1,0:T(8,128)S(1)} %get-tuple-element.21.odd_ref), channel_id=1, source_target_pairs={{8,16},{16,8},{24,32},{32,24},{40,48},{48,40},{56,64},{64,56},{72,... | collective-permute-start | bytes 159752 | tf_op jit(solution)/shard_map/ppermute | solution.py:590
  23.5 0.0 copy-start.6
  23.5 0.0 copy-start.7
  23.6 0.0 copy-start.8
  23.6 0.0 copy-done.1
  23.6 0.0 copy-done.3
  23.6 0.0 copy-done
  23.6 0.0 copy-done.4
  23.6 0.0 copy-done.5
  23.6 0.6 %copy-done.6 = s32[8]{0:T(128)S(1)} copy-done((s32[8]{0:T(128)S(1)}, s32[8]{0:T(128)}, u32[]{:S(2)}) %copy-start.6) | copy-done | bytes 56
  24.2 0.0 copy-done.7
  24.2 0.0 copy-done.8
  24.2 0.0 copy-start.2
  24.2 1.2 %shard_map.100 = (f32[6,8,512]{2,1,0:T(8,128)S(1)}, f32[144,128]{1,0:T(8,128)S(1)}, f32[128,128]{1,0:T(8,128)S(1)}, f32[19,64,128]{2,1,0:T(8,128)S(1)}, f32[8,12...) custom-call(f32[6,8,512]{2,1,0:T(8,128)S(1)} %bitcast.8, ...), custom_call_target="tpu_custom_call" | custom-call | tf_op jit(solution)/shard_map/pallas_call | solution.py:522
  25.4 0.0 collective-permute-done.from_even_ref
  25.4 2.2 %collective-permute-done.1.from_odd_ref = f32[104,128]{1,0:T(8,128)S(1)} collective-permute-done((f32[104,128]{1,0:T(8,128)S(1)}, f32[104,128]{1,0:T(8,128)S(1)}, u32[]{:S(2)}, u32[]{:S(2)}) %collective-permute-start.1) | collective-permute-done | bytes 53280 | tf_op jit(solution)/shard_map/ppermute | solution.py:590
  27.6 0.0 all-to-all-done
  27.6 0.0 copy-done.2
  27.6 1.7 %mortar.1 = f32[6,8,512]{2,1,0:T(8,128)} custom-call(f32[200,128]{1,0:T(8,128)S(1)} %bitcast.6, f32[104,128]{1,0:T(8,128)S(1)} %collective-permute-done.from_even_ref, f32[104,128]{1,0:T(8,128)S(1)} %collective-permute-done.1.from_odd_ref, bf16[512,256]{1,0:T(8,128)(2,1)S(1)} %copy-done.2, f32[6,8,512]{2,1,0:T(8,128)S(1)} %get-tuple-element.25.base_ref, ...), custom_call_target="tpu_custom_call" | custom-call | tf_op jit(solution)/shard_map/mortar/pallas_call | solution.py:561
Async XLA Ops:
  0.0 23.6 %copy-start.1 = (f32[8,6,512]{2,0,1:T(8,128)S(1)}, f32[8,6,512]{2,0,1:T(8,128)}, u32[]{:S(2)}) copy-start(f32[8,6,512]{2,0,1:T(8,128)} %param.10) | copy-start | bytes 294916
  0.0 23.6 %copy-start.3 = (bf16[256,256]{1,0:T(8,128)(2,1)S(1)}, bf16[256,256]{1,0:T(8,128)(2,1)}, u32[]{:S(2)}) copy-start(bf16[256,256]{1,0:T(8,128)(2,1)} %constant.7.clone.deriv_ref) | copy-start | bytes 393220
  2.7 20.9 %copy-start = (f32[4,64,64]{2,1,0:T(8,128)S(1)}, f32[4,64,64]{2,1,0:T(8,128)}, u32[]{:S(2)}) copy-start(f32[4,64,64]{2,1,0:T(8,128)} %proj_ref.1) | copy-start | bytes 196612
  2.7 20.9 %copy-start.4 = (bf16[16,896]{1,0:T(8,128)(2,1)S(1)}, bf16[16,896]{1,0:T(8,128)(2,1)}, u32[]{:S(2)}) copy-start(bf16[16,896]{1,0:T(8,128)(2,1)} %constant.8.clone.code_ref) | copy-start | bytes 86020
  2.7 25.0 %all-to-all-start = ((f32[8,25,1,128]{3,2,1,0:T(1,128)}), f32[8,25,1,128]{3,2,1,0:T(1,128)S(1)}, u32[]{:S(2)}, u32[]{:S(2)}) async-start(f32[8,25,1,128]{3,2,1,0:T(1,128)} %bitcast.2), calls=%async_computation | async-start | bytes 204800 | tf_op jit(solution)/shard_map/all_to_all | solution.py:588
  7.7 17.7 %collective-permute-start = (f32[104,128]{1,0:T(8,128)S(1)}, f32[104,128]{1,0:T(8,128)S(1)}, u32[]{:S(2)}, u32[]{:S(2)}) collective-permute-start(f32[104,128]{1,0:T(8,128)S(1)} %get-tuple-element.20.even_ref), channel_id=1, source_target_pairs={{0,8},{8,0},{16,24},{24,16},{32,40},{40,32},{48,56},{56,48},{64,72... | collective-permute-start | bytes 159752 | tf_op jit(solution)/shard_map/ppermute | solution.py:589
  21.6 2.0 %copy-start.5 = (s32[8,6]{1,0:T(8,128)S(1)}, s32[8,6]{1,0:T(8,128)}, u32[]{:S(2)}) copy-start(s32[8,6]{1,0:T(8,128)} %near_ref.1) | copy-start | bytes 580
  21.6 6.0 %collective-permute-start.1 = (f32[104,128]{1,0:T(8,128)S(1)}, f32[104,128]{1,0:T(8,128)S(1)}, u32[]{:S(2)}, u32[]{:S(2)}) collective-permute-start(f32[104,128]{1,0:T(8,128)S(1)} %get-tuple-element.21.odd_ref), channel_id=1, source_target_pairs={{8,16},{16,8},{24,32},{32,24},{40,48},{48,40},{56,64},{64,56},{72,... | collective-permute-start | bytes 159752 | tf_op jit(solution)/shard_map/ppermute | solution.py:590
  23.5 0.7 %copy-start.6 = (s32[8]{0:T(128)S(1)}, s32[8]{0:T(128)}, u32[]{:S(2)}) copy-start(s32[8]{0:T(128)} %mat_ref.1) | copy-start | bytes 100
  23.5 0.7 %copy-start.7 = (f32[8]{0:T(128)S(1)}, f32[8]{0:T(128)}, u32[]{:S(2)}) copy-start(f32[8]{0:T(128)} %metric_ref.1) | copy-start | bytes 100
  23.6 0.7 %copy-start.8 = (s32[1,10]{1,0:T(1,128)S(1)}, s32[1,10]{1,0:T(1,128)}, u32[]{:S(2)}) copy-start(s32[1,10]{1,0:T(1,128)} %param.15) | copy-start | bytes 124
  24.2 3.4 %copy-start.2 = (bf16[512,256]{1,0:T(8,128)(2,1)S(1)}, bf16[512,256]{1,0:T(8,128)(2,1)}, u32[]{:S(2)}) copy-start(bf16[512,256]{1,0:T(8,128)(2,1)} %constant.6.clone.sel_ref) | copy-start | bytes 786436

commit v10 on v9

--- a/solution.py
+++ b/solution.py
@@ -416,7 +416,7 @@
 
 
 def mortar_kernel(
-    from_grp_ref, from_even_ref, from_odd_ref, sel_ref,
+    from_grp_ref, from_even_ref, from_late_ref, from_odd_ref, sel_ref,
     base_ref, local_ref, sub_ref, own_ref, scale_ref, hot_ref, back_ref, turn_ref, out_hbm, new_ref, sem,
 ):
     chunk = 32
@@ -432,17 +432,23 @@
     for at in range(0, 64, chunk):
         r = slice(at, at + chunk)
 
-        elem_ref = from_even_ref if at < 32 else from_odd_ref
+
+        def from_elem(x):
+            if at < 32:
+                return from_even_ref[x : x + 8, :] + from_late_ref[x : x + 8, :]
+            return from_odd_ref[x : x + 8, :]
+
         blocks = [(at % 32) // 8 + n for n in range(chunk // 8)]
 
         theirs = []
         for j in range(3):
             starts = [ROWS * (at // 8 + n) + 8 * j for n in range(chunk // 8)]
             grp = jnp.concatenate([from_grp_ref[x : x + 8, :] for x in starts], axis=0)
-            elem = jnp.concatenate([elem_ref[24 * t + 8 * j : 24 * t + 8 * j + 8, :] for t in blocks], axis=0)
+            elem = jnp.concatenate([from_elem(24 * t + 8 * j) for t in blocks], axis=0)
             theirs += two_halves(low, grp, elem)
+        heats = from_elem(96)
         elem_heat = jnp.concatenate(
-            [jnp.broadcast_to(elem_ref[96:104, 32 * t : 32 * t + 1], (8, 128)) for t in blocks], axis=0
+            [jnp.broadcast_to(heats[:, 32 * t : 32 * t + 1], (8, 128)) for t in blocks], axis=0
         )
         g = jnp.where(low, grp_heat[r], elem_heat)
         mine = [own_ref[n, r] for n in range(6)]
@@ -583,11 +589,17 @@
     codes_c = jnp.asarray(code_table([{n: 1} for n in range(7)]), bf16)
 
     grp, even, odd, faces, mine, kept = traces(groups, elements, material, info, mortar_proj)
-    swaps = [[(i + n, i + 1 - n) for i in range(first, n_elem - 1, 2) for n in range(2)] for first in range(2)]
+    swaps = [
+        [((i + n) * groups + g, (i + 1 - n) * groups + g) for i in range(first, n_elem - 1, 2) for g in range(groups) for n in range(2)]
+        for first in range(2)
+    ]
+    late = [(0, groups), (groups, 0)]
+    axes = ("elem", "grp")
+    from_even = lax.ppermute(even, axes, [pair for pair in swaps[0] if pair not in late])
     blocks = grp.reshape(groups, ROWS, 1, 128)
     arrived = lax.all_to_all(blocks, "grp", split_axis=0, concat_axis=0, tiled=True).reshape(groups * ROWS, 128)
-    from_even = lax.ppermute(even, "elem", swaps[0])
-    from_odd = lax.ppermute(odd, "elem", swaps[1])
+    from_odd = lax.ppermute(odd, axes, swaps[1])
+    from_late = lax.ppermute(even, axes, late)
     held = call(
         local_kernel,
         [
@@ -600,7 +612,7 @@
             mine, even, odd,
         ),
     )
-    new = finish(arrived, from_even, from_odd, select, *held)
+    new = finish(arrived, from_even, from_late, from_odd, select, *held)
     return jnp.transpose(new, (1, 0, 2))
 
 

time: 29.7 us -> 30.3 us (1.020)
  starting transfers between devices: 20.8 us -> 21.5 us
    ppermute x2 -> x3, starting transfers between devices: 15.8 us -> 16.4 us  [the longest x1 13.8 us: section(): lax.ppermute(even, axes, [pair for pair in swaps[0] if pair not in late])]
    ppermute x2 -> x3, waiting for transfers between devices: 2.23 us -> 2.22 us  [the longest x1 2.21 us: section(): from_odd = lax.ppermute(odd, axes, swaps[1])]
  transfers between devices with their start and end apart: 3 -> 4, of which waited for: 1 -> 1; matrix products, arithmetic and copies ran while one was open for 0% -> 0% of each run, Pallas kernels for 4% -> 4%
where the time goes in v10:
time: 30.3 us; the launch traced here: 30.1 us
  starting transfers between devices  21.5 us (71%)
  Pallas kernels  5.55 us (18%)
  waiting for transfers between devices  2.22 us (7%)
  local copies, waits for them, and re-layouts  0.65 us (2%)
    ppermute x1, starting transfers between devices, section(): lax.ppermute(even, axes, [pair for pair in swaps[0] if pair not in late])  13.8 us
    all_to_all x1, starting transfers between devices, section(): lax.all_to_all(blocks, 'grp', split_axis=0, concat_axis=0, tiled=True)  5.06 us
    pallas_call x1, Pallas kernels, traces(): pl.pallas_call(trace_kernel, out_shape=[jax.ShapeDtypeStruct((groups * RO...  2.63 us
    ppermute x1, waiting for transfers between devices, section(): from_odd = lax.ppermute(odd, axes, swaps[1])  2.21 us
    ppermute x1, starting transfers between devices, section(): from_odd = lax.ppermute(odd, axes, swaps[1])  1.92 us
    pallas_call x1, Pallas kernels, finish(): pl.pallas_call(mortar_kernel, out_shape=jax.ShapeDtypeStruct((6, 8, 512),...  1.75 us
    pallas_call x1, Pallas kernels, call(): pl.pallas_call(kernel, out_shape=[jax.ShapeDtypeStruct(*s) if n in free e...  1.17 us
    ppermute x1, starting transfers between devices, section(): from_late = lax.ppermute(even, axes, late)  0.66 us
  transfers between devices with their start and end apart: 4, of which 1 were waited for; matrix products, arithmetic and copies ran while one was open for 0% of the time, Pallas kernels for 4%

profile of v10, /device:TPU:10, one launch (start us, length us, event | category | flops | bytes accessed | tf_op | source)
XLA Modules:
  0.0 30.1 jit_solution(16984848826470188094)
XLA Ops:
  0.0 0.0 copy-start.1
  0.0 0.0 copy-start.3
  0.0 2.6 %traces.1 = (f32[200,128]{1,0:T(8,128)}, f32[104,128]{1,0:T(8,128)S(1)}, f32[104,128]{1,0:T(8,128)S(1)}, f32[144,128]{1,0:T(8,128)S(1)}, f32[8,8,384]{2,1,0:T(8,128)S(1)}, /*index=5*/s32[8,128]{1,0:T(8,128)S(1)}) custom-call(f32[6,8,512]{2,1,0:T(8,128)} %bitcast.7, s32[8]{0:T(128)} %mat_ref.1, s32[4,128]{1,0:T(4,128)} %bitcast.10, f32[4,64,64]{2,1,0:T(8,128)} %proj_ref.1), custom_call_target="tpu_custom_call" | custom-call | tf_op jit(solution)/shard_map/traces/pallas_call | solution.py:539
  2.6 0.0 copy-start
  2.7 0.0 copy-start.4
  2.7 5.1 %all-to-all-start = ((f32[8,25,1,128]{3,2,1,0:T(1,128)}), f32[8,25,1,128]{3,2,1,0:T(1,128)S(1)}, u32[]{:S(2)}, u32[]{:S(2)}) async-start(f32[8,25,1,128]{3,2,1,0:T(1,128)} %bitcast.2), calls=%async_computation | async-start | bytes 204800 | tf_op jit(solution)/shard_map/all_to_all | solution.py:600
  7.7 13.8 %collective-permute-start = (f32[104,128]{1,0:T(8,128)S(1)}, f32[104,128]{1,0:T(8,128)S(1)}, u32[]{:S(2)}, u32[]{:S(2)}) collective-permute-start(f32[104,128]{1,0:T(8,128)S(1)} %get-tuple-element.20.even_ref), channel_id=1, source_target_pairs={{1,9},{9,1},{2,10},{10,2},{3,11},{11,3},{4,12},{12,4},{5,13},{13,5... | collective-permute-start | bytes 159752 | tf_op jit(solution)/shard_map/ppermute | solution.py:598
  21.6 0.7 %collective-permute-start.1 = (f32[104,128]{1,0:T(8,128)S(1)}, f32[104,128]{1,0:T(8,128)S(1)}, u32[]{:S(2)}, u32[]{:S(2)}) collective-permute-start(f32[104,128]{1,0:T(8,128)S(1)} %get-tuple-element.20.even_ref), channel_id=1, source_target_pairs={{0,8},{8,0}} | collective-permute-start | bytes 159752 | tf_op jit(solution)/shard_map/ppermute | solution.py:602
  22.3 0.0 copy-start.5
  22.3 1.9 %collective-permute-start.2 = (f32[104,128]{1,0:T(8,128)S(1)}, f32[104,128]{1,0:T(8,128)S(1)}, u32[]{:S(2)}, u32[]{:S(2)}) collective-permute-start(f32[104,128]{1,0:T(8,128)S(1)} %get-tuple-element.21.odd_ref), channel_id=1, source_target_pairs={{8,16},{16,8},{9,17},{17,9},{10,18},{18,10},{11,19},{19,11},{12,20... | collective-permute-start | bytes 159752 | tf_op jit(solution)/shard_map/ppermute | solution.py:601
  24.2 0.0 copy-start.6
  24.2 0.0 copy-start.7
  24.2 0.0 copy-start.8
  24.2 0.0 copy-done.1
  24.2 0.0 copy-done.3
  24.3 0.0 copy-done
  24.3 0.0 copy-done.4
  24.3 0.0 copy-done.5
  24.3 0.6 %copy-done.6 = s32[8]{0:T(128)S(1)} copy-done((s32[8]{0:T(128)S(1)}, s32[8]{0:T(128)}, u32[]{:S(2)}) %copy-start.6) | copy-done | bytes 56
  24.9 0.0 copy-done.7
  24.9 0.0 copy-done.8
  24.9 0.0 copy-start.2
  24.9 1.2 %shard_map.100 = (f32[6,8,512]{2,1,0:T(8,128)S(1)}, f32[144,128]{1,0:T(8,128)S(1)}, f32[128,128]{1,0:T(8,128)S(1)}, f32[19,64,128]{2,1,0:T(8,128)S(1)}, f32[8,12...) custom-call(f32[6,8,512]{2,1,0:T(8,128)S(1)} %bitcast.8, ...), custom_call_target="tpu_custom_call" | custom-call | tf_op jit(solution)/shard_map/pallas_call | solution.py:528
  26.1 0.0 collective-permute-done.from_even_ref
  26.1 0.0 collective-permute-done.1.from_late_ref
  26.1 2.2 %collective-permute-done.2.from_odd_ref = f32[104,128]{1,0:T(8,128)S(1)} collective-permute-done((f32[104,128]{1,0:T(8,128)S(1)}, f32[104,128]{1,0:T(8,128)S(1)}, u32[]{:S(2)}, u32[]{:S(2)}) %collective-permute-start.2) | collective-permute-done | bytes 53280 | tf_op jit(solution)/shard_map/ppermute | solution.py:601
  28.3 0.0 all-to-all-done
  28.3 0.0 copy-done.2
  28.3 1.7 %mortar.1 = f32[6,8,512]{2,1,0:T(8,128)} custom-call(f32[200,128]{1,0:T(8,128)S(1)} %bitcast.6, f32[104,128]{1,0:T(8,128)S(1)} %collective-permute-done.from_even_ref, f32[104,128]{1,0:T(8,128)S(1)} %collective-permute-done.1.from_late_ref, f32[104,128]{1,0:T(8,128)S(1)} %collective-permute-done.2.from_odd_ref, bf16[512,256]{1,0:T(8,128)(2,1)S(1)} %copy-done.2, ...), custom_call_target="tpu_custom_call" | custom-call | tf_op jit(solution)/shard_map/mortar/pallas_call | solution.py:567
Async XLA Ops:
  0.0 24.2 %copy-start.1 = (f32[8,6,512]{2,0,1:T(8,128)S(1)}, f32[8,6,512]{2,0,1:T(8,128)}, u32[]{:S(2)}) copy-start(f32[8,6,512]{2,0,1:T(8,128)} %param.10) | copy-start | bytes 294916
  0.0 24.2 %copy-start.3 = (bf16[256,256]{1,0:T(8,128)(2,1)S(1)}, bf16[256,256]{1,0:T(8,128)(2,1)}, u32[]{:S(2)}) copy-start(bf16[256,256]{1,0:T(8,128)(2,1)} %constant.7.clone.deriv_ref) | copy-start | bytes 393220
  2.6 21.6 %copy-start = (f32[4,64,64]{2,1,0:T(8,128)S(1)}, f32[4,64,64]{2,1,0:T(8,128)}, u32[]{:S(2)}) copy-start(f32[4,64,64]{2,1,0:T(8,128)} %proj_ref.1) | copy-start | bytes 196612
  2.7 21.6 %copy-start.4 = (bf16[16,896]{1,0:T(8,128)(2,1)S(1)}, bf16[16,896]{1,0:T(8,128)(2,1)}, u32[]{:S(2)}) copy-start(bf16[16,896]{1,0:T(8,128)(2,1)} %constant.8.clone.code_ref) | copy-start | bytes 86020
  2.7 25.6 %all-to-all-start = ((f32[8,25,1,128]{3,2,1,0:T(1,128)}), f32[8,25,1,128]{3,2,1,0:T(1,128)S(1)}, u32[]{:S(2)}, u32[]{:S(2)}) async-start(f32[8,25,1,128]{3,2,1,0:T(1,128)} %bitcast.2), calls=%async_computation | async-start | bytes 204800 | tf_op jit(solution)/shard_map/all_to_all | solution.py:600
  7.7 18.3 %collective-permute-start = (f32[104,128]{1,0:T(8,128)S(1)}, f32[104,128]{1,0:T(8,128)S(1)}, u32[]{:S(2)}, u32[]{:S(2)}) collective-permute-start(f32[104,128]{1,0:T(8,128)S(1)} %get-tuple-element.20.even_ref), channel_id=1, source_target_pairs={{1,9},{9,1},{2,10},{10,2},{3,11},{11,3},{4,12},{12,4},{5,13},{13,5... | collective-permute-start | bytes 159752 | tf_op jit(solution)/shard_map/ppermute | solution.py:598
  21.6 4.5 %collective-permute-start.1 = (f32[104,128]{1,0:T(8,128)S(1)}, f32[104,128]{1,0:T(8,128)S(1)}, u32[]{:S(2)}, u32[]{:S(2)}) collective-permute-start(f32[104,128]{1,0:T(8,128)S(1)} %get-tuple-element.20.even_ref), channel_id=1, source_target_pairs={{0,8},{8,0}} | collective-permute-start | bytes 159752 | tf_op jit(solution)/shard_map/ppermute | solution.py:602
  22.3 2.0 %copy-start.5 = (s32[8,6]{1,0:T(8,128)S(1)}, s32[8,6]{1,0:T(8,128)}, u32[]{:S(2)}) copy-start(s32[8,6]{1,0:T(8,128)} %near_ref.1) | copy-start | bytes 580
  22.3 6.0 %collective-permute-start.2 = (f32[104,128]{1,0:T(8,128)S(1)}, f32[104,128]{1,0:T(8,128)S(1)}, u32[]{:S(2)}, u32[]{:S(2)}) collective-permute-start(f32[104,128]{1,0:T(8,128)S(1)} %get-tuple-element.21.odd_ref), channel_id=1, source_target_pairs={{8,16},{16,8},{9,17},{17,9},{10,18},{18,10},{11,19},{19,11},{12,20... | collective-permute-start | bytes 159752 | tf_op jit(solution)/shard_map/ppermute | solution.py:601
  24.2 0.7 %copy-start.6 = (s32[8]{0:T(128)S(1)}, s32[8]{0:T(128)}, u32[]{:S(2)}) copy-start(s32[8]{0:T(128)} %mat_ref.1) | copy-start | bytes 100
  24.2 0.7 %copy-start.7 = (f32[8]{0:T(128)S(1)}, f32[8]{0:T(128)}, u32[]{:S(2)}) copy-start(f32[8]{0:T(128)} %metric_ref.1) | copy-start | bytes 100
  24.2 0.7 %copy-start.8 = (s32[1,10]{1,0:T(1,128)S(1)}, s32[1,10]{1,0:T(1,128)}, u32[]{:S(2)}) copy-start(s32[1,10]{1,0:T(1,128)} %param.15) | copy-start | bytes 124
  24.9 3.4 %copy-start.2 = (bf16[512,256]{1,0:T(8,128)(2,1)S(1)}, bf16[512,256]{1,0:T(8,128)(2,1)}, u32[]{:S(2)}) copy-start(bf16[512,256]{1,0:T(8,128)(2,1)} %constant.6.clone.sel_ref) | copy-start | bytes 786436
